TPU v7x, 256 devices: a whole 4x4x8 slice. The times are simulated.
256 devices in a mesh: seq: 32 (over z, y_lo, core), fsdp: 8 (over x, y_hi).
Axes of the slice: x: 4, y: 4 (y_hi: 2, y_lo: 2; y = y_hi * 2 + y_lo), z: 8, core: 2. Of those that a mesh axis runs over, the one named last changes fastest.
Arguments:
- inputs: bfloat16 [16, 4096, 1536], P('fsdp', 'seq'), may hold values from -6 to 6
- gain: float32 [1536], replicated, may hold values from 0.1 to 1.9
- param: bfloat16 [1536, 3, 1536], P('fsdp'), may hold values from -6 to 6
- cotangent: bfloat16 [16, 4096, 1536], P('fsdp', 'seq'), may hold values from -12 to 12
- noise: bfloat16 [1536, 3, 1536], P('fsdp'), may hold values from -6 to 6
Outputs:
- outputs: bfloat16 [16, 4096, 1536], P('fsdp', 'seq')
- new_param: bfloat16 [1536, 3, 1536], P('fsdp')
All inputs are finite; a program needn't handle non-finite values.
Results may differ from a plain program's by a relative error of at most 0.012.
Values may be sent and summed in bfloat16 or wider, within the bound.
No kernel may reach another device: no remote copies, remote signals or barrier semaphores. Data moves between devices by JAX's collectives and lax.ppermute only.
A program may use at most 128 MiB of HBM per device.

v0:
```python
import math

import jax
import jax.numpy as jnp
from jax import lax
from jax.sharding import PartitionSpec as P

DILATION_STEP = 16


def padded(x, sides, width):
    for axis, dim in sides:
        count, length = (lax.axis_size(axis), x.shape[dim])
        up = [(i, (i + 1) % count) for i in range(count - 1)]
        down = [(j, i) for i, j in up]
        last = lax.slice_in_dim(x, length - width, length, axis=dim)
        first = lax.slice_in_dim(x, 0, width, axis=dim)
        before = lax.ppermute(last, axis, up)
        after = lax.ppermute(first, axis, down)
        x = jnp.concatenate([before, x, after], axis=dim)
    return x


def normalise(values, gain):
    floats = values.astype(jnp.float32)
    factor = lax.rsqrt(jnp.mean(floats * floats, axis=-1, keepdims=True) + 1e-06)
    return jax.nn.gelu(floats * factor * gain).astype(jnp.bfloat16)


def convolve(source_rows, kernel, scale):
    span_length = source_rows.shape[1] - 2 * DILATION_STEP
    total = jnp.zeros((source_rows.shape[0], span_length, kernel.shape[0]), jnp.float32)
    for kernel_tap in range(3):
        input_window = source_rows[
            :, kernel_tap * DILATION_STEP : kernel_tap * DILATION_STEP + span_length, :
        ]
        total = total + lax.dot_general(
            input_window,
            kernel[:, kernel_tap, :],
            (((2,), (1,)), ((), ())),
            preferred_element_type=jnp.float32,
        )
    return total * scale


def shards(inputs, gain, param, cotangent, noise):
    seqs, span_length, width = inputs.shape
    scale = 1.0 / math.sqrt(3.0 * width)
    total_rows = seqs * lax.axis_size("fsdp") * span_length * lax.axis_size("seq")
    eta = math.sqrt(3.0 * width / total_rows)
    hidden_state = normalise(inputs, gain)
    padded_input = padded(hidden_state, (("seq", 1),), DILATION_STEP)
    mixed = convolve(padded_input, lax.all_gather(param, "fsdp", axis=0, tiled=True), scale)
    taps = []
    for kernel_tap in range(3):
        input_window = padded_input[
            :, kernel_tap * DILATION_STEP : kernel_tap * DILATION_STEP + span_length, :
        ]
        taps.append(
            lax.dot_general(
                cotangent,
                input_window,
                (((0, 1), (0, 1)), ((), ())),
                preferred_element_type=jnp.float32,
            )
        )
    term = (jnp.stack(taps, axis=1) * scale).astype(jnp.bfloat16)
    term = lax.optimization_barrier(term)
    share = lax.psum_scatter(
        term.astype(jnp.float32).astype(jnp.bfloat16), "fsdp", scatter_dimension=0, tiled=True
    ).astype(jnp.float32)
    seq_share = lax.psum_scatter(share, "seq", scatter_dimension=0, tiled=True)
    piece_rows = seq_share.shape[0]
    offset = lax.axis_index("seq") * piece_rows
    own_param = lax.dynamic_slice_in_dim(param, offset, piece_rows, 0)
    own_noise = lax.dynamic_slice_in_dim(noise, offset, piece_rows, 0)
    updated = (
        own_param.astype(jnp.float32)
        - eta * seq_share
        + math.sqrt(2.0 * eta) * own_noise.astype(jnp.float32)
    )
    new_param = lax.all_gather(updated.astype(jnp.bfloat16), "seq", axis=0, tiled=True)
    outputs = (inputs.astype(jnp.float32) + mixed).astype(jnp.bfloat16)
    return (outputs, new_param)


def solution(mesh):
    placed = (
        P("fsdp", "seq", None),
        P(),
        P("fsdp", None, None),
        P("fsdp", "seq", None),
        P("fsdp", None, None),
    )
    return jax.shard_map(
        shards,
        mesh=mesh,
        in_specs=placed,
        out_specs=(P("fsdp", "seq", None), P("fsdp", None, None)),
        check_vma=False,
    )
```

profile of v0, /device:TPU:1, one launch (start us, length us, event | category | flops | bytes accessed | tf_op | source)
XLA Modules:
  0.0 720.0 jit_solution(8907818899789513406)
XLA Ops:
  7.2 0.0 copy-start
  7.2 0.0 reduce-scatter.4.cloned.1.call-start
  7.2 1.5 fusion.9
  8.8 1.8 fusion.13
  10.6 5.1 collective-permute-start.1
  15.8 1.9 collective-permute-start
  17.7 1.4 convolution_bitcast_fusion.1
  19.2 1.4 convolution_bitcast_fusion
  20.6 1.4 convolution_bitcast_fusion.2
  22.0 7.4 %fusion = bf16[1536,3,1536]{0,2,1:T(8,128)(2,1)} fusion(f32[1536,1,1536]{0,2,1:T(8,128)S(1)} %convolution_bitcast_fusion, f32[1536,1,1536]{0,2,1:T(8,128)S(1)} %convolution_bitcast_fusion.1, f32[1536,1,1536]{0,2,1:T(8,128)S(1)} %convolution_bitcast_fusion.2), kind=kLoop, calls=%fused_computation.1 | loop fusion | flops 28311552 | bytes 42467328 | tf_op jit(solution)/shard_map/convert_element_type | solution.py:67
  29.4 17.9 %copy.33 = bf16[1536,4608]{1,0:T(8,128)(2,1)} copy(bf16[1536,4608]{0,1:T(8,128)(2,1)} %bitcast.49) | data formatting | bytes 28311552
  47.3 0.0 reduce-scatter.4.cloned.1.call-update
  47.4 0.0 all-reduce.3.cloned.1.call-start
  47.4 174.2 %reduce-scatter.4.cloned.1.call-done = bf16[192,4608]{1,0:T(8,128)(2,1)} async-done(((bf16[1536,4608]{1,0:T(8,128)(2,1)}), bf16[192,4608]{1,0:T(8,128)(2,1)}) %reduce-scatter.4.cloned.1.call-update) | async-done | bytes 1769488
  221.6 4.0 copy.34
  225.5 4.0 copy.24
  229.6 5.2 copy.25
  234.7 0.0 all-reduce.3.cloned.1.call-update
  234.8 0.0 all-gather.3.cloned.1.call-start
  234.8 0.7 all-gather.3.cloned.1.call-update
  235.5 0.0 all-gather.5.cloned.1.call-start
  235.6 0.6 dynamic-slice
  236.8 0.9 constant_dynamic-slice_fusion.1
  237.8 236.0 %all-reduce.3.cloned.1.call-done = f32[192,3,1536]{2,1,0:T(4,128)} async-done(((f32[192,3,1536]{2,1,0:T(4,128)}), f32[192,3,1536]{2,1,0:T(4,128)}) %all-reduce.3.cloned.1.call-update) | async-done | bytes 3538960
  473.8 1.6 fusion.21
  475.5 0.0 all-gather.5.cloned.1.call-update
  475.5 168.2 %all-gather.3.cloned.1.call-done = bf16[1536,3,1536]{2,0,1:T(8,128)(2,1)} async-done(((bf16[192,3,1536]{2,0,1:T(8,128)(2,1)}), bf16[1536,3,1536]{2,0,1:T(8,128)(2,1)}) %all-gather.3.cloned.1.call-update) | async-done | bytes 14155792 | tf_op jit(solution)/shard_map/all_gather | solution.py:53
  643.8 3.7 fusion.1
  647.5 3.8 fusion.2
  651.4 4.8 fusion.8
  656.1 54.1 %all-gather.5.cloned.1.call-done = bf16[192,3,1536]{2,1,0:T(4,128)(2,1)} async-done(((bf16[6,3,1536]{2,1,0:T(4,128)(2,1)}), bf16[192,3,1536]{2,1,0:T(4,128)(2,1)}) %all-gather.5.cloned.1.call-update) | async-done | bytes 1769488 | tf_op jit(solution)/shard_map/all_gather | solution.py:82
  710.2 3.2 copy.27
  (12 shorter events, 0.1 us)
Async XLA Ops:
  7.2 230.6 %copy-start = (bf16[192,3,1536]{2,0,1:T(8,128)(2,1)S(1)}, bf16[192,3,1536]{2,0,1:T(8,128)(2,1)}, u32[]{:S(2)}) copy-start(bf16[192,3,1536]{2,0,1:T(8,128)(2,1)} %param.9) | copy-start | bytes 5308420
  7.2 10.6 %copy-start.1 = (bf16[2,128,1536]{2,1,0:T(8,128)(2,1)S(1)}, bf16[2,128,1536]{2,1,0:T(8,128)(2,1)}, u32[]{:S(2)}) copy-start(bf16[2,128,1536]{2,1,0:T(8,128)(2,1)} %param.8) | copy-start | bytes 2359300
  7.2 214.4 %reduce-scatter.4.cloned.1.call-start = ((), (), s32[]{:S(2)}) async-start(), calls=%async_computation.3 | async-start | bytes 15925248
  10.6 8.5 %collective-permute-start.1 = (bf16[2,16,1536]{2,1,0:T(8,128)(2,1)S(1)}, bf16[2,16,1536]{2,1,0:T(8,128)(2,1)S(1)}, u32[]{:S(2)}, u32[]{:S(2)}) collective-permute-start(bf16[2,16,1536]{2,1,0:T(8,128)(2,1)S(1)} %get-tuple-element.9), channel_id=1, source_target_pairs={{8,0},{16,8},{24,16},{32,24},{40,32},{48,40},{56,48},{64,56},{72,6... | collective-permute-start | bytes 294920 | tf_op jit(solution)/shard_map/ppermute | solution.py:19
  15.8 4.8 collective-permute-start
  47.4 426.5 %all-reduce.3.cloned.1.call-start = ((), (), s32[]{:S(2)}) async-start(), calls=%async_computation.4 | async-start | bytes 9437184
  234.8 0.8 copy-start.3
  234.8 409.0 %all-gather.3.cloned.1.call-start = ((), (), s32[]{:S(2)}) async-start(), calls=%async_computation.1 | async-start | bytes 15925248 | tf_op jit(solution)/shard_map/all_gather | solution.py:53
  235.5 474.7 %all-gather.5.cloned.1.call-start = ((), (), s32[]{:S(2)}) async-start(), calls=%async_computation.2 | async-start | bytes 2433024 | tf_op jit(solution)/shard_map/all_gather | solution.py:82
  647.5 3.8 copy-start.2
Sparse Core Ops, SparseCore 0:
  47.5 174.0 reduce-scatter.3
  234.9 238.9 all-reduce.2
  476.8 166.8 all-gather.2
  646.2 63.9 all-gather.4
where the time goes:
time: 721 us; the launch traced here: 720 us
  waiting for transfers between devices  633 us (88%)
  local copies, waits for them, and re-layouts  36 us (5%)
  matrix products  16.6 us (2%)
  between operations  14.6 us (2%)
  other arithmetic  12.4 us (2%)
  starting transfers between devices  7.23 us (1%)
    unnamed x6, waiting for transfers between devices  411 us
    all_gather x1, waiting for transfers between devices, shards(): lax.all_gather(param, 'fsdp', axis=0, tiled=True)  168 us
    all_gather x1, waiting for transfers between devices, shards(): lax.all_gather(updated.astype(jnp.bfloat16), 'seq', axis=0, tiled=True)  54.1 us
    unnamed x12, local copies, waits for them, and re-layouts  25.8 us
  transfers between devices with their start and end apart: 6, of which 4 were waited for; matrix products, arithmetic and copies ran while one was open for 3% of the time, Pallas kernels for 0%

commit v1 on v0

v1 whole, which is shorter than its diff:
```python
import math

import jax
import jax.numpy as jnp
from jax import lax
from jax.sharding import Mesh, PartitionSpec as P

D = 16
F32, BF16 = jnp.float32, jnp.bfloat16
SEQ = ("z", "ylo", "core")
PLANE = ("ylo", "core", "x", "yhi")
SIZES = (2, 2, 4, 2)


def plane_perm(move):
    pairs = []
    for ylo in range(2):
        for core in range(2):
            for x in range(4):
                for yhi in range(2):
                    tx, ty = (v % 4 for v in move(core, x, 2 * yhi + ylo))
                    source = ((ylo * 2 + core) * 4 + x) * 2 + yhi
                    target = (((ty % 2) * 2 + core) * 4 + tx) * 2 + ty // 2
                    pairs.append((source, target))
    return pairs


def along(step):
    return plane_perm(lambda c, x, y: (x + step, y) if c == 0 else (x, y + step))


def across(step):
    return plane_perm(lambda c, x, y: (x, y + step) if c == 0 else (x + step, y))


def outward():
    n = lax.axis_size(SEQ)
    pairs = []
    for i in range(n):
        j = i - 1 if i % 2 == 0 else i + 1
        if 0 <= j < n:
            pairs.append((i, j))
    return pairs


def swap(v):
    return lax.ppermute(v, "core", [(0, 1), (1, 0)])


def normalise(values, gain):
    floats = values.astype(F32)
    factor = lax.rsqrt(jnp.mean(floats * floats, axis=-1, keepdims=True) + 1e-06)
    return jax.nn.gelu(floats * factor * gain).astype(BF16)


def shards(inputs, gain, param, cotangent, noise):
    seqs, span, width = inputs.shape
    rows = param.shape[0]
    outs = 2 * rows
    half = width // 2
    scale = 1.0 / math.sqrt(3.0 * width)
    total_rows = seqs * span * 256
    eta = math.sqrt(3.0 * width / total_rows)
    core, ylo, yhi, x, z = (lax.axis_index(a) for a in ("core", "ylo", "yhi", "x", "z"))
    y = 2 * yhi + ylo
    first = core == 0
    me = jnp.where(first, x, y)
    over = jnp.where(first, y, x)

    edge = jnp.where(first, inputs[:, :D], inputs[:, span - D :])
    edge = lax.ppermute(edge, SEQ, outward())

    mate = swap(cotangent)
    chip = jnp.stack([jnp.where(first, cotangent, mate), jnp.where(first, mate, cotangent)], 1)
    cots = [lax.dynamic_slice_in_dim(chip, lax.rem(me + d, 4) * outs, outs, 3) for d in range(4)]
    cots = [cots[0]] + [lax.ppermute(cots[d], PLANE, along(d)) for d in range(1, 4)]
    cots = [c.reshape(seqs, 2 * span, outs) for c in cots]

    own = normalise(inputs, gain)
    edge = normalise(edge, gain)
    ext = jnp.where(
        first, jnp.concatenate([edge, own], axis=1), jnp.concatenate([own, edge], axis=1)
    )
    low, high = ext[:, :, :half], ext[:, :, half:]
    mine = jnp.where(first, low, high)
    mate = swap(jnp.where(first, high, low))
    block = jnp.concatenate([jnp.where(first, mine, mate), jnp.where(first, mate, mine)], axis=1)

    left = lax.ppermute(block, PLANE, along(1))
    right = lax.ppermute(block, PLANE, along(-1))
    far0 = lax.ppermute(left[:1], PLANE, along(1))
    far1 = lax.ppermute(right[1:], PLANE, along(-1))
    blocks = jnp.concatenate([block, left, far0, far1, right], axis=0)
    cot = jnp.concatenate(cots, axis=0)

    windows = [blocks[:, k * D : k * D + 2 * span] for k in range(3)]
    grad = jnp.stack(
        [
            lax.dot_general(cot, w, (((0, 1), (0, 1)), ((), ())), preferred_element_type=F32)
            for w in windows
        ]
    )
    grad = (grad * scale).astype(BF16)
    quarter = half // 2
    grad = jnp.transpose(grad.reshape(3, 2, rows, 2, quarter), (1, 3, 0, 2, 4))
    grad = grad.reshape(4, 3 * rows, quarter)
    terms = [lax.dynamic_index_in_dim(grad, lax.rem(over + d, 4), 0, False) for d in range(4)]
    terms = [terms[0]] + [lax.ppermute(terms[d], PLANE, across(d)) for d in range(1, 4)]
    summed = sum(t.astype(F32) for t in terms).astype(BF16)
    piece = 3 * rows // 8
    terms = lax.all_to_all(summed.reshape(8, piece, quarter), "z", 0, 0, tiled=True)
    summed = jnp.sum(terms.astype(F32), axis=0).astype(BF16)
    summed = lax.ppermute(
        summed, PLANE, plane_perm(lambda c, x, y: (x, y) if c == 0 else (y, x))
    )
    kernel = jnp.transpose(param, (1, 0, 2))
    at = (z * piece, core * half + ylo * quarter)
    own_param = lax.dynamic_slice(kernel.reshape(3 * rows, width), at, (piece, quarter))
    own_noise = lax.dynamic_slice(
        jnp.transpose(noise, (1, 0, 2)).reshape(3 * rows, width), at, (piece, quarter)
    )
    new = (
        own_param.astype(F32)
        - eta * summed.astype(F32)
        + math.sqrt(2.0 * eta) * own_noise.astype(F32)
    ).astype(BF16)
    new = jnp.broadcast_to(new[None], (16, piece, quarter))
    new = lax.all_to_all(new, ("z", "ylo"), 0, 0, tiled=True)
    new = jnp.transpose(new.reshape(8, 2, piece, quarter), (0, 2, 1, 3)).reshape(3 * rows, half)
    mate = swap(new)
    new = jnp.concatenate([jnp.where(first, new, mate), jnp.where(first, mate, new)], axis=1)
    new_param = jnp.transpose(new.reshape(3, rows, width), (1, 0, 2))

    share = lax.dynamic_slice_in_dim(kernel, core * half, half, 2)
    one = lax.ppermute(share, PLANE, plane_perm(lambda c, x, y: (x, y) if c == 0 else (y, x)))
    two = lax.ppermute(
        share, PLANE, plane_perm(lambda c, x, y: (x, 3 - y) if c == 0 else (y + 2, x))
    )
    order = over < 2
    weights = jnp.concatenate([jnp.where(order, one, two), jnp.where(order, two, one)], axis=1)
    mixed = sum(
        lax.dot_general(w, weights[k], (((2,), (1,)), ((), ())), preferred_element_type=F32)
        for k, w in enumerate(windows)
    )
    mixed = (mixed * scale).astype(BF16).reshape(4, seqs, 2 * span, outs)
    back = [mixed[0]] + [lax.ppermute(mixed[d], PLANE, along(-d)) for d in range(1, 4)]
    total = jnp.zeros((seqs, 2 * span, width), BF16)
    for d in range(4):
        total = lax.dynamic_update_slice_in_dim(total, back[d], lax.rem(me + d, 4) * outs, 2)
    near, away = total[:, :span], total[:, span:]
    mate = swap(jnp.where(first, away, near))
    near = jnp.where(first, near, away)
    outputs = (inputs.astype(F32) + (near.astype(F32) + mate.astype(F32))).astype(BF16)
    return (outputs, new_param)


def solution(mesh):
    fine = Mesh(mesh.devices.reshape(8, 2, 2, 4, 2), ("z", "ylo", "core", "x", "yhi"))
    spread = P(("x", "yhi"), SEQ, None)
    placed = (spread, P(), P(("x", "yhi"), None, None), spread, P(("x", "yhi"), None, None))
    return jax.shard_map(
        shards,
        mesh=fine,
        in_specs=placed,
        out_specs=(spread, P(("x", "yhi"), None, None)),
        check_vma=False,
    )
```

time: 721 us -> 160 us (0.22)
  waiting for transfers between devices: 633 us -> 34.2 us
  starting transfers between devices: 7.23 us -> 55.8 us
  between operations: 14.6 us -> 1.04 us
    unnamed x6 -> x0, waiting for transfers between devices: 411 us -> none
    all_gather x2 -> x0, waiting for transfers between devices: 222 us -> none  [the longest x1 168 us: shards(): lax.all_gather(param, 'fsdp', axis=0, tiled=True)]
    ppermute x2 -> x21, starting transfers between devices: 7.07 us -> 42.5 us  [the longest x3 14.1 us: shards(): lax.ppermute(mixed[d], PLANE, along(-d))]
    ppermute x2 -> x21, waiting for transfers between devices: 0.01 us -> 27.2 us  [the longest x3 14.9 us: shards(): lax.ppermute(mixed[d], PLANE, along(-d))]
    unnamed x12 -> x34, local copies, waits for them, and re-layouts: 25.8 us -> 8.74 us
    all_to_all x0 -> x2, starting transfers between devices: none -> 13.3 us  [the longest x1 9.68 us: shards(): lax.all_to_all(summed.reshape(8, piece, quarter), 'z', 0, 0, tiled=True)]
  transfers between devices with their start and end apart: 6 -> 23, of which waited for: 4 -> 7; matrix products, arithmetic and copies ran while one was open for 3% -> 37% of each run, Pallas kernels for 0% -> 0%
where the time goes in v1:
time: 160 us; the launch traced here: 158 us
  starting transfers between devices  55.8 us (35%)
  waiting for transfers between devices  34.2 us (21%)
  local copies, waits for them, and re-layouts  29.5 us (18%)
  matrix products  20.7 us (13%)
  other arithmetic  17 us (11%)
    ppermute x3, waiting for transfers between devices, shards(): lax.ppermute(mixed[d], PLANE, along(-d))  14.9 us
    ppermute x3, starting transfers between devices, shards(): lax.ppermute(mixed[d], PLANE, along(-d))  14.1 us
    dot_general x3, matrix products, shards(): lax.dot_general(w, weights[k], (((2,), (1,)), ((), ())), preferred_elemen...  10.5 us
    dot_general x3, matrix products, shards(): lax.dot_general(cot, w, (((0, 1), (0, 1)), ((), ())), preferred_element_t...  10.1 us
    all_to_all x1, starting transfers between devices, shards(): lax.all_to_all(summed.reshape(8, piece, quarter), 'z', 0, 0, tiled=True)  9.68 us
    unnamed x34, local copies, waits for them, and re-layouts  8.74 us
    ppermute x1, starting transfers between devices, shards(): lax.ppermute(share, PLANE, plane_perm(lambda c, x, y: (x, y) if c == 0 el...  8.2 us
    ppermute x1, waiting for transfers between devices, shards(): left = lax.ppermute(block, PLANE, along(1))  6.64 us
  transfers between devices with their start and end apart: 23, of which 7 were waited for; matrix products, arithmetic and copies ran while one was open for 37% of the time, Pallas kernels for 0%

profile of v1, /device:TPU:1, one launch (start us, length us, event | category | flops | bytes accessed | tf_op | source)
XLA Modules:
  0.0 158.2 jit_solution(1922131202045812929)
XLA Ops:
  1.7 4.6 %collective-permute-start = (bf16[2,16,1536]{2,1,0:T(8,128)(2,1)S(1)}, bf16[2,16,1536]{2,1,0:T(8,128)(2,1)S(1)}, u32[]{:S(2)}, u32[]{:S(2)}) collective-permute-start(bf16[2,16,1536]{2,1,0:T(8,128)(2,1)S(1)} %slice_select_fusion), channel_id=1, source_target_pairs={{8,16},{16,8},{24,32},{32,24},{40,48},{48,40},{56,64},{64,56},{72,... | collective-permute-start | bytes 294920 | tf_op jit(solution)/shard_map/ppermute | solution.py:71
  12.9 2.0 %collective-permute-start.2 = (bf16[2,288,768]{2,1,0:T(8,128)(2,1)}, bf16[2,288,768]{2,1,0:T(8,128)(2,1)S(1)}, u32[]{:S(2)}, u32[]{:S(2)}) collective-permute-start(bf16[2,288,768]{2,1,0:T(8,128)(2,1)} %get-tuple-element.21), channel_id=1, source_target_pairs={{0,2},{1,3},{2,4},{3,5},{4,6},{5,7},{6,0},{7,1},{8,24},{9,25},{10,... | collective-permute-start | bytes 2654216 | tf_op jit(solution)/shard_map/ppermute | solution.py:89
  14.9 1.4 collective-permute-start.4
  18.7 1.5 collective-permute-start.15
  20.8 6.6 %collective-permute-done.2 = bf16[2,288,768]{2,1,0:T(8,128)(2,1)S(1)} collective-permute-done((bf16[2,288,768]{2,1,0:T(8,128)(2,1)}, bf16[2,288,768]{2,1,0:T(8,128)(2,1)S(1)}, u32[]{:S(2)}, u32[]{:S(2)}) %collective-permute-start.2) | collective-permute-done | bytes 884768 | tf_op jit(solution)/shard_map/ppermute | solution.py:89
  29.0 2.7 %collective-permute-start.5 = (bf16[1,288,768]{2,1,0:T(8,128)(2,1)}, bf16[1,288,768]{2,1,0:T(8,128)(2,1)}, u32[]{:S(2)}, u32[]{:S(2)}) collective-permute-start(bf16[1,288,768]{2,1,0:T(8,128)(2,1)} %slice.79), channel_id=1, source_target_pairs={{0,6},{1,7},{2,0},{3,1},{4,2},{5,3},{6,4},{7,5},{8,25},{9,24},{10,... | collective-permute-start | bytes 1327112 | tf_op jit(solution)/shard_map/ppermute | solution.py:92
  31.7 2.1 %dynamic-slice_bitcast_fusion = bf16[3,192,768]{2,1,0:T(8,128)(2,1)} fusion(bf16[192,3,1536]{2,0,1:T(8,128)(2,1)} %param.7, s32[]{:T(128)S(6)} %select_n.139), kind=kLoop, calls=%fused_computation.53 | loop fusion | bytes 1769476 | tf_op jit(solution)/shard_map/dynamic_slice | solution.py:134
  34.1 2.7 %collective-permute-start.7 = (bf16[3,192,768]{2,1,0:T(8,128)(2,1)}, bf16[3,192,768]{2,1,0:T(8,128)(2,1)}, u32[]{:S(2)}, u32[]{:S(2)}) collective-permute-start(bf16[3,192,768]{2,1,0:T(8,128)(2,1)} %dynamic-slice_bitcast_fusion), channel_id=1, source_target_pairs={{0,17},{1,16},{2,19},{3,18},{4,21},{5,20},{6,23},{7,22},{8,12},{9,... | collective-permute-start | bytes 2654216 | tf_op jit(solution)/shard_map/ppermute | solution.py:136
  38.7 8.2 %collective-permute-start.6 = (bf16[3,192,768]{2,1,0:T(8,128)(2,1)}, bf16[3,192,768]{2,1,0:T(8,128)(2,1)}, u32[]{:S(2)}, u32[]{:S(2)}) collective-permute-start(bf16[3,192,768]{2,1,0:T(8,128)(2,1)} %dynamic-slice_bitcast_fusion), channel_id=1, source_target_pairs={{0,0},{1,1},{2,2},{3,3},{4,4},{5,5},{6,6},{7,7},{8,8},{9,12},{10,2... | collective-permute-start | bytes 2654216 | tf_op jit(solution)/shard_map/ppermute | solution.py:135
  51.9 1.9 %constant_dynamic-update-slice_fusion.2 = bf16[8,288,768]{2,1,0:T(8,128)(2,1)} fusion(bf16[8,288,768]{2,1,0:T(8,128)(2,1)} %constant_dynamic-update-slice_fusion.3, bf16[1,288,768]{2,1,0:T(8,128)(2,1)} %collective-permute-done.3), kind=kLoop, calls=%fused_computation.97 | loop fusion | bytes 884736
  53.8 1.8 %constant_dynamic-update-slice_fusion.1 = bf16[8,288,768]{2,1,0:T(8,128)(2,1)} fusion(bf16[8,288,768]{2,1,0:T(8,128)(2,1)} %constant_dynamic-update-slice_fusion.2, bf16[1,288,768]{2,1,0:T(8,128)(2,1)} %collective-permute-done.5), kind=kLoop, calls=%fused_computation.96 | loop fusion | bytes 884736
  56.7 3.4 %fusion.30 = f32[384,768]{1,0:T(8,128)S(1)} fusion(bf16[8,288,768]{2,1,0:T(8,128)(2,1)} %constant_dynamic-update-slice_fusion, bf16[2,256,384]{1,2,0:T(8,128)(2,1)S(1)} %copy-done.8, bf16[2,256,384]{1,2,0:T(8,128)(2,1)S(1)} %copy-done.10, bf16[2,256,384]{1,2,0:T(8,128)(2,1)S(1)} %copy-done.12, bf16[2,256,384]{1,2,0:T(8,128)(2,1)S(1)} %copy.22), kind=kOutput, calls=%fused_computation.46 | convolution fusion | flops 1210318848 | bytes 5898240 | tf_op jit(solution)/shard_map/dot_general | solution.py:99
  60.1 2.4 %fusion.27 = f32[384,768]{1,0:T(8,128)} fusion(bf16[8,288,768]{2,1,0:T(8,128)(2,1)S(1)} %copy-done.3, bf16[2,256,384]{1,2,0:T(8,128)(2,1)S(1)} %copy-done.8, bf16[2,256,384]{1,2,0:T(8,128)(2,1)S(1)} %copy-done.10, bf16[2,256,384]{1,2,0:T(8,128)(2,1)S(1)} %copy-done.12, bf16[2,256,384]{1,2,0:T(8,128)(2,1)S(1)} %copy.22), kind=kOutput, calls=%fused_computation.45 | convolution fusion | flops 1210318848 | bytes 5898240 | tf_op jit(solution)/shard_map/dot_general | solution.py:99
  63.3 1.9 %stack.25 = f32[1,2,192,2,384]{4,3,2,1,0:T(2,128)S(1)} reshape(f32[384,768]{1,0:T(8,128)} %fusion.27) | data formatting | bytes 2359296 | tf_op jit(solution)/shard_map/stack | solution.py:97
  66.8 4.3 %fusion.24 = f32[384,768]{1,0:T(8,128)} fusion(bf16[8,288,768]{2,1,0:T(8,128)(2,1)} %constant_dynamic-update-slice_fusion, bf16[2,256,384]{1,2,0:T(8,128)(2,1)S(1)} %copy-done.9, bf16[2,256,384]{1,2,0:T(8,128)(2,1)S(1)} %copy-done.11, bf16[2,256,384]{1,2,0:T(8,128)(2,1)S(1)} %copy-done.13, bf16[2,256,384]{1,2,0:T(8,128)(2,1)S(1)} %copy.22), kind=kOutput, calls=%fused_computation.44 | convolution fusion | flops 1210318848 | bytes 5898240 | tf_op jit(solution)/shard_map/dot_general | solution.py:99
  71.1 1.9 %stack.24 = f32[1,2,192,2,384]{4,3,2,1,0:T(2,128)S(1)} reshape(f32[384,768]{1,0:T(8,128)} %fusion.24) | data formatting | bytes 2359296 | tf_op jit(solution)/shard_map/stack | solution.py:97
  75.0 3.7 %collective-permute-start.17 = (bf16[576,384]{1,0:T(8,128)(2,1)S(1)}, bf16[576,384]{1,0:T(8,128)(2,1)S(1)}, u32[]{:S(2)}, u32[]{:S(2)}) collective-permute-start(bf16[576,384]{1,0:T(8,128)(2,1)S(1)} %get-tuple-element.6), channel_id=1, source_target_pairs={{0,1},{1,0},{2,3},{3,2},{4,5},{5,4},{6,7},{7,6},{8,12},{9,13},{10,... | collective-permute-start | bytes 1327112 | tf_op jit(solution)/shard_map/ppermute | solution.py:108
  78.8 1.7 %broadcast_select_fusion.2 = (bf16[3,192,768]{2,1,0:T(8,128)(2,1)S(1)}, bf16[3,192,768]{2,1,0:T(8,128)(2,1)S(1)}) fusion(bf16[3,192,768]{2,1,0:T(8,128)(2,1)} %collective-permute-done.7, bf16[3,192,768]{2,1,0:T(8,128)(2,1)} %collective-permute-done.6, pred[]{:T(512)S(6)} %lt.43), kind=kLoop, calls=%fused_computation.56 | loop fusion | flops 884736 | bytes 3538945 | tf_op jit(solution)/shard_map/jit(_where)/select_n | solution.py:140
  81.3 3.5 %fusion.11 = f32[8,256,384]{2,1,0:T(8,128)} fusion(bf16[8,288,768]{2,1,0:T(8,128)(2,1)S(1)} %copy-done.4, bf16[3,192,768]{2,1,0:T(8,128)(2,1)S(1)} %get-tuple-element.8, bf16[3,192,768]{2,1,0:T(8,128)(2,1)S(1)} %get-tuple-element.7), kind=kOutput, calls=%fused_computation.13 | convolution fusion | flops 1209139200 | bytes 8060928 | tf_op jit(solution)/shard_map/dot_general | solution.py:142
  84.8 4.7 %collective-permute-done.16 = bf16[576,384]{1,0:T(8,128)(2,1)S(1)} collective-permute-done((bf16[576,384]{1,0:T(8,128)(2,1)S(1)}, bf16[576,384]{1,0:T(8,128)(2,1)S(1)}, u32[]{:S(2)}, u32[]{:S(2)}) %collective-permute-start.16) | collective-permute-done | bytes 442400 | tf_op jit(solution)/shard_map/ppermute | solution.py:108
  90.5 9.7 %all-to-all-start = ((bf16[8,72,384]{2,1,0:T(8,128)(2,1)}), bf16[8,72,384]{2,1,0:T(8,128)(2,1)S(1)}, u32[]{:S(2)}, u32[]{:S(2)}) async-start(bf16[8,72,384]{2,1,0:T(8,128)(2,1)} %bitcast.25), calls=%async_computation | async-start | bytes 884736 | tf_op jit(solution)/shard_map/all_to_all | solution.py:111
  100.2 3.9 %fusion.7 = f32[8,256,384]{2,1,0:T(8,128)S(1)} fusion(bf16[8,288,768]{2,1,0:T(8,128)(2,1)} %constant_dynamic-update-slice_fusion, bf16[3,192,768]{2,1,0:T(8,128)(2,1)S(1)} %get-tuple-element.8, bf16[3,192,768]{2,1,0:T(8,128)(2,1)S(1)} %get-tuple-element.7), kind=kOutput, calls=%fused_computation.9 | convolution fusion | flops 1209139200 | bytes 8060928 | tf_op jit(solution)/shard_map/dot_general | solution.py:142
  104.1 3.1 %multiply_convert_fusion = bf16[8,256,384]{2,1,0:T(8,128)(2,1)} fusion(f32[8,256,384]{2,1,0:T(8,128)S(1)} %copy-done.6, f32[8,256,384]{2,1,0:T(8,128)S(1)} %fusion.7, bf16[8,288,768]{2,1,0:T(8,128)(2,1)S(1)} %copy-done.5, bf16[3,192,768]{2,1,0:T(8,128)(2,1)S(1)} %get-tuple-element.7, bf16[3,192,768]{2,1,0:T(8,128)(2,1)S(1)} %get-tuple-element.8), kind=kOutput, calls=%fused_computation.2 | convolution fusion | flops 1212284928 | bytes 12779520 | tf_op jit(solution)/shard_map/dot_general | solution.py:142
  107.2 5.1 %all-to-all-done = bf16[8,72,384]{2,1,0:T(8,128)(2,1)S(1)} async-done(((bf16[8,72,384]{2,1,0:T(8,128)(2,1)}), bf16[8,72,384]{2,1,0:T(8,128)(2,1)S(1)}, u32[]{:S(2)}, u32[]{:S(2)}) %all-to-all-start) | async-done | bytes 442400 | tf_op jit(solution)/shard_map/all_to_all | solution.py:111
  114.8 8.3 %collective-permute-start.8 = (bf16[2,256,384]{2,1,0:T(8,128)(2,1)}, bf16[2,256,384]{2,1,0:T(8,128)(2,1)}, u32[]{:S(2)}, u32[]{:S(2)}) collective-permute-start(bf16[2,256,384]{2,1,0:T(8,128)(2,1)} %get-tuple-element.17), channel_id=1, source_target_pairs={{0,6},{1,7},{2,0},{3,1},{4,2},{5,3},{6,4},{7,5},{8,25},{9,24},{10,... | collective-permute-start | bytes 1179656 | tf_op jit(solution)/shard_map/ppermute | solution.py:146
  125.0 3.6 %all-to-all-start.1 = ((bf16[16,72,384]{2,1,0:T(8,128)(2,1)}), bf16[16,72,384]{2,1,0:T(8,128)(2,1)S(1)}, u32[]{:S(2)}, u32[]{:S(2)}) async-start(bf16[16,72,384]{2,1,0:T(8,128)(2,1)} %broadcast_in_dim.5), calls=%async_computation.1 | async-start | bytes 1769472 | tf_op jit(solution)/shard_map/all_to_all | solution.py:128
  128.6 4.2 %collective-permute-start.9 = (bf16[2,256,384]{2,1,0:T(8,128)(2,1)}, bf16[2,256,384]{2,1,0:T(8,128)(2,1)S(1)}, u32[]{:S(2)}, u32[]{:S(2)}) collective-permute-start(bf16[2,256,384]{2,1,0:T(8,128)(2,1)} %get-tuple-element.16), channel_id=1, source_target_pairs={{0,4},{1,5},{2,6},{3,7},{4,0},{5,1},{6,2},{7,3},{8,9},{9,8},{10,11... | collective-permute-start | bytes 1179656 | tf_op jit(solution)/shard_map/ppermute | solution.py:146
  132.9 1.5 collective-permute-start.10
  135.5 5.0 %collective-permute-done.9 = bf16[2,256,384]{2,1,0:T(8,128)(2,1)S(1)} collective-permute-done((bf16[2,256,384]{2,1,0:T(8,128)(2,1)}, bf16[2,256,384]{2,1,0:T(8,128)(2,1)S(1)}, u32[]{:S(2)}, u32[]{:S(2)}) %collective-permute-start.9) | collective-permute-done | bytes 393248 | tf_op jit(solution)/shard_map/ppermute | solution.py:146
  140.5 9.9 %collective-permute-done.10 = bf16[2,256,384]{2,1,0:T(8,128)(2,1)S(1)} collective-permute-done((bf16[2,256,384]{2,1,0:T(8,128)(2,1)}, bf16[2,256,384]{2,1,0:T(8,128)(2,1)S(1)}, u32[]{:S(2)}, u32[]{:S(2)}) %collective-permute-start.10) | collective-permute-done | bytes 393248 | tf_op jit(solution)/shard_map/ppermute | solution.py:146
  151.5 1.9 %all-to-all-done.1 = bf16[16,72,384]{2,1,0:T(8,128)(2,1)S(1)} async-done(((bf16[16,72,384]{2,1,0:T(8,128)(2,1)}), bf16[16,72,384]{2,1,0:T(8,128)(2,1)S(1)}, u32[]{:S(2)}, u32[]{:S(2)}) %all-to-all-start.1) | async-done | bytes 884768 | tf_op jit(solution)/shard_map/all_to_all | solution.py:128
  154.3 2.4 %fusion.22 = bf16[2,128,1536]{2,1,0:T(8,128)(2,1)} fusion(bf16[2,128,1536]{2,1,0:T(8,128)(2,1)S(1)} %copy-done, bf16[2,128,1536]{2,1,0:T(8,128)(2,1)} %collective-permute-done.11, pred[]{:T(512)S(6)} %eq.3, bf16[2,256,1536]{2,1,0:T(8,128)(2,1)S(1)} %constant_dynamic-update-slice_fusion.5), kind=kLoop, calls=%fused_computation.41 | loop fusion | flops 2752512 | bytes 3932161 | tf_op jit(solution)/shard_map/convert_element_type | solution.py:153
  (102 shorter events, 35.4 us)
Async XLA Ops:
  0.6 7.0 %copy-start = (bf16[2,128,1536]{2,1,0:T(8,128)(2,1)S(1)}, bf16[2,128,1536]{2,1,0:T(8,128)(2,1)}, u32[]{:S(2)}) copy-start(bf16[2,128,1536]{2,1,0:T(8,128)(2,1)} %param.5) | copy-start | bytes 2359300
  0.6 8.6 %copy-start.14 = (f32[1536]{0:T(1024)S(1)}, f32[1536]{0:T(1024)}, u32[]{:S(2)}) copy-start(f32[1536]{0:T(1024)} %param.6) | copy-start | bytes 18436
  1.7 7.4 %collective-permute-start = (bf16[2,16,1536]{2,1,0:T(8,128)(2,1)S(1)}, bf16[2,16,1536]{2,1,0:T(8,128)(2,1)S(1)}, u32[]{:S(2)}, u32[]{:S(2)}) collective-permute-start(bf16[2,16,1536]{2,1,0:T(8,128)(2,1)S(1)} %slice_select_fusion), channel_id=1, source_target_pairs={{8,16},{16,8},{24,32},{32,24},{40,48},{48,40},{56,64},{64,56},{72,... | collective-permute-start | bytes 294920 | tf_op jit(solution)/shard_map/ppermute | solution.py:71
  9.6 1.9 %collective-permute-start.1 = (bf16[2,144,768]{2,1,0:T(8,128)(2,1)S(1)}, bf16[2,144,768]{2,1,0:T(8,128)(2,1)S(1)}, u32[]{:S(2)}, u32[]{:S(2)}) collective-permute-start(bf16[2,144,768]{2,1,0:T(8,128)(2,1)S(1)} %broadcast_select_fusion.7), channel_id=1, source_target_pairs={{0,8},{8,0},{1,9},{9,1},{2,10},{10,2},{3,11},{11,3},{4,12},{12,4},... | collective-permute-start | bytes 1327112 | tf_op jit(solution)/shard_map/ppermute | solution.py:47
  10.5 5.9 %collective-permute-start.12 = (bf16[2,128,1536]{2,1,0:T(8,128)(2,1)S(1)}, bf16[2,128,1536]{2,1,0:T(8,128)(2,1)}, u32[]{:S(2)}, u32[]{:S(2)}) collective-permute-start(bf16[2,128,1536]{2,1,0:T(8,128)(2,1)S(1)} %copy-done.7), channel_id=1, source_target_pairs={{0,8},{8,0},{1,9},{9,1},{2,10},{10,2},{3,11},{11,3},{4,12},{12,4},... | collective-permute-start | bytes 2359304 | tf_op jit(solution)/shard_map/ppermute | solution.py:47
  12.9 14.5 %collective-permute-start.2 = (bf16[2,288,768]{2,1,0:T(8,128)(2,1)}, bf16[2,288,768]{2,1,0:T(8,128)(2,1)S(1)}, u32[]{:S(2)}, u32[]{:S(2)}) collective-permute-start(bf16[2,288,768]{2,1,0:T(8,128)(2,1)} %get-tuple-element.21), channel_id=1, source_target_pairs={{0,2},{1,3},{2,4},{3,5},{4,6},{5,7},{6,0},{7,1},{8,24},{9,25},{10,... | collective-permute-start | bytes 2654216 | tf_op jit(solution)/shard_map/ppermute | solution.py:89
  14.9 13.3 %collective-permute-start.4 = (bf16[2,288,768]{2,1,0:T(8,128)(2,1)}, bf16[2,288,768]{2,1,0:T(8,128)(2,1)S(1)}, u32[]{:S(2)}, u32[]{:S(2)}) collective-permute-start(bf16[2,288,768]{2,1,0:T(8,128)(2,1)} %get-tuple-element.21), channel_id=1, source_target_pairs={{0,6},{1,7},{2,0},{3,1},{4,2},{5,3},{6,4},{7,5},{8,25},{9,24},{10,... | collective-permute-start | bytes 2654216 | tf_op jit(solution)/shard_map/ppermute | solution.py:90
  18.7 15.3 %collective-permute-start.15 = (bf16[2,2,128,384]{3,2,0,1:T(8,128)(2,1)}, bf16[2,2,128,384]{3,2,0,1:T(8,128)(2,1)}, u32[]{:S(2)}, u32[]{:S(2)}) collective-permute-start(bf16[2,2,128,384]{3,2,0,1:T(8,128)(2,1)} %get-tuple-element.12), channel_id=1, source_target_pairs={{0,6},{1,7},{2,0},{3,1},{4,2},{5,3},{6,4},{7,5},{8,25},{9,24},{10,... | collective-permute-start | bytes 1179656 | tf_op jit(solution)/shard_map/ppermute | solution.py:76
  20.2 18.5 %collective-permute-start.14 = (bf16[2,2,128,384]{3,2,0,1:T(8,128)(2,1)}, bf16[2,2,128,384]{3,2,0,1:T(8,128)(2,1)}, u32[]{:S(2)}, u32[]{:S(2)}) collective-permute-start(bf16[2,2,128,384]{3,2,0,1:T(8,128)(2,1)} %get-tuple-element.11), channel_id=1, source_target_pairs={{0,4},{1,5},{2,6},{3,7},{4,0},{5,1},{6,2},{7,3},{8,9},{9,8},{10,11... | collective-permute-start | bytes 1179656 | tf_op jit(solution)/shard_map/ppermute | solution.py:76
  20.5 28.4 %collective-permute-start.13 = (bf16[2,2,128,384]{3,2,0,1:T(8,128)(2,1)}, bf16[2,2,128,384]{3,2,0,1:T(8,128)(2,1)}, u32[]{:S(2)}, u32[]{:S(2)}) collective-permute-start(bf16[2,2,128,384]{3,2,0,1:T(8,128)(2,1)} %get-tuple-element.10), channel_id=1, source_target_pairs={{0,2},{1,3},{2,4},{3,5},{4,6},{5,7},{6,0},{7,1},{8,24},{9,25},{10,... | collective-permute-start | bytes 1179656 | tf_op jit(solution)/shard_map/ppermute | solution.py:76
  28.2 23.7 %collective-permute-start.3 = (bf16[1,288,768]{2,1,0:T(8,128)(2,1)}, bf16[1,288,768]{2,1,0:T(8,128)(2,1)}, u32[]{:S(2)}, u32[]{:S(2)}) collective-permute-start(bf16[1,288,768]{2,1,0:T(8,128)(2,1)} %slice.78), channel_id=1, source_target_pairs={{0,2},{1,3},{2,4},{3,5},{4,6},{5,7},{6,0},{7,1},{8,24},{9,25},{10,... | collective-permute-start | bytes 1327112 | tf_op jit(solution)/shard_map/ppermute | solution.py:91
  29.0 24.8 %collective-permute-start.5 = (bf16[1,288,768]{2,1,0:T(8,128)(2,1)}, bf16[1,288,768]{2,1,0:T(8,128)(2,1)}, u32[]{:S(2)}, u32[]{:S(2)}) collective-permute-start(bf16[1,288,768]{2,1,0:T(8,128)(2,1)} %slice.79), channel_id=1, source_target_pairs={{0,6},{1,7},{2,0},{3,1},{4,2},{5,3},{6,4},{7,5},{8,25},{9,24},{10,... | collective-permute-start | bytes 1327112 | tf_op jit(solution)/shard_map/ppermute | solution.py:92
  34.1 44.7 %collective-permute-start.7 = (bf16[3,192,768]{2,1,0:T(8,128)(2,1)}, bf16[3,192,768]{2,1,0:T(8,128)(2,1)}, u32[]{:S(2)}, u32[]{:S(2)}) collective-permute-start(bf16[3,192,768]{2,1,0:T(8,128)(2,1)} %dynamic-slice_bitcast_fusion), channel_id=1, source_target_pairs={{0,17},{1,16},{2,19},{3,18},{4,21},{5,20},{6,23},{7,22},{8,12},{9,... | collective-permute-start | bytes 2654216 | tf_op jit(solution)/shard_map/ppermute | solution.py:136
  38.7 40.1 %collective-permute-start.6 = (bf16[3,192,768]{2,1,0:T(8,128)(2,1)}, bf16[3,192,768]{2,1,0:T(8,128)(2,1)}, u32[]{:S(2)}, u32[]{:S(2)}) collective-permute-start(bf16[3,192,768]{2,1,0:T(8,128)(2,1)} %dynamic-slice_bitcast_fusion), channel_id=1, source_target_pairs={{0,0},{1,1},{2,2},{3,3},{4,4},{5,5},{6,6},{7,7},{8,8},{9,12},{10,2... | collective-permute-start | bytes 2654216 | tf_op jit(solution)/shard_map/ppermute | solution.py:135
  51.9 4.7 %copy-start.8 = (bf16[2,256,384]{1,2,0:T(8,128)(2,1)S(1)}, bf16[2,256,384]{1,2,0:T(8,128)(2,1)}, u32[]{:S(2)}) copy-start(bf16[2,256,384]{1,2,0:T(8,128)(2,1)} %copy.25) | copy-start | bytes 1179652
  51.9 4.7 %copy-start.10 = (bf16[2,256,384]{1,2,0:T(8,128)(2,1)S(1)}, bf16[2,256,384]{1,2,0:T(8,128)(2,1)}, u32[]{:S(2)}) copy-start(bf16[2,256,384]{1,2,0:T(8,128)(2,1)} %copy.24) | copy-start | bytes 1179652
  51.9 4.7 %copy-start.12 = (bf16[2,256,384]{1,2,0:T(8,128)(2,1)S(1)}, bf16[2,256,384]{1,2,0:T(8,128)(2,1)}, u32[]{:S(2)}) copy-start(bf16[2,256,384]{1,2,0:T(8,128)(2,1)} %copy.23) | copy-start | bytes 1179652
  56.7 3.4 %copy-start.3 = (bf16[8,288,768]{2,1,0:T(8,128)(2,1)S(1)}, bf16[8,288,768]{2,1,0:T(8,128)(2,1)}, u32[]{:S(2)}) copy-start(bf16[8,288,768]{2,1,0:T(8,128)(2,1)} %constant_dynamic-update-slice_fusion) | copy-start | bytes 10616836
  74.9 9.9 %collective-permute-start.18 = (bf16[576,384]{1,0:T(8,128)(2,1)S(1)}, bf16[576,384]{1,0:T(8,128)(2,1)S(1)}, u32[]{:S(2)}, u32[]{:S(2)}) collective-permute-start(bf16[576,384]{1,0:T(8,128)(2,1)S(1)} %get-tuple-element.5), channel_id=1, source_target_pairs={{0,17},{1,16},{2,19},{3,18},{4,21},{5,20},{6,23},{7,22},{8,14},{9,... | collective-permute-start | bytes 1327112 | tf_op jit(solution)/shard_map/ppermute | solution.py:108
  75.0 9.8 %collective-permute-start.17 = (bf16[576,384]{1,0:T(8,128)(2,1)S(1)}, bf16[576,384]{1,0:T(8,128)(2,1)S(1)}, u32[]{:S(2)}, u32[]{:S(2)}) collective-permute-start(bf16[576,384]{1,0:T(8,128)(2,1)S(1)} %get-tuple-element.6), channel_id=1, source_target_pairs={{0,1},{1,0},{2,3},{3,2},{4,5},{5,4},{6,7},{7,6},{8,12},{9,13},{10,... | collective-permute-start | bytes 1327112 | tf_op jit(solution)/shard_map/ppermute | solution.py:108
  78.8 2.5 %copy-start.4 = (bf16[8,288,768]{2,1,0:T(8,128)(2,1)S(1)}, bf16[8,288,768]{2,1,0:T(8,128)(2,1)}, u32[]{:S(2)}) copy-start(bf16[8,288,768]{2,1,0:T(8,128)(2,1)} %constant_dynamic-update-slice_fusion) | copy-start | bytes 10616836
  78.8 10.7 %collective-permute-start.16 = (bf16[576,384]{1,0:T(8,128)(2,1)S(1)}, bf16[576,384]{1,0:T(8,128)(2,1)S(1)}, u32[]{:S(2)}, u32[]{:S(2)}) collective-permute-start(bf16[576,384]{1,0:T(8,128)(2,1)S(1)} %get-tuple-element.4), channel_id=1, source_target_pairs={{0,16},{1,17},{2,18},{3,19},{4,20},{5,21},{6,22},{7,23},{8,10},{9,... | collective-permute-start | bytes 1327112 | tf_op jit(solution)/shard_map/ppermute | solution.py:108
  90.5 21.9 %all-to-all-start = ((bf16[8,72,384]{2,1,0:T(8,128)(2,1)}), bf16[8,72,384]{2,1,0:T(8,128)(2,1)S(1)}, u32[]{:S(2)}, u32[]{:S(2)}) async-start(bf16[8,72,384]{2,1,0:T(8,128)(2,1)} %bitcast.25), calls=%async_computation | async-start | bytes 884736 | tf_op jit(solution)/shard_map/all_to_all | solution.py:111
  100.2 3.9 %copy-start.5 = (bf16[8,288,768]{2,1,0:T(8,128)(2,1)S(1)}, bf16[8,288,768]{2,1,0:T(8,128)(2,1)}, u32[]{:S(2)}) copy-start(bf16[8,288,768]{2,1,0:T(8,128)(2,1)} %constant_dynamic-update-slice_fusion) | copy-start | bytes 10616836
  100.2 3.9 %copy-start.6 = (f32[8,256,384]{2,1,0:T(8,128)S(1)}, f32[8,256,384]{2,1,0:T(8,128)}, u32[]{:S(2)}) copy-start(f32[8,256,384]{2,1,0:T(8,128)} %fusion.11) | copy-start | bytes 9437188
  112.4 10.7 %collective-permute-start.19 = (bf16[72,384]{1,0:T(8,128)(2,1)S(1)}, bf16[72,384]{1,0:T(8,128)(2,1)S(1)}, u32[]{:S(2)}, u32[]{:S(2)}) collective-permute-start(bf16[72,384]{1,0:T(8,128)(2,1)S(1)} %reduce_sum.32), channel_id=1, source_target_pairs={{0,0},{1,1},{2,2},{3,3},{4,4},{5,5},{6,6},{7,7},{8,8},{9,12},{10,2... | collective-permute-start | bytes 165896 | tf_op jit(solution)/shard_map/ppermute | solution.py:113
  114.8 19.6 %collective-permute-start.8 = (bf16[2,256,384]{2,1,0:T(8,128)(2,1)}, bf16[2,256,384]{2,1,0:T(8,128)(2,1)}, u32[]{:S(2)}, u32[]{:S(2)}) collective-permute-start(bf16[2,256,384]{2,1,0:T(8,128)(2,1)} %get-tuple-element.17), channel_id=1, source_target_pairs={{0,6},{1,7},{2,0},{3,1},{4,2},{5,3},{6,4},{7,5},{8,25},{9,24},{10,... | collective-permute-start | bytes 1179656 | tf_op jit(solution)/shard_map/ppermute | solution.py:146
  125.0 28.4 %all-to-all-start.1 = ((bf16[16,72,384]{2,1,0:T(8,128)(2,1)}), bf16[16,72,384]{2,1,0:T(8,128)(2,1)S(1)}, u32[]{:S(2)}, u32[]{:S(2)}) async-start(bf16[16,72,384]{2,1,0:T(8,128)(2,1)} %broadcast_in_dim.5), calls=%async_computation.1 | async-start | bytes 1769472 | tf_op jit(solution)/shard_map/all_to_all | solution.py:128
  128.6 11.8 %collective-permute-start.9 = (bf16[2,256,384]{2,1,0:T(8,128)(2,1)}, bf16[2,256,384]{2,1,0:T(8,128)(2,1)S(1)}, u32[]{:S(2)}, u32[]{:S(2)}) collective-permute-start(bf16[2,256,384]{2,1,0:T(8,128)(2,1)} %get-tuple-element.16), channel_id=1, source_target_pairs={{0,4},{1,5},{2,6},{3,7},{4,0},{5,1},{6,2},{7,3},{8,9},{9,8},{10,11... | collective-permute-start | bytes 1179656 | tf_op jit(solution)/shard_map/ppermute | solution.py:146
  132.9 17.6 %collective-permute-start.10 = (bf16[2,256,384]{2,1,0:T(8,128)(2,1)}, bf16[2,256,384]{2,1,0:T(8,128)(2,1)S(1)}, u32[]{:S(2)}, u32[]{:S(2)}) collective-permute-start(bf16[2,256,384]{2,1,0:T(8,128)(2,1)} %get-tuple-element.15), channel_id=1, source_target_pairs={{0,2},{1,3},{2,4},{3,5},{4,6},{5,7},{6,0},{7,1},{8,24},{9,25},{10,... | collective-permute-start | bytes 1179656 | tf_op jit(solution)/shard_map/ppermute | solution.py:146
  151.5 2.8 %collective-permute-start.11 = (bf16[2,128,1536]{2,1,0:T(8,128)(2,1)}, bf16[2,128,1536]{2,1,0:T(8,128)(2,1)}, u32[]{:S(2)}, u32[]{:S(2)}) collective-permute-start(bf16[2,128,1536]{2,1,0:T(8,128)(2,1)} %broadcast_select_fusion.4), channel_id=1, source_target_pairs={{0,8},{8,0},{1,9},{9,1},{2,10},{10,2},{3,11},{11,3},{4,12},{12,4},... | collective-permute-start | bytes 2359304 | tf_op jit(solution)/shard_map/ppermute | solution.py:47
  154.2 2.5 %collective-permute-start.20 = (bf16[576,768]{1,0:T(8,128)(2,1)S(1)}, bf16[576,768]{1,0:T(8,128)(2,1)S(1)}, u32[]{:S(2)}, u32[]{:S(2)}) collective-permute-start(bf16[576,768]{1,0:T(8,128)(2,1)S(1)} %bitcast.60), channel_id=1, source_target_pairs={{0,8},{8,0},{1,9},{9,1},{2,10},{10,2},{3,11},{11,3},{4,12},{12,4},... | collective-permute-start | bytes 2654216 | tf_op jit(solution)/shard_map/ppermute | solution.py:47
  (6 other events, 8.0 us)

commit v2 on v1

--- a/solution.py
+++ b/solution.py
@@ -1,8 +1,11 @@
+import functools
 import math
 
 import jax
 import jax.numpy as jnp
 from jax import lax
+from jax.experimental import pallas as pl
+from jax.experimental.pallas import tpu as pltpu
 from jax.sharding import Mesh, PartitionSpec as P
 
 D = 16
@@ -51,6 +54,78 @@
     floats = values.astype(F32)
     factor = lax.rsqrt(jnp.mean(floats * floats, axis=-1, keepdims=True) + 1e-06)
     return jax.nn.gelu(floats * factor * gain).astype(BF16)
+
+
+def in_vmem(count):
+    return [pl.BlockSpec(memory_space=pltpu.VMEM)] * count
+
+
+def call(kernel, shapes, scalars, arrays, flops, scratch=()):
+    size = sum(math.prod(a.shape) * a.dtype.itemsize for a in (*arrays, *shapes))
+    return pl.pallas_call(
+        kernel,
+        out_shape=shapes,
+        in_specs=[pl.BlockSpec(memory_space=pltpu.SMEM)] * len(scalars) + in_vmem(len(arrays)),
+        out_specs=in_vmem(len(shapes)),
+        scratch_shapes=list(scratch),
+        cost_estimate=pl.CostEstimate(flops=flops, bytes_accessed=size, transcendentals=0),
+        compiler_params=pltpu.CompilerParams(vmem_limit_bytes=40 * 2**20),
+    )(*scalars, *arrays)
+
+
+def turn_kernel(*refs):
+    for source, target in zip(refs[:4], refs[4:]):
+        for b in range(2):
+            n = source.shape[1]
+            target[:, b * n : (b + 1) * n] = source[b].T
+
+
+def grad_kernel(scale, over, *refs):
+    turned, blocks, out = refs[:4], refs[4:8], refs[8]
+    outs = turned[0].shape[0]
+    rows, n = outs // 2, turned[0].shape[1] // 2
+    width = blocks[0].shape[2]
+    quarter, tile = width // 2, 256
+    for k in range(3):
+        for at in range(0, width, tile):
+            total = jnp.zeros((outs, tile), F32)
+            for t, block in zip(turned, blocks):
+                for b in range(2):
+                    total += jnp.dot(
+                        t[:, b * n : (b + 1) * n],
+                        block[b, k * D : k * D + n, at : at + tile],
+                        preferred_element_type=F32,
+                    )
+            total = (total * scale).astype(BF16)
+            for sub in range(2):
+                lo, hi = max(at, sub * quarter), min(at + tile, (sub + 1) * quarter)
+                if lo >= hi:
+                    continue
+                for part in range(2):
+                    slot = (2 * part + sub - over[0] + 4) & 3
+                    out[slot, k * rows : (k + 1) * rows, lo - sub * quarter : hi - sub * quarter] = (
+                        total[part * rows : (part + 1) * rows, lo - at : hi - at]
+                    )
+
+
+def mixed_kernel(scale, over, one, two, *refs):
+    blocks, results, weights = refs[:4], refs[4:8], refs[8]
+    rows, n = one.shape[1], results[0].shape[1]
+    swapped = jnp.where(over[0] < 2, 0, rows)
+    for k in range(3):
+        weights[k, pl.ds(pl.multiple_of(swapped, rows), rows), :] = one[k]
+        weights[k, pl.ds(pl.multiple_of(rows - swapped, rows), rows), :] = two[k]
+    for block, result in zip(blocks, results):
+        for b in range(2):
+            total = jnp.zeros((n, 2 * rows), F32)
+            for k in range(3):
+                total += lax.dot_general(
+                    block[b, k * D : k * D + n],
+                    weights[k],
+                    (((1,), (1,)), ((), ())),
+                    preferred_element_type=F32,
+                )
+            result[b] = (total * scale).astype(BF16)
 
 
 def shards(inputs, gain, param, cotangent, noise):
@@ -71,10 +146,11 @@
     edge = lax.ppermute(edge, SEQ, outward())
 
     mate = swap(cotangent)
-    chip = jnp.stack([jnp.where(first, cotangent, mate), jnp.where(first, mate, cotangent)], 1)
-    cots = [lax.dynamic_slice_in_dim(chip, lax.rem(me + d, 4) * outs, outs, 3) for d in range(4)]
+    chip = jnp.concatenate(
+        [jnp.where(first, cotangent, mate), jnp.where(first, mate, cotangent)], axis=1
+    )
+    cots = [lax.dynamic_slice_in_dim(chip, lax.rem(me + d, 4) * outs, outs, 2) for d in range(4)]
     cots = [cots[0]] + [lax.ppermute(cots[d], PLANE, along(d)) for d in range(1, 4)]
-    cots = [c.reshape(seqs, 2 * span, outs) for c in cots]
 
     own = normalise(inputs, gain)
     edge = normalise(edge, gain)
@@ -86,26 +162,25 @@
     mate = swap(jnp.where(first, high, low))
     block = jnp.concatenate([jnp.where(first, mine, mate), jnp.where(first, mate, mine)], axis=1)
 
-    left = lax.ppermute(block, PLANE, along(1))
-    right = lax.ppermute(block, PLANE, along(-1))
-    far0 = lax.ppermute(left[:1], PLANE, along(1))
-    far1 = lax.ppermute(right[1:], PLANE, along(-1))
-    blocks = jnp.concatenate([block, left, far0, far1, right], axis=0)
-    cot = jnp.concatenate(cots, axis=0)
-
-    windows = [blocks[:, k * D : k * D + 2 * span] for k in range(3)]
-    grad = jnp.stack(
-        [
-            lax.dot_general(cot, w, (((0, 1), (0, 1)), ((), ())), preferred_element_type=F32)
-            for w in windows
-        ]
-    )
-    grad = (grad * scale).astype(BF16)
+    blocks = [block] + [lax.ppermute(block, PLANE, along(d)) for d in (1, 2, 3)]
+
+    at_over = over.astype(jnp.int32).reshape(1)
+    sums = 2 * 4 * seqs * 2 * span * outs * half * 3
+    turned = call(
+        turn_kernel, [jax.ShapeDtypeStruct((outs, seqs * 2 * span), BF16)] * 4, (), cots, 0
+    )
     quarter = half // 2
-    grad = jnp.transpose(grad.reshape(3, 2, rows, 2, quarter), (1, 3, 0, 2, 4))
-    grad = grad.reshape(4, 3 * rows, quarter)
-    terms = [lax.dynamic_index_in_dim(grad, lax.rem(over + d, 4), 0, False) for d in range(4)]
-    terms = [terms[0]] + [lax.ppermute(terms[d], PLANE, across(d)) for d in range(1, 4)]
+    (grad,) = call(
+        functools.partial(grad_kernel, scale),
+        [jax.ShapeDtypeStruct((4, 3 * rows, quarter), BF16)],
+        (at_over,),
+        (*turned, *blocks),
+        sums,
+    )
+    kernel = jnp.transpose(param, (1, 0, 2))
+    share = lax.dynamic_slice_in_dim(kernel, core * half, half, 2)
+    grad, share = lax.optimization_barrier((grad, share))
+    terms = [grad[0]] + [lax.ppermute(grad[d], PLANE, across(d)) for d in range(1, 4)]
     summed = sum(t.astype(F32) for t in terms).astype(BF16)
     piece = 3 * rows // 8
     terms = lax.all_to_all(summed.reshape(8, piece, quarter), "z", 0, 0, tiled=True)
@@ -113,7 +188,6 @@
     summed = lax.ppermute(
         summed, PLANE, plane_perm(lambda c, x, y: (x, y) if c == 0 else (y, x))
     )
-    kernel = jnp.transpose(param, (1, 0, 2))
     at = (z * piece, core * half + ylo * quarter)
     own_param = lax.dynamic_slice(kernel.reshape(3 * rows, width), at, (piece, quarter))
     own_noise = lax.dynamic_slice(
@@ -131,18 +205,18 @@
     new = jnp.concatenate([jnp.where(first, new, mate), jnp.where(first, mate, new)], axis=1)
     new_param = jnp.transpose(new.reshape(3, rows, width), (1, 0, 2))
 
-    share = lax.dynamic_slice_in_dim(kernel, core * half, half, 2)
     one = lax.ppermute(share, PLANE, plane_perm(lambda c, x, y: (x, y) if c == 0 else (y, x)))
     two = lax.ppermute(
         share, PLANE, plane_perm(lambda c, x, y: (x, 3 - y) if c == 0 else (y + 2, x))
     )
-    order = over < 2
-    weights = jnp.concatenate([jnp.where(order, one, two), jnp.where(order, two, one)], axis=1)
-    mixed = sum(
-        lax.dot_general(w, weights[k], (((2,), (1,)), ((), ())), preferred_element_type=F32)
-        for k, w in enumerate(windows)
-    )
-    mixed = (mixed * scale).astype(BF16).reshape(4, seqs, 2 * span, outs)
+    mixed = call(
+        functools.partial(mixed_kernel, scale),
+        [jax.ShapeDtypeStruct((seqs, 2 * span, outs), BF16)] * 4,
+        (at_over,),
+        (one, two, *blocks),
+        sums,
+        [pltpu.VMEM((3, outs, half), BF16)],
+    )
     back = [mixed[0]] + [lax.ppermute(mixed[d], PLANE, along(-d)) for d in range(1, 4)]
     total = jnp.zeros((seqs, 2 * span, width), BF16)
     for d in range(4):

time: 160 us -> 155 us (0.969)
  local copies, waits for them, and re-layouts: 29.5 us -> 8.03 us
  matrix products: 20.7 us -> 0 us
  waiting for transfers between devices: 34.2 us -> 49.8 us
  starting transfers between devices: 55.8 us -> 68.6 us
  Pallas kernels: 0 us -> 12.5 us
  other arithmetic: 17 us -> 12.3 us
    ppermute x3, waiting for transfers between devices: 0.01 us -> 23.4 us  [shards(): lax.ppermute(cots[d], PLANE, along(d))]
    dot_general x6 -> x0, matrix products: 20.7 us -> none  [the longest x3 10.5 us: shards(): lax.dot_general(w, weights[k], (((2,), (1,)), ((), ())), preferred_elemen...]
    ppermute x4, starting transfers between devices: 0.19 us -> 19.3 us  [swap(): return lax.ppermute(v, 'core', [(0, 1), (1, 0)])]
    pallas_call x0 -> x3, Pallas kernels: none -> 12.5 us  [call(): pl.pallas_call(kernel, out_shape=shapes, in_specs=[pl.BlockSpec(memory_sp...]
    ppermute x7 -> x6, waiting for transfers between devices: 11.3 us -> 1.01 us  [the longest x3 1 us: shards(): lax.ppermute(grad[d], PLANE, across(d))]
    ppermute x3, starting transfers between devices: 14.1 us -> 7.06 us  [shards(): lax.ppermute(mixed[d], PLANE, along(-d))]
    unnamed x34 -> x17, local copies, waits for them, and re-layouts: 8.74 us -> 2.47 us
    all_to_all x1, waiting for transfers between devices: 5.12 us -> 11.4 us  [shards(): lax.all_to_all(summed.reshape(8, piece, quarter), 'z', 0, 0, tiled=True)]
  transfers between devices with their start and end apart: 23 -> 22, of which waited for: 7 -> 9; matrix products, arithmetic and copies ran while one was open for 37% -> 10% of each run, Pallas kernels for 0% -> 5%
where the time goes in v2:
time: 155 us; the launch traced here: 152 us
  starting transfers between devices  68.6 us (44%)
  waiting for transfers between devices  49.8 us (32%)
  Pallas kernels  12.5 us (8%)
  other arithmetic  12.3 us (8%)
  local copies, waits for them, and re-layouts  8.03 us (5%)
    ppermute x3, waiting for transfers between devices, shards(): lax.ppermute(cots[d], PLANE, along(d))  23.4 us
    ppermute x4, starting transfers between devices, swap(): return lax.ppermute(v, 'core', [(0, 1), (1, 0)])  19.3 us
    pallas_call x3, Pallas kernels, call(): pl.pallas_call(kernel, out_shape=shapes, in_specs=[pl.BlockSpec(memory_sp...  12.5 us
    ppermute x3, waiting for transfers between devices, shards(): lax.ppermute(mixed[d], PLANE, along(-d))  12.1 us
    all_to_all x1, waiting for transfers between devices, shards(): lax.all_to_all(summed.reshape(8, piece, quarter), 'z', 0, 0, tiled=True)  11.4 us
    all_to_all x1, starting transfers between devices, shards(): lax.all_to_all(summed.reshape(8, piece, quarter), 'z', 0, 0, tiled=True)  11.1 us
    ppermute x1, starting transfers between devices, shards(): lax.ppermute(share, PLANE, plane_perm(lambda c, x, y: (x, y) if c == 0 el...  8.24 us
    ppermute x3, starting transfers between devices, shards(): lax.ppermute(mixed[d], PLANE, along(-d))  7.06 us
  transfers between devices with their start and end apart: 22, of which 9 were waited for; matrix products, arithmetic and copies ran while one was open for 10% of the time, Pallas kernels for 5%

profile of v2, /device:TPU:1, one launch (start us, length us, event | category | flops | bytes accessed | tf_op | source)
XLA Modules:
  0.0 152.2 jit_solution(8490527574238875005)
XLA Ops:
  0.7 1.0 slice_select_fusion
  1.7 4.6 %collective-permute-start.4 = (bf16[2,16,1536]{2,1,0:T(8,128)(2,1)S(1)}, bf16[2,16,1536]{2,1,0:T(8,128)(2,1)S(1)}, u32[]{:S(2)}, u32[]{:S(2)}) collective-permute-start(bf16[2,16,1536]{2,1,0:T(8,128)(2,1)S(1)} %slice_select_fusion), channel_id=1, source_target_pairs={{8,16},{16,8},{24,32},{32,24},{40,48},{48,40},{56,64},{64,56},{72,... | collective-permute-start | bytes 294920 | tf_op jit(solution)/shard_map/ppermute | solution.py:146
  6.3 1.4 fusion
  7.7 1.4 fusion.4
  10.5 1.1 collective-permute-done.5
  11.6 1.1 broadcast_select_fusion.6
  12.8 2.1 %collective-permute-start.6 = (bf16[2,288,768]{2,1,0:T(8,128)(2,1)S(1)}, bf16[2,288,768]{2,1,0:T(8,128)(2,1)S(1)}, u32[]{:S(2)}, u32[]{:S(2)}) collective-permute-start(bf16[2,288,768]{2,1,0:T(8,128)(2,1)S(1)} %pad_maximum_fusion.1.refs_4_.refs_0_), channel_id=1, source_target_pairs={{0,2},{1,3},{2,4},{3,5},{4,6},{5,7},{6,0},{7,1},{8,24},{9,25},{10,... | collective-permute-start | bytes 2654216 | tf_op jit(solution)/shard_map/ppermute | solution.py:165
  14.9 2.6 %collective-permute-start.7 = (bf16[2,288,768]{2,1,0:T(8,128)(2,1)S(1)}, bf16[2,288,768]{2,1,0:T(8,128)(2,1)}, u32[]{:S(2)}, u32[]{:S(2)}) collective-permute-start(bf16[2,288,768]{2,1,0:T(8,128)(2,1)S(1)} %pad_maximum_fusion.1.refs_4_.refs_0_), channel_id=1, source_target_pairs={{0,4},{1,5},{2,6},{3,7},{4,0},{5,1},{6,2},{7,3},{8,9},{9,8},{10,11... | collective-permute-start | bytes 2654216 | tf_op jit(solution)/shard_map/ppermute | solution.py:165
  17.7 1.1 fusion.14
  18.7 1.4 collective-permute-start.1
  20.5 20.1 %collective-permute-done.1.refs_1_ = bf16[2,256,384]{2,1,0:T(8,128)(2,1)S(1)} collective-permute-done((bf16[2,256,384]{2,1,0:T(8,128)(2,1)S(1)}, bf16[2,256,384]{2,1,0:T(8,128)(2,1)S(1)}, u32[]{:S(2)}, u32[]{:S(2)}) %collective-permute-start.1) | collective-permute-done | bytes 393248 | tf_op jit(solution)/shard_map/ppermute | solution.py:153
  40.6 1.7 %collective-permute-start.3 = (bf16[2,256,384]{2,1,0:T(8,128)(2,1)}, bf16[2,256,384]{2,1,0:T(8,128)(2,1)S(1)}, u32[]{:S(2)}, u32[]{:S(2)}) collective-permute-start(bf16[2,256,384]{2,1,0:T(8,128)(2,1)} %get-tuple-element.27), channel_id=1, source_target_pairs={{0,6},{1,7},{2,0},{3,1},{4,2},{5,3},{6,4},{7,5},{8,25},{9,24},{10,... | collective-permute-start | bytes 1179656 | tf_op jit(solution)/shard_map/ppermute | solution.py:153
  42.2 2.1 %dynamic-slice_bitcast_fusion = bf16[3,192,768]{2,1,0:T(8,128)(2,1)} fusion(bf16[192,3,1536]{2,0,1:T(8,128)(2,1)} %param.7, s32[]{:T(128)S(6)} %select_n.120), kind=kLoop, calls=%fused_computation.30 | loop fusion | bytes 1769476 | tf_op jit(solution)/shard_map/dynamic_slice | solution.py:181
  44.4 1.5 collective-permute-done.2.refs_2_
  45.9 1.8 %collective-permute-done.3.refs_3_ = bf16[2,256,384]{2,1,0:T(8,128)(2,1)S(1)} collective-permute-done((bf16[2,256,384]{2,1,0:T(8,128)(2,1)}, bf16[2,256,384]{2,1,0:T(8,128)(2,1)S(1)}, u32[]{:S(2)}, u32[]{:S(2)}) %collective-permute-start.3) | collective-permute-done | bytes 393248 | tf_op jit(solution)/shard_map/ppermute | solution.py:153
  48.2 5.2 %shard_map.69 = bf16[4,576,384]{2,1,0:T(8,128)(2,1)S(1)} custom-call(s32[1]{0:T(128)} %bitcast.over, bf16[384,512]{1,0:T(8,128)(2,1)S(1)} %get-tuple-element.12.refs_0_, bf16[384,512]{1,0:T(8,128)(2,1)S(1)} %get-tuple-element.13.refs_1_, bf16[384,512]{1,0:T(8,128)(2,1)S(1)} %get-tuple-element.14.refs_2_, bf16[384,512]{1,0:T(8,128)(2,1)S(1)} %get-tuple-element.15.refs_3_, ...), custom_call_target="tpu_custom_call" | custom-call | flops 3623878656 | bytes 6881280 | tf_op jit(solution)/shard_map/pallas_call | solution.py:65
  53.6 1.0 collective-permute-start.15
  54.6 2.9 %collective-permute-start.16 = (bf16[576,384]{1,0:T(8,128)(2,1)S(1)}, bf16[576,384]{1,0:T(8,128)(2,1)S(1)}, u32[]{:S(2)}, u32[]{:S(2)}) collective-permute-start(bf16[576,384]{1,0:T(8,128)(2,1)S(1)} %get-tuple-element.26), channel_id=1, source_target_pairs={{0,1},{1,0},{2,3},{3,2},{4,5},{5,4},{6,7},{7,6},{8,12},{9,13},{10,... | collective-permute-start | bytes 1327112 | tf_op jit(solution)/shard_map/ppermute | solution.py:183
  58.8 8.2 %collective-permute-start.9 = (bf16[3,192,768]{2,1,0:T(8,128)(2,1)}, bf16[3,192,768]{2,1,0:T(8,128)(2,1)}, u32[]{:S(2)}, u32[]{:S(2)}) collective-permute-start(bf16[3,192,768]{2,1,0:T(8,128)(2,1)} %dynamic-slice_bitcast_fusion), channel_id=1, source_target_pairs={{0,0},{1,1},{2,2},{3,3},{4,4},{5,5},{6,6},{7,7},{8,8},{9,12},{10,2... | collective-permute-start | bytes 2654216 | tf_op jit(solution)/shard_map/ppermute | solution.py:208
  69.0 11.1 %all-to-all-start = ((bf16[8,72,384]{2,1,0:T(8,128)(2,1)}), bf16[8,72,384]{2,1,0:T(8,128)(2,1)}, u32[]{:S(2)}, u32[]{:S(2)}) async-start(bf16[8,72,384]{2,1,0:T(8,128)(2,1)} %bitcast.8), calls=%async_computation | async-start | bytes 884736 | tf_op jit(solution)/shard_map/all_to_all | solution.py:186
  80.1 11.4 %all-to-all-done = bf16[8,72,384]{2,1,0:T(8,128)(2,1)} async-done(((bf16[8,72,384]{2,1,0:T(8,128)(2,1)}), bf16[8,72,384]{2,1,0:T(8,128)(2,1)}, u32[]{:S(2)}, u32[]{:S(2)}) %all-to-all-start) | async-done | bytes 442400 | tf_op jit(solution)/shard_map/all_to_all | solution.py:186
  91.5 1.1 reduce_sum.32
  93.3 6.8 %shard_map.70 = (bf16[2,256,384]{2,1,0:T(8,128)(2,1)S(1)}, bf16[2,256,384]{2,1,0:T(8,128)(2,1)}, bf16[2,256,384]{2,1,0:T(8,128)(2,1)S(1)}, bf16[2,256,384]{2,1,0:T(8,128)(2,1)S(1)}) custom-call(s32[1]{0:T(128)} %bitcast.over, bf16[3,192,768]{2,1,0:T(8,128)(2,1)} %collective-permute-done.9.one, bf16[3,192,768]{2,1,0:T(8,128)(2,1)S(1)} %collective-permute-done.10.two, ...), custom_call_target="tpu_custom_call" | custom-call | flops 3623878656 | bytes 6881280 | tf_op jit(solution)/shard_map/pallas_call | solution.py:65
  101.6 5.6 %collective-permute-start.11 = (bf16[2,256,384]{2,1,0:T(8,128)(2,1)}, bf16[2,256,384]{2,1,0:T(8,128)(2,1)S(1)}, u32[]{:S(2)}, u32[]{:S(2)}) collective-permute-start(bf16[2,256,384]{2,1,0:T(8,128)(2,1)} %get-tuple-element.18), channel_id=1, source_target_pairs={{0,6},{1,7},{2,0},{3,1},{4,2},{5,3},{6,4},{7,5},{8,25},{9,24},{10,... | collective-permute-start | bytes 1179656 | tf_op jit(solution)/shard_map/ppermute | solution.py:220
  109.1 4.3 %all-to-all-start.1 = ((bf16[16,72,384]{2,1,0:T(8,128)(2,1)}), bf16[16,72,384]{2,1,0:T(8,128)(2,1)}, u32[]{:S(2)}, u32[]{:S(2)}) async-start(bf16[16,72,384]{2,1,0:T(8,128)(2,1)} %broadcast_in_dim.5), calls=%async_computation.1 | async-start | bytes 1769472 | tf_op jit(solution)/shard_map/all_to_all | solution.py:202
  115.2 7.1 %collective-permute-done.12 = bf16[2,256,384]{2,1,0:T(8,128)(2,1)S(1)} collective-permute-done((bf16[2,256,384]{2,1,0:T(8,128)(2,1)S(1)}, bf16[2,256,384]{2,1,0:T(8,128)(2,1)S(1)}, u32[]{:S(2)}, u32[]{:S(2)}) %collective-permute-start.12) | collective-permute-done | bytes 393248 | tf_op jit(solution)/shard_map/ppermute | solution.py:220
  122.3 5.0 %collective-permute-done.13 = bf16[2,256,384]{2,1,0:T(8,128)(2,1)S(1)} collective-permute-done((bf16[2,256,384]{2,1,0:T(8,128)(2,1)S(1)}, bf16[2,256,384]{2,1,0:T(8,128)(2,1)S(1)}, u32[]{:S(2)}, u32[]{:S(2)}) %collective-permute-start.13) | collective-permute-done | bytes 393248 | tf_op jit(solution)/shard_map/ppermute | solution.py:220
  127.5 16.5 %collective-permute-start.14 = (bf16[2,128,1536]{2,1,0:T(8,128)(2,1)S(1)}, bf16[2,128,1536]{2,1,0:T(8,128)(2,1)S(1)}, u32[]{:S(2)}, u32[]{:S(2)}) collective-permute-start(bf16[2,128,1536]{2,1,0:T(8,128)(2,1)S(1)} %broadcast_select_fusion.2), channel_id=1, source_target_pairs={{0,8},{8,0},{1,9},{9,1},{2,10},{10,2},{3,11},{11,3},{4,12},{12,4},... | collective-permute-start | bytes 2359304 | tf_op jit(solution)/shard_map/ppermute | solution.py:50
  144.0 1.9 %copy.7 = bf16[8,72,2,384]{3,2,1,0:T(2,128)(2,1)S(1)} copy(bf16[8,72,2,384]{3,1,2,0:T(8,128)(2,1)} %bitcast.12) | data formatting | bytes 1769472 | tf_op jit(solution)/shard_map/transpose | solution.py:203
  146.0 2.7 %collective-permute-start.19 = (bf16[576,768]{1,0:T(8,128)(2,1)S(1)}, bf16[576,768]{1,0:T(8,128)(2,1)S(1)}, u32[]{:S(2)}, u32[]{:S(2)}) collective-permute-start(bf16[576,768]{1,0:T(8,128)(2,1)S(1)} %bitcast.29), channel_id=1, source_target_pairs={{0,8},{8,0},{1,9},{9,1},{2,10},{10,2},{3,11},{11,3},{4,12},{12,4},... | collective-permute-start | bytes 2654216 | tf_op jit(solution)/shard_map/ppermute | solution.py:50
  148.7 1.3 fusion.9
  150.9 1.3 pad_maximum_fusion
  (61 shorter events, 12.9 us)
Async XLA Ops:
  0.6 7.0 %copy-start.4 = (bf16[2,128,1536]{2,1,0:T(8,128)(2,1)S(1)}, bf16[2,128,1536]{2,1,0:T(8,128)(2,1)}, u32[]{:S(2)}) copy-start(bf16[2,128,1536]{2,1,0:T(8,128)(2,1)} %param.5) | copy-start | bytes 2359300
  0.6 8.6 %copy-start.7 = (f32[1536]{0:T(1024)S(1)}, f32[1536]{0:T(1024)}, u32[]{:S(2)}) copy-start(f32[1536]{0:T(1024)} %param.6) | copy-start | bytes 18436
  1.7 7.4 %collective-permute-start.4 = (bf16[2,16,1536]{2,1,0:T(8,128)(2,1)S(1)}, bf16[2,16,1536]{2,1,0:T(8,128)(2,1)S(1)}, u32[]{:S(2)}, u32[]{:S(2)}) collective-permute-start(bf16[2,16,1536]{2,1,0:T(8,128)(2,1)S(1)} %slice_select_fusion), channel_id=1, source_target_pairs={{8,16},{16,8},{24,32},{32,24},{40,48},{48,40},{56,64},{64,56},{72,... | collective-permute-start | bytes 294920 | tf_op jit(solution)/shard_map/ppermute | solution.py:146
  9.4 1.1 copy-start.6
  9.6 2.0 %collective-permute-start.5 = (bf16[2,144,768]{2,1,0:T(8,128)(2,1)S(1)}, bf16[2,144,768]{2,1,0:T(8,128)(2,1)}, u32[]{:S(2)}, u32[]{:S(2)}) collective-permute-start(bf16[2,144,768]{2,1,0:T(8,128)(2,1)S(1)} %broadcast_select_fusion.7), channel_id=1, source_target_pairs={{0,8},{8,0},{1,9},{9,1},{2,10},{10,2},{3,11},{11,3},{4,12},{12,4},... | collective-permute-start | bytes 1327112 | tf_op jit(solution)/shard_map/ppermute | solution.py:50
  10.5 7.0 %collective-permute-start = (bf16[2,128,1536]{2,1,0:T(8,128)(2,1)S(1)}, bf16[2,128,1536]{2,1,0:T(8,128)(2,1)S(1)}, u32[]{:S(2)}, u32[]{:S(2)}) collective-permute-start(bf16[2,128,1536]{2,1,0:T(8,128)(2,1)S(1)} %copy-done.6), channel_id=1, source_target_pairs={{0,8},{8,0},{1,9},{9,1},{2,10},{10,2},{3,11},{11,3},{4,12},{12,4},... | collective-permute-start | bytes 2359304 | tf_op jit(solution)/shard_map/ppermute | solution.py:50
  12.8 35.4 %collective-permute-start.6 = (bf16[2,288,768]{2,1,0:T(8,128)(2,1)S(1)}, bf16[2,288,768]{2,1,0:T(8,128)(2,1)S(1)}, u32[]{:S(2)}, u32[]{:S(2)}) collective-permute-start(bf16[2,288,768]{2,1,0:T(8,128)(2,1)S(1)} %pad_maximum_fusion.1.refs_4_.refs_0_), channel_id=1, source_target_pairs={{0,2},{1,3},{2,4},{3,5},{4,6},{5,7},{6,0},{7,1},{8,24},{9,25},{10,... | collective-permute-start | bytes 2654216 | tf_op jit(solution)/shard_map/ppermute | solution.py:165
  14.9 33.3 %collective-permute-start.7 = (bf16[2,288,768]{2,1,0:T(8,128)(2,1)S(1)}, bf16[2,288,768]{2,1,0:T(8,128)(2,1)}, u32[]{:S(2)}, u32[]{:S(2)}) collective-permute-start(bf16[2,288,768]{2,1,0:T(8,128)(2,1)S(1)} %pad_maximum_fusion.1.refs_4_.refs_0_), channel_id=1, source_target_pairs={{0,4},{1,5},{2,6},{3,7},{4,0},{5,1},{6,2},{7,3},{8,9},{9,8},{10,11... | collective-permute-start | bytes 2654216 | tf_op jit(solution)/shard_map/ppermute | solution.py:165
  17.5 30.7 %collective-permute-start.8 = (bf16[2,288,768]{2,1,0:T(8,128)(2,1)S(1)}, bf16[2,288,768]{2,1,0:T(8,128)(2,1)}, u32[]{:S(2)}, u32[]{:S(2)}) collective-permute-start(bf16[2,288,768]{2,1,0:T(8,128)(2,1)S(1)} %pad_maximum_fusion.1.refs_4_.refs_0_), channel_id=1, source_target_pairs={{0,6},{1,7},{2,0},{3,1},{4,2},{5,3},{6,4},{7,5},{8,25},{9,24},{10,... | collective-permute-start | bytes 2654216 | tf_op jit(solution)/shard_map/ppermute | solution.py:165
  18.7 21.8 %collective-permute-start.1 = (bf16[2,256,384]{2,1,0:T(8,128)(2,1)S(1)}, bf16[2,256,384]{2,1,0:T(8,128)(2,1)S(1)}, u32[]{:S(2)}, u32[]{:S(2)}) collective-permute-start(bf16[2,256,384]{2,1,0:T(8,128)(2,1)S(1)} %get-tuple-element.29), channel_id=1, source_target_pairs={{0,2},{1,3},{2,4},{3,5},{4,6},{5,7},{6,0},{7,1},{8,24},{9,25},{10,... | collective-permute-start | bytes 1179656 | tf_op jit(solution)/shard_map/ppermute | solution.py:153
  20.1 25.7 %collective-permute-start.2 = (bf16[2,256,384]{2,1,0:T(8,128)(2,1)}, bf16[2,256,384]{2,1,0:T(8,128)(2,1)S(1)}, u32[]{:S(2)}, u32[]{:S(2)}) collective-permute-start(bf16[2,256,384]{2,1,0:T(8,128)(2,1)} %get-tuple-element.30), channel_id=1, source_target_pairs={{0,4},{1,5},{2,6},{3,7},{4,0},{5,1},{6,2},{7,3},{8,9},{9,8},{10,11... | collective-permute-start | bytes 1179656 | tf_op jit(solution)/shard_map/ppermute | solution.py:153
  40.6 7.1 %collective-permute-start.3 = (bf16[2,256,384]{2,1,0:T(8,128)(2,1)}, bf16[2,256,384]{2,1,0:T(8,128)(2,1)S(1)}, u32[]{:S(2)}, u32[]{:S(2)}) collective-permute-start(bf16[2,256,384]{2,1,0:T(8,128)(2,1)} %get-tuple-element.27), channel_id=1, source_target_pairs={{0,6},{1,7},{2,0},{3,1},{4,2},{5,3},{6,4},{7,5},{8,25},{9,24},{10,... | collective-permute-start | bytes 1179656 | tf_op jit(solution)/shard_map/ppermute | solution.py:153
  53.6 13.4 %collective-permute-start.15 = (bf16[576,384]{1,0:T(8,128)(2,1)S(1)}, bf16[576,384]{1,0:T(8,128)(2,1)S(1)}, u32[]{:S(2)}, u32[]{:S(2)}) collective-permute-start(bf16[576,384]{1,0:T(8,128)(2,1)S(1)} %get-tuple-element.24), channel_id=1, source_target_pairs={{0,16},{1,17},{2,18},{3,19},{4,20},{5,21},{6,22},{7,23},{8,10},{9,... | collective-permute-start | bytes 1327112 | tf_op jit(solution)/shard_map/ppermute | solution.py:183
  54.6 13.4 %collective-permute-start.16 = (bf16[576,384]{1,0:T(8,128)(2,1)S(1)}, bf16[576,384]{1,0:T(8,128)(2,1)S(1)}, u32[]{:S(2)}, u32[]{:S(2)}) collective-permute-start(bf16[576,384]{1,0:T(8,128)(2,1)S(1)} %get-tuple-element.26), channel_id=1, source_target_pairs={{0,1},{1,0},{2,3},{3,2},{4,5},{5,4},{6,7},{7,6},{8,12},{9,13},{10,... | collective-permute-start | bytes 1327112 | tf_op jit(solution)/shard_map/ppermute | solution.py:183
  57.5 10.5 %collective-permute-start.17 = (bf16[576,384]{1,0:T(8,128)(2,1)S(1)}, bf16[576,384]{1,0:T(8,128)(2,1)S(1)}, u32[]{:S(2)}, u32[]{:S(2)}) collective-permute-start(bf16[576,384]{1,0:T(8,128)(2,1)S(1)} %get-tuple-element.25), channel_id=1, source_target_pairs={{0,17},{1,16},{2,19},{3,18},{4,21},{5,20},{6,23},{7,22},{8,14},{9,... | collective-permute-start | bytes 1327112 | tf_op jit(solution)/shard_map/ppermute | solution.py:183
  58.2 35.0 %collective-permute-start.10 = (bf16[3,192,768]{2,1,0:T(8,128)(2,1)}, bf16[3,192,768]{2,1,0:T(8,128)(2,1)S(1)}, u32[]{:S(2)}, u32[]{:S(2)}) collective-permute-start(bf16[3,192,768]{2,1,0:T(8,128)(2,1)} %dynamic-slice_bitcast_fusion), channel_id=1, source_target_pairs={{0,17},{1,16},{2,19},{3,18},{4,21},{5,20},{6,23},{7,22},{8,12},{9,... | collective-permute-start | bytes 2654216 | tf_op jit(solution)/shard_map/ppermute | solution.py:209
  58.8 34.5 %collective-permute-start.9 = (bf16[3,192,768]{2,1,0:T(8,128)(2,1)}, bf16[3,192,768]{2,1,0:T(8,128)(2,1)}, u32[]{:S(2)}, u32[]{:S(2)}) collective-permute-start(bf16[3,192,768]{2,1,0:T(8,128)(2,1)} %dynamic-slice_bitcast_fusion), channel_id=1, source_target_pairs={{0,0},{1,1},{2,2},{3,3},{4,4},{5,5},{6,6},{7,7},{8,8},{9,12},{10,2... | collective-permute-start | bytes 2654216 | tf_op jit(solution)/shard_map/ppermute | solution.py:208
  69.0 22.5 %all-to-all-start = ((bf16[8,72,384]{2,1,0:T(8,128)(2,1)}), bf16[8,72,384]{2,1,0:T(8,128)(2,1)}, u32[]{:S(2)}, u32[]{:S(2)}) async-start(bf16[8,72,384]{2,1,0:T(8,128)(2,1)} %bitcast.8), calls=%async_computation | async-start | bytes 884736 | tf_op jit(solution)/shard_map/all_to_all | solution.py:186
  92.6 14.6 %collective-permute-start.18 = (bf16[72,384]{1,0:T(8,128)(2,1)S(1)}, bf16[72,384]{1,0:T(8,128)(2,1)S(1)}, u32[]{:S(2)}, u32[]{:S(2)}) collective-permute-start(bf16[72,384]{1,0:T(8,128)(2,1)S(1)} %reduce_sum.32), channel_id=1, source_target_pairs={{0,0},{1,1},{2,2},{3,3},{4,4},{5,5},{6,6},{7,7},{8,8},{9,12},{10,2... | collective-permute-start | bytes 165896 | tf_op jit(solution)/shard_map/ppermute | solution.py:188
  100.1 0.8 copy-start
  100.9 0.7 copy-start.2
  101.6 11.8 %copy-start.3 = (bf16[2,256,384]{2,1,0:T(8,128)(2,1)S(1)}, bf16[2,256,384]{2,1,0:T(8,128)(2,1)}, u32[]{:S(2)}) copy-start(bf16[2,256,384]{2,1,0:T(8,128)(2,1)} %copy-done.2) | copy-start | bytes 1179652
  101.6 12.6 %copy-start.1 = (bf16[2,256,384]{2,1,0:T(8,128)(2,1)S(1)}, bf16[2,256,384]{2,1,0:T(8,128)(2,1)}, u32[]{:S(2)}) copy-start(bf16[2,256,384]{2,1,0:T(8,128)(2,1)} %copy-done) | copy-start | bytes 1179652
  101.6 13.4 %collective-permute-start.11 = (bf16[2,256,384]{2,1,0:T(8,128)(2,1)}, bf16[2,256,384]{2,1,0:T(8,128)(2,1)S(1)}, u32[]{:S(2)}, u32[]{:S(2)}) collective-permute-start(bf16[2,256,384]{2,1,0:T(8,128)(2,1)} %get-tuple-element.18), channel_id=1, source_target_pairs={{0,6},{1,7},{2,0},{3,1},{4,2},{5,3},{6,4},{7,5},{8,25},{9,24},{10,... | collective-permute-start | bytes 1179656 | tf_op jit(solution)/shard_map/ppermute | solution.py:220
  109.1 34.9 %all-to-all-start.1 = ((bf16[16,72,384]{2,1,0:T(8,128)(2,1)}), bf16[16,72,384]{2,1,0:T(8,128)(2,1)}, u32[]{:S(2)}, u32[]{:S(2)}) async-start(bf16[16,72,384]{2,1,0:T(8,128)(2,1)} %broadcast_in_dim.5), calls=%async_computation.1 | async-start | bytes 1769472 | tf_op jit(solution)/shard_map/all_to_all | solution.py:202
  113.4 8.9 %collective-permute-start.12 = (bf16[2,256,384]{2,1,0:T(8,128)(2,1)S(1)}, bf16[2,256,384]{2,1,0:T(8,128)(2,1)S(1)}, u32[]{:S(2)}, u32[]{:S(2)}) collective-permute-start(bf16[2,256,384]{2,1,0:T(8,128)(2,1)S(1)} %copy-done.3), channel_id=1, source_target_pairs={{0,4},{1,5},{2,6},{3,7},{4,0},{5,1},{6,2},{7,3},{8,9},{9,8},{10,11... | collective-permute-start | bytes 1179656 | tf_op jit(solution)/shard_map/ppermute | solution.py:220
  114.2 13.1 %collective-permute-start.13 = (bf16[2,256,384]{2,1,0:T(8,128)(2,1)S(1)}, bf16[2,256,384]{2,1,0:T(8,128)(2,1)S(1)}, u32[]{:S(2)}, u32[]{:S(2)}) collective-permute-start(bf16[2,256,384]{2,1,0:T(8,128)(2,1)S(1)} %copy-done.1), channel_id=1, source_target_pairs={{0,2},{1,3},{2,4},{3,5},{4,6},{5,7},{6,0},{7,1},{8,24},{9,25},{10,... | collective-permute-start | bytes 1179656 | tf_op jit(solution)/shard_map/ppermute | solution.py:220
  127.5 21.2 %collective-permute-start.14 = (bf16[2,128,1536]{2,1,0:T(8,128)(2,1)S(1)}, bf16[2,128,1536]{2,1,0:T(8,128)(2,1)S(1)}, u32[]{:S(2)}, u32[]{:S(2)}) collective-permute-start(bf16[2,128,1536]{2,1,0:T(8,128)(2,1)S(1)} %broadcast_select_fusion.2), channel_id=1, source_target_pairs={{0,8},{8,0},{1,9},{9,1},{2,10},{10,2},{3,11},{11,3},{4,12},{12,4},... | collective-permute-start | bytes 2359304 | tf_op jit(solution)/shard_map/ppermute | solution.py:50
  144.0 4.8 %copy-start.5 = (bf16[2,128,1536]{2,1,0:T(8,128)(2,1)S(1)}, bf16[2,128,1536]{2,1,0:T(8,128)(2,1)}, u32[]{:S(2)}) copy-start(bf16[2,128,1536]{2,1,0:T(8,128)(2,1)} %param.5) | copy-start | bytes 2359300
  146.0 4.8 %collective-permute-start.19 = (bf16[576,768]{1,0:T(8,128)(2,1)S(1)}, bf16[576,768]{1,0:T(8,128)(2,1)S(1)}, u32[]{:S(2)}, u32[]{:S(2)}) collective-permute-start(bf16[576,768]{1,0:T(8,128)(2,1)S(1)} %bitcast.29), channel_id=1, source_target_pairs={{0,8},{8,0},{1,9},{9,1},{2,10},{10,2},{3,11},{11,3},{4,12},{12,4},... | collective-permute-start | bytes 2654216 | tf_op jit(solution)/shard_map/ppermute | solution.py:50

commit v3 on v2

v3 whole, which is shorter than its diff:
```python
import functools
import math

import jax
import jax.numpy as jnp
from jax import lax
from jax.experimental import pallas as pl
from jax.experimental.pallas import tpu as pltpu
from jax.sharding import Mesh, PartitionSpec as P

D = 16
F32, BF16 = jnp.float32, jnp.bfloat16
SEQ = ("z", "ylo", "core")
PLANE = ("ylo", "yhi")


def around_x(step):
    return [(i, (i + step) % 4) for i in range(4)]


def around_y(step):
    at = [(y % 2) * 2 + y // 2 for y in range(4)]
    return [(at[y], at[(y + step) % 4]) for y in range(4)]


def other_y():
    at = [(y % 2) * 2 + y // 2 for y in range(4)]
    return [(at[y], at[3 - y]) for y in range(4)]


def outward():
    n = lax.axis_size(SEQ)
    pairs = []
    for i in range(n):
        j = i - 1 if i % 2 == 0 else i + 1
        if 0 <= j < n:
            pairs.append((i, j))
    return pairs


def swap(v):
    return lax.ppermute(v, "core", [(0, 1), (1, 0)])


def normalise(values, gain):
    floats = values.astype(F32)
    factor = lax.rsqrt(jnp.mean(floats * floats, axis=-1, keepdims=True) + 1e-06)
    return jax.nn.gelu(floats * factor * gain).astype(BF16)


def in_vmem(count):
    return [pl.BlockSpec(memory_space=pltpu.VMEM)] * count


def call(kernel, shapes, scalars, arrays, flops, scratch=()):
    size = sum(math.prod(a.shape) * a.dtype.itemsize for a in (*arrays, *shapes))
    return pl.pallas_call(
        kernel,
        out_shape=shapes,
        in_specs=[pl.BlockSpec(memory_space=pltpu.SMEM)] * len(scalars) + in_vmem(len(arrays)),
        out_specs=in_vmem(len(shapes)),
        scratch_shapes=list(scratch),
        cost_estimate=pl.CostEstimate(flops=flops, bytes_accessed=size, transcendentals=0),
        compiler_params=pltpu.CompilerParams(vmem_limit_bytes=40 * 2**20),
    )(*scalars, *arrays)


ORDER = (0, 1, 3, 2)


def turn_kernel(x, source, *targets):
    n = source.shape[1] - 2 * D
    for k, target in enumerate(targets):
        for i, d in enumerate(ORDER):
            for b in range(2):
                place = ((x[0] - d) & 3) * 2 + b
                at = (2 * i + b) * n
                target[:, at : at + n] = source[place, (2 - k) * D : (2 - k) * D + n].T


def sequences(blocks):
    return [ref.at[b] for ref in blocks for b in range(ref.shape[0])]


def near_grad_kernel(*refs):
    turned, blocks, out = refs[:3], sequences(refs[3:-1]), refs[-1]
    n, width = blocks[0].shape
    tile = 256
    for k in range(3):
        for at in range(0, width, tile):
            total = jnp.zeros((out.shape[1], tile), F32)
            for b, block in enumerate(blocks):
                total += jnp.dot(
                    turned[k][:, b * n : (b + 1) * n],
                    block[:, at : at + tile],
                    preferred_element_type=F32,
                )
            out[k, :, at : at + tile] = total


def grad_kernel(scale, over, sums, *refs):
    turned, blocks, out = refs[:3], sequences(refs[3:-1]), refs[-1]
    outs = turned[0].shape[0]
    rows = outs // 2
    n, width = blocks[0].shape
    quarter, tile = width // 2, 256
    seen = turned[0].shape[1] - len(blocks) * n
    for k in range(3):
        for at in range(0, width, tile):
            total = sums[k, :, at : at + tile]
            for b, block in enumerate(blocks):
                total += jnp.dot(
                    turned[k][:, seen + b * n : seen + (b + 1) * n],
                    block[:, at : at + tile],
                    preferred_element_type=F32,
                )
            total = (total * scale).astype(BF16)
            for sub in range(2):
                lo, hi = max(at, sub * quarter), min(at + tile, (sub + 1) * quarter)
                if lo >= hi:
                    continue
                for part in range(2):
                    slot = (2 * part + sub - over[0] + 4) & 3
                    out[slot, k * rows : (k + 1) * rows, lo - sub * quarter : hi - sub * quarter] = (
                        total[part * rows : (part + 1) * rows, lo - at : hi - at]
                    )


def mixed_kernel(scale, over, one, two, *refs):
    blocks, (result, weights, total) = sequences(refs[:-3]), refs[-3:]
    rows, n = one.shape[1], blocks[0].shape[0]
    swapped = jnp.where(over[0] < 2, 0, rows)
    for k in range(3):
        weights[k, pl.ds(pl.multiple_of(swapped, rows), rows), :] = one[k]
        weights[k, pl.ds(pl.multiple_of(rows - swapped, rows), rows), :] = two[k]
    for b, block in enumerate(blocks):
        for k in (0, 2, 1):
            part = lax.dot_general(
                block[...], weights[k], (((1,), (1,)), ((), ())), preferred_element_type=F32
            )
            if k == 0:
                total[2 * D :] = part
            elif k == 2:
                total[: 2 * D] = part[: 2 * D]
                total[2 * D : n] += part[2 * D :]
            else:
                total[D : D + n] += part
        result[b] = (total[...] * scale).astype(BF16)


def shards(inputs, gain, param, cotangent, noise):
    seqs, span, width = inputs.shape
    rows = param.shape[0]
    outs = 2 * rows
    half = width // 2
    quarter = half // 2
    piece = 3 * rows // 8
    scale = 1.0 / math.sqrt(3.0 * width)
    total_rows = seqs * span * 256
    eta = math.sqrt(3.0 * width / total_rows)
    core, ylo, yhi, x, z = (lax.axis_index(a) for a in ("core", "ylo", "yhi", "x", "z"))
    y = 2 * yhi + ylo
    first = core == 0
    at_x = x.astype(jnp.int32).reshape(1)
    at_y = y.astype(jnp.int32).reshape(1)

    edge = jnp.where(first, cotangent[:, :D], cotangent[:, span - D :])
    values, edge = lax.optimization_barrier((inputs, edge))
    edge = lax.ppermute(edge, SEQ, outward())
    cot = jnp.where(
        first,
        jnp.concatenate([edge, cotangent], axis=1),
        jnp.concatenate([cotangent, edge], axis=1),
    )
    cot = jnp.transpose(cot.reshape(seqs, span + D, 4, outs), (2, 0, 1, 3))
    cot = lax.all_to_all(cot.reshape(8, span + D, outs), "x", 0, 0, tiled=True)

    own = normalise(values, gain)
    low, high = own[:, :, :half], own[:, :, half:]
    mine = jnp.where(first, low, high)
    mate = swap(jnp.where(first, high, low))
    block = jnp.concatenate([jnp.where(first, mine, mate), jnp.where(first, mate, mine)], axis=1)
    left = lax.ppermute(block, "x", around_x(1))
    right = lax.ppermute(block, "x", around_x(-1))
    far = [lax.ppermute(left[:1], "x", around_x(1)), lax.ppermute(right[1:], "x", around_x(-1))]
    kernel = jnp.transpose(param, (1, 0, 2))
    block, kernel = lax.optimization_barrier((block, kernel))
    share = lax.dynamic_slice_in_dim(kernel, core * half, half, 2)
    other = lax.ppermute(share, PLANE, other_y())

    cot, other, left, right = lax.optimization_barrier((cot, other, left, right))
    mate = swap(cot)
    cot = jnp.concatenate([jnp.where(first, cot, mate), jnp.where(first, mate, cot)], axis=1)
    turned = call(
        turn_kernel, [jax.ShapeDtypeStruct((outs, 8 * 2 * span), BF16)] * 3, (at_x,), (cot,), 0
    )

    work = 2 * 2 * span * outs * half * 3
    (sums,) = call(
        near_grad_kernel,
        [jax.ShapeDtypeStruct((3, outs, half), F32)],
        (),
        (*turned, block, left, right),
        6 * work,
    )
    far, sums = lax.optimization_barrier((far, sums))
    (grad,) = call(
        functools.partial(grad_kernel, scale),
        [jax.ShapeDtypeStruct((4, 3 * rows, quarter), BF16)],
        (at_y,),
        (sums, *turned, *far),
        2 * work,
    )
    grad, far = lax.optimization_barrier((grad, far))
    terms = [grad[0]] + [lax.ppermute(grad[d], PLANE, around_y(d)) for d in range(1, 4)]
    summed = sum(t.astype(F32) for t in terms).astype(BF16)

    terms = lax.all_to_all(summed.reshape(8, piece, quarter), "z", 0, 0, tiled=True)

    mixed = []
    for group in ((block, left, right), far):
        (part,) = call(
            functools.partial(mixed_kernel, scale),
            [jax.ShapeDtypeStruct((sum(g.shape[0] for g in group), 2 * (span + D), outs), BF16)],
            (at_y,),
            (share, other, *group),
            0,
            [pltpu.VMEM((3, outs, half), BF16), pltpu.VMEM((2 * (span + D), outs), F32)],
        )
        mixed.append(part)
    near = jnp.concatenate([m[:, : span + D] for m in mixed], axis=0)
    away = jnp.concatenate([m[:, span + D :] for m in mixed], axis=0)
    mate = swap(jnp.where(first, away, near))
    total = jnp.where(first, near, away).astype(F32) + mate.astype(F32)
    edge = jnp.where(first, total[:, :D], total[:, span:]).astype(BF16)
    edge = lax.ppermute(edge, SEQ, outward())
    terms, edge = lax.optimization_barrier((terms, edge))
    edge = edge.astype(F32)
    total = jnp.where(
        first,
        jnp.concatenate([total[:, D : 2 * D] + edge, total[:, 2 * D :]], axis=1),
        jnp.concatenate([total[:, : span - D], total[:, span - D : span] + edge], axis=1),
    )
    total = total.astype(BF16).reshape(4, seqs, span, outs)
    back = [total[0]] + [
        lax.ppermute(total[i], "x", around_x(-d)) for i, d in enumerate(ORDER) if d > 0
    ]

    summed = jnp.sum(terms.astype(F32), axis=0)
    at = (z * piece, core * half + ylo * quarter)
    own_param = lax.dynamic_slice(kernel.reshape(3 * rows, width), at, (piece, quarter))
    own_noise = lax.dynamic_slice(
        jnp.transpose(noise, (1, 0, 2)).reshape(3 * rows, width), at, (piece, quarter)
    )
    new = (
        own_param.astype(F32) - eta * summed + math.sqrt(2.0 * eta) * own_noise.astype(F32)
    ).astype(BF16)
    copies = jnp.broadcast_to(new[None], (16, piece, quarter))
    sent = lax.all_to_all(copies, ("z", "ylo"), 0, 0, tiled=True)

    back, sent = lax.optimization_barrier((back, sent))
    result = jnp.zeros((seqs, span, width), BF16)
    for rows_back, d in zip(back, ORDER):
        result = lax.dynamic_update_slice_in_dim(result, rows_back, lax.rem(x + d, 4) * outs, 2)
    outputs = (inputs.astype(F32) + result.astype(F32)).astype(BF16)

    sent = jnp.transpose(sent.reshape(8, 2, piece, quarter), (0, 2, 1, 3)).reshape(3 * rows, half)
    mate = swap(sent)
    sent = jnp.concatenate([jnp.where(first, sent, mate), jnp.where(first, mate, sent)], axis=1)
    new_param = jnp.transpose(sent.reshape(3, rows, width), (1, 0, 2))
    return (outputs, new_param)


def solution(mesh):
    fine = Mesh(mesh.devices.reshape(8, 2, 2, 4, 2), ("z", "ylo", "core", "x", "yhi"))
    spread = P(("x", "yhi"), SEQ, None)
    placed = (spread, P(), P(("x", "yhi"), None, None), spread, P(("x", "yhi"), None, None))
    return jax.shard_map(
        shards,
        mesh=fine,
        in_specs=placed,
        out_specs=(spread, P(("x", "yhi"), None, None)),
        check_vma=False,
    )
```

time: 155 us -> 150 us (0.968); the launches traced: 152 us -> 150 us
  starting transfers between devices: 68.6 us -> 37.9 us
  blocking collectives: 0 us -> 28.2 us
  local copies, waits for them, and re-layouts: 8.03 us -> 5.02 us
  waiting for transfers between devices: 49.8 us -> 52.7 us
  Pallas kernels: 12.5 us -> 10.9 us
    all_to_all x0 -> x1, blocking collectives: none -> 28.2 us  [shards(): cot = lax.all_to_all(cot.reshape(8, span + D, outs), 'x', 0, 0, tiled=True)]
    ppermute x15 -> x11, starting transfers between devices: 29.4 us -> 13.4 us  [the longest x3 2.81 us: shards(): lax.ppermute(total[i], 'x', around_x(-d))]
    ppermute x4, starting transfers between devices: 19.3 us -> 8.22 us  [swap(): return lax.ppermute(v, 'core', [(0, 1), (1, 0)])]
    all_to_all x1, waiting for transfers between devices: 0.01 us -> 9.59 us  [shards(): sent = lax.all_to_all(copies, ('z', 'ylo'), 0, 0, tiled=True)]
    ppermute x15 -> x11, waiting for transfers between devices: 36.5 us -> 31 us  [the longest x3 21.1 us: shards(): lax.ppermute(grad[d], PLANE, around_y(d))]
    all_to_all x1, starting transfers between devices: 11.1 us -> 7.41 us  [shards(): lax.all_to_all(summed.reshape(8, piece, quarter), 'z', 0, 0, tiled=True)]
    ppermute x1 -> x2, waiting for transfers between devices: 0.01 us -> 2.97 us  [shards(): edge = lax.ppermute(edge, SEQ, outward())]
    all_to_all x1, waiting for transfers between devices: 11.4 us -> 8.46 us  [shards(): lax.all_to_all(summed.reshape(8, piece, quarter), 'z', 0, 0, tiled=True)]
  transfers between devices with their start and end apart: 22 -> 19, of which waited for: 9 -> 9; matrix products, arithmetic and copies ran while one was open for 10% -> 5% of each run, Pallas kernels for 5% -> 6%
where the time goes in v3:
time: 150 us
  waiting for transfers between devices  52.7 us (35%)
  starting transfers between devices  37.9 us (25%)
  blocking collectives  28.2 us (19%)
  other arithmetic  13.8 us (9%)
  Pallas kernels  10.9 us (7%)
  local copies, waits for them, and re-layouts  5.02 us (3%)
    all_to_all x1, blocking collectives, shards(): cot = lax.all_to_all(cot.reshape(8, span + D, outs), 'x', 0, 0, tiled=True)  28.2 us
    ppermute x3, waiting for transfers between devices, shards(): lax.ppermute(grad[d], PLANE, around_y(d))  21.1 us
    pallas_call x5, Pallas kernels, call(): pl.pallas_call(kernel, out_shape=shapes, in_specs=[pl.BlockSpec(memory_sp...  10.9 us
    ppermute x3, waiting for transfers between devices, shards(): lax.ppermute(total[i], 'x', around_x(-d))  9.81 us
    all_to_all x1, waiting for transfers between devices, shards(): sent = lax.all_to_all(copies, ('z', 'ylo'), 0, 0, tiled=True)  9.59 us
    all_to_all x1, waiting for transfers between devices, shards(): lax.all_to_all(summed.reshape(8, piece, quarter), 'z', 0, 0, tiled=True)  8.46 us
    ppermute x4, starting transfers between devices, swap(): return lax.ppermute(v, 'core', [(0, 1), (1, 0)])  8.22 us
    all_to_all x1, starting transfers between devices, shards(): lax.all_to_all(summed.reshape(8, piece, quarter), 'z', 0, 0, tiled=True)  7.41 us
  transfers between devices with their start and end apart: 19, of which 9 were waited for; matrix products, arithmetic and copies ran while one was open for 5% of the time, Pallas kernels for 6%

profile of v3, /device:TPU:1, one launch (start us, length us, event | category | flops | bytes accessed | tf_op | source)
XLA Modules:
  0.0 149.6 jit_solution(2672718541912462978)
XLA Ops:
  1.7 1.4 fusion
  3.1 1.4 fusion.4
  4.5 3.3 %collective-permute-start = (bf16[2,128,768]{2,1,0:T(8,128)(2,1)S(1)}, bf16[2,128,768]{2,1,0:T(8,128)(2,1)S(1)}, u32[]{:S(2)}, u32[]{:S(2)}) collective-permute-start(bf16[2,128,768]{2,1,0:T(8,128)(2,1)S(1)} %broadcast_select_fusion.7), channel_id=1, source_target_pairs={{0,8},{8,0},{1,9},{9,1},{2,10},{10,2},{3,11},{11,3},{4,12},{12,4},... | collective-permute-start | bytes 1179656 | tf_op jit(solution)/shard_map/ppermute | solution.py:42
  7.9 1.9 %collective-permute-start.1 = (bf16[2,16,1536]{2,1,0:T(8,128)(2,1)S(1)}, bf16[2,16,1536]{2,1,0:T(8,128)(2,1)S(1)}, u32[]{:S(2)}, u32[]{:S(2)}) collective-permute-start(bf16[2,16,1536]{2,1,0:T(8,128)(2,1)S(1)} %slice_select_fusion.1), channel_id=1, source_target_pairs={{8,16},{16,8},{24,32},{32,24},{40,48},{48,40},{56,64},{64,56},{72,... | collective-permute-start | bytes 294920 | tf_op jit(solution)/shard_map/ppermute | solution.py:169
  9.9 1.3 copy-done.9
  11.3 2.8 %collective-permute-start.2 = (bf16[3,192,768]{2,1,0:T(8,128)(2,1)S(1)}, bf16[3,192,768]{2,1,0:T(8,128)(2,1)S(1)}, u32[]{:S(2)}, u32[]{:S(2)}) collective-permute-start(bf16[3,192,768]{2,1,0:T(8,128)(2,1)S(1)} %constant_dynamic-slice_fusion.one), channel_id=1, source_target_pairs={{0,17},{16,1},{1,16},{17,0},{2,19},{18,3},{3,18},{19,2},{4,21},{20... | collective-permute-start | bytes 2654216 | tf_op jit(solution)/shard_map/ppermute | solution.py:189
  14.2 1.3 collective-permute-start.3
  15.5 1.5 collective-permute-start.4
  17.2 28.2 %all_to_all.15 = bf16[8,144,384]{2,1,0:T(8,128)(2,1)} all-to-all(bf16[8,144,384]{2,1,0:T(8,128)(2,1)S(1)} %bitcast.39), channel_id=1, replica_groups=mesh['z'=8,'ylo'=2,'core'=2,'x'=4,'yhi'=2] {'x'}, dimensions={0} | all-to-all | bytes 1769472 | tf_op jit(solution)/shard_map/all_to_all | solution.py:176
  48.0 1.8 %collective-permute-start.6 = (bf16[1,256,768]{2,1,0:T(8,128)(2,1)S(1)}, bf16[1,256,768]{2,1,0:T(8,128)(2,1)S(1)}, u32[]{:S(2)}, u32[]{:S(2)}) collective-permute-start(bf16[1,256,768]{2,1,0:T(8,128)(2,1)S(1)} %slice.104), channel_id=1, source_target_pairs={{0,6},{2,0},{4,2},{6,4},{1,7},{3,1},{5,3},{7,5},{8,14},{10,8},{12,... | collective-permute-start | bytes 1179656 | tf_op jit(solution)/shard_map/ppermute | solution.py:185
  49.8 3.9 %shard_map.68 = bf16[6,288,384]{2,1,0:T(8,128)(2,1)S(1)} custom-call(s32[1]{0:T(128)} %bitcast.over, bf16[3,192,768]{2,1,0:T(8,128)(2,1)S(1)} %constant_dynamic-slice_fusion.one, bf16[3,192,768]{2,1,0:T(8,128)(2,1)S(1)} %copy-done.1, bf16[2,256,768]{2,1,0:T(8,128)(2,1)S(1)} %pad_maximum_fusion.4.refs_0_.refs_3_, ...), custom_call_target="tpu_custom_call" | custom-call | bytes 5455872 | tf_op jit(solution)/shard_map/pallas_call | solution.py:57
  53.9 2.1 %broadcast_select_fusion.4 = (bf16[8,144,384]{2,1,0:T(8,128)(2,1)S(1)}, bf16[8,144,384]{2,1,0:T(8,128)(2,1)S(1)}) fusion(bf16[8,144,384]{2,1,0:T(8,128)(2,1)} %all_to_all.15, bf16[8,144,384]{2,1,0:T(8,128)(2,1)} %collective-permute-done.7, pred[]{:T(512)S(6)} %eq.3), kind=kLoop, calls=%fused_computation.31 | loop fusion | flops 884736 | bytes 3538945 | tf_op jit(solution)/shard_map/jit(_where)/select_n | solution.py:193
  56.2 1.3 shard_map.69
  57.5 2.9 %shard_map.70.sums = f32[3,384,768]{2,1,0:T(8,128)S(1)} custom-call(bf16[384,2048]{1,0:T(8,128)(2,1)S(1)} %get-tuple-element.34.refs_0_, bf16[384,2048]{1,0:T(8,128)(2,1)S(1)} %get-tuple-element.35.refs_1_, bf16[384,2048]{1,0:T(8,128)(2,1)S(1)} %get-tuple-element.36.refs_2_, bf16[2,256,768]{2,1,0:T(8,128)(2,1)S(1)} %pad_maximum_fusion.4.refs_0_.refs_3_, ...), custom_call_target="tpu_custom_call" | custom-call | flops 2717908992 | bytes 10616832 | tf_op jit(solution)/shard_map/pallas_call | solution.py:57
  61.6 1.5 %shard_map.72 = bf16[2,288,384]{2,1,0:T(8,128)(2,1)S(1)} custom-call(s32[1]{0:T(128)} %bitcast.over, bf16[3,192,768]{2,1,0:T(8,128)(2,1)S(1)} %constant_dynamic-slice_fusion.one, bf16[3,192,768]{2,1,0:T(8,128)(2,1)S(1)} %copy-done.1, bf16[1,256,768]{2,1,0:T(8,128)(2,1)S(1)} %collective-permute-done.5.refs_3_.refs_0_, ...), custom_call_target="tpu_custom_call" | custom-call | bytes 2998272 | tf_op jit(solution)/shard_map/pallas_call | solution.py:57
  64.5 1.9 %collective-permute-start.11 = (bf16[576,384]{1,0:T(8,128)(2,1)S(1)}, bf16[576,384]{1,0:T(8,128)(2,1)S(1)}, u32[]{:S(2)}, u32[]{:S(2)}) collective-permute-start(bf16[576,384]{1,0:T(8,128)(2,1)S(1)} %get-tuple-element.57), channel_id=1, source_target_pairs={{0,17},{16,0},{1,16},{17,1},{2,19},{18,2},{3,18},{19,3},{4,21},{20... | collective-permute-start | bytes 1327112 | tf_op jit(solution)/shard_map/ppermute | solution.py:215
  66.4 11.4 %collective-permute-done.10 = bf16[576,384]{1,0:T(8,128)(2,1)S(1)} collective-permute-done((bf16[576,384]{1,0:T(8,128)(2,1)S(1)}, bf16[576,384]{1,0:T(8,128)(2,1)S(1)}, u32[]{:S(2)}, u32[]{:S(2)}) %collective-permute-start.10) | collective-permute-done | bytes 442400 | tf_op jit(solution)/shard_map/ppermute | solution.py:215
  77.8 8.1 %collective-permute-done.11 = bf16[576,384]{1,0:T(8,128)(2,1)S(1)} collective-permute-done((bf16[576,384]{1,0:T(8,128)(2,1)S(1)}, bf16[576,384]{1,0:T(8,128)(2,1)S(1)}, u32[]{:S(2)}, u32[]{:S(2)}) %collective-permute-start.11) | collective-permute-done | bytes 442400 | tf_op jit(solution)/shard_map/ppermute | solution.py:215
  85.8 1.7 %collective-permute-done.9 = bf16[576,384]{1,0:T(8,128)(2,1)S(1)} collective-permute-done((bf16[576,384]{1,0:T(8,128)(2,1)S(1)}, bf16[576,384]{1,0:T(8,128)(2,1)S(1)}, u32[]{:S(2)}, u32[]{:S(2)}) %collective-permute-start.9) | collective-permute-done | bytes 442400 | tf_op jit(solution)/shard_map/ppermute | solution.py:215
  88.5 7.4 %all-to-all-start.1 = ((bf16[8,72,384]{2,1,0:T(8,128)(2,1)}), bf16[8,72,384]{2,1,0:T(8,128)(2,1)}, u32[]{:S(2)}, u32[]{:S(2)}) async-start(bf16[8,72,384]{2,1,0:T(8,128)(2,1)} %bitcast.9), calls=%async_computation.1 | async-start | bytes 884736 | tf_op jit(solution)/shard_map/all_to_all | solution.py:218
  96.0 1.5 convert_add_fusion
  97.5 3.3 %collective-permute-start.12 = (bf16[8,16,384]{2,1,0:T(8,128)(2,1)S(1)}, bf16[8,16,384]{2,1,0:T(8,128)(2,1)S(1)}, u32[]{:S(2)}, u32[]{:S(2)}) collective-permute-start(bf16[8,16,384]{2,1,0:T(8,128)(2,1)S(1)} %fusion.14), channel_id=1, source_target_pairs={{8,16},{16,8},{24,32},{32,24},{40,48},{48,40},{56,64},{64,56},{72,... | collective-permute-start | bytes 294920 | tf_op jit(solution)/shard_map/ppermute | solution.py:236
  100.8 3.0 %collective-permute-done.12 = bf16[8,16,384]{2,1,0:T(8,128)(2,1)S(1)} collective-permute-done((bf16[8,16,384]{2,1,0:T(8,128)(2,1)S(1)}, bf16[8,16,384]{2,1,0:T(8,128)(2,1)S(1)}, u32[]{:S(2)}, u32[]{:S(2)}) %collective-permute-start.12) | collective-permute-done | bytes 98336 | tf_op jit(solution)/shard_map/ppermute | solution.py:236
  103.8 8.5 %all-to-all-done.1 = bf16[8,72,384]{2,1,0:T(8,128)(2,1)} async-done(((bf16[8,72,384]{2,1,0:T(8,128)(2,1)}), bf16[8,72,384]{2,1,0:T(8,128)(2,1)}, u32[]{:S(2)}, u32[]{:S(2)}) %all-to-all-start.1) | async-done | bytes 442400 | tf_op jit(solution)/shard_map/all_to_all | solution.py:218
  115.2 3.6 %all-to-all-start.2 = ((bf16[16,72,384]{2,1,0:T(8,128)(2,1)}), bf16[16,72,384]{2,1,0:T(8,128)(2,1)S(1)}, u32[]{:S(2)}, u32[]{:S(2)}) async-start(bf16[16,72,384]{2,1,0:T(8,128)(2,1)} %broadcast_in_dim.5), calls=%async_computation.2 | async-start | bytes 1769472 | tf_op jit(solution)/shard_map/all_to_all | solution.py:259
  119.3 1.5 %collective-permute-start.13 = (bf16[2,128,384]{2,1,0:T(8,128)(2,1)S(1)}, bf16[2,128,384]{2,1,0:T(8,128)(2,1)S(1)}, u32[]{:S(2)}, u32[]{:S(2)}) collective-permute-start(bf16[2,128,384]{2,1,0:T(8,128)(2,1)S(1)} %get-tuple-element.67), channel_id=1, source_target_pairs={{0,6},{2,0},{4,2},{6,4},{1,7},{3,1},{5,3},{7,5},{8,14},{10,8},{12,... | collective-permute-start | bytes 589832 | tf_op jit(solution)/shard_map/ppermute | solution.py:246
  120.9 1.3 collective-permute-start.15
  122.1 3.2 %collective-permute-done.13 = bf16[2,128,384]{2,1,0:T(8,128)(2,1)S(1)} collective-permute-done((bf16[2,128,384]{2,1,0:T(8,128)(2,1)S(1)}, bf16[2,128,384]{2,1,0:T(8,128)(2,1)S(1)}, u32[]{:S(2)}, u32[]{:S(2)}) %collective-permute-start.13) | collective-permute-done | bytes 196640 | tf_op jit(solution)/shard_map/ppermute | solution.py:246
  125.4 6.6 %collective-permute-done.14 = bf16[2,128,384]{2,1,0:T(8,128)(2,1)S(1)} collective-permute-done((bf16[2,128,384]{2,1,0:T(8,128)(2,1)S(1)}, bf16[2,128,384]{2,1,0:T(8,128)(2,1)S(1)}, u32[]{:S(2)}, u32[]{:S(2)}) %collective-permute-start.14) | collective-permute-done | bytes 196640 | tf_op jit(solution)/shard_map/ppermute | solution.py:246
  132.0 9.6 %all-to-all-done.2 = bf16[16,72,384]{2,1,0:T(8,128)(2,1)S(1)} async-done(((bf16[16,72,384]{2,1,0:T(8,128)(2,1)}), bf16[16,72,384]{2,1,0:T(8,128)(2,1)S(1)}, u32[]{:S(2)}, u32[]{:S(2)}) %all-to-all-start.2) | async-done | bytes 884768 | tf_op jit(solution)/shard_map/all_to_all | solution.py:259
  142.4 3.7 %collective-permute-start.16 = (bf16[576,768]{1,0:T(8,128)(2,1)S(1)}, bf16[576,768]{1,0:T(8,128)(2,1)S(1)}, u32[]{:S(2)}, u32[]{:S(2)}) collective-permute-start(bf16[576,768]{1,0:T(8,128)(2,1)S(1)} %bitcast.40), channel_id=1, source_target_pairs={{0,8},{8,0},{1,9},{9,1},{2,10},{10,2},{3,11},{11,3},{4,12},{12,4},... | collective-permute-start | bytes 2654216 | tf_op jit(solution)/shard_map/ppermute | solution.py:42
  148.3 1.3 pad_maximum_fusion.1
  (71 shorter events, 14.2 us)
Async XLA Ops:
  0.6 2.4 %copy-start.2 = (bf16[2,128,1536]{2,1,0:T(8,128)(2,1)S(1)}, bf16[2,128,1536]{2,1,0:T(8,128)(2,1)}, u32[]{:S(2)}) copy-start(bf16[2,128,1536]{2,1,0:T(8,128)(2,1)} %param.5) | copy-start | bytes 2359300
  4.5 5.3 %collective-permute-start = (bf16[2,128,768]{2,1,0:T(8,128)(2,1)S(1)}, bf16[2,128,768]{2,1,0:T(8,128)(2,1)S(1)}, u32[]{:S(2)}, u32[]{:S(2)}) collective-permute-start(bf16[2,128,768]{2,1,0:T(8,128)(2,1)S(1)} %broadcast_select_fusion.7), channel_id=1, source_target_pairs={{0,8},{8,0},{1,9},{9,1},{2,10},{10,2},{3,11},{11,3},{4,12},{12,4},... | collective-permute-start | bytes 1179656 | tf_op jit(solution)/shard_map/ppermute | solution.py:42
  7.9 6.4 %collective-permute-start.1 = (bf16[2,16,1536]{2,1,0:T(8,128)(2,1)S(1)}, bf16[2,16,1536]{2,1,0:T(8,128)(2,1)S(1)}, u32[]{:S(2)}, u32[]{:S(2)}) collective-permute-start(bf16[2,16,1536]{2,1,0:T(8,128)(2,1)S(1)} %slice_select_fusion.1), channel_id=1, source_target_pairs={{8,16},{16,8},{24,32},{32,24},{40,48},{48,40},{56,64},{64,56},{72,... | collective-permute-start | bytes 294920 | tf_op jit(solution)/shard_map/ppermute | solution.py:169
  9.8 1.5 copy-start.9
  9.9 4.2 %copy-start.8 = (bf16[2,128,1536]{2,1,0:T(8,128)(2,1)S(1)}, bf16[2,128,1536]{2,1,0:T(8,128)(2,1)}, u32[]{:S(2)}) copy-start(bf16[2,128,1536]{2,1,0:T(8,128)(2,1)} %param.8) | copy-start | bytes 2359300
  11.3 34.1 %collective-permute-start.2 = (bf16[3,192,768]{2,1,0:T(8,128)(2,1)S(1)}, bf16[3,192,768]{2,1,0:T(8,128)(2,1)S(1)}, u32[]{:S(2)}, u32[]{:S(2)}) collective-permute-start(bf16[3,192,768]{2,1,0:T(8,128)(2,1)S(1)} %constant_dynamic-slice_fusion.one), channel_id=1, source_target_pairs={{0,17},{16,1},{1,16},{17,0},{2,19},{18,3},{3,18},{19,2},{4,21},{20... | collective-permute-start | bytes 2654216 | tf_op jit(solution)/shard_map/ppermute | solution.py:189
  14.2 31.2 %collective-permute-start.3 = (bf16[2,256,768]{2,1,0:T(8,128)(2,1)S(1)}, bf16[2,256,768]{2,1,0:T(8,128)(2,1)S(1)}, u32[]{:S(2)}, u32[]{:S(2)}) collective-permute-start(bf16[2,256,768]{2,1,0:T(8,128)(2,1)S(1)} %pad_maximum_fusion.4.refs_0_.refs_3_), channel_id=1, source_target_pairs={{0,2},{2,4},{4,6},{6,0},{1,3},{3,5},{5,7},{7,1},{8,10},{10,12},{12... | collective-permute-start | bytes 2359304 | tf_op jit(solution)/shard_map/ppermute | solution.py:183
  15.5 29.9 %collective-permute-start.4 = (bf16[2,256,768]{2,1,0:T(8,128)(2,1)S(1)}, bf16[2,256,768]{2,1,0:T(8,128)(2,1)S(1)}, u32[]{:S(2)}, u32[]{:S(2)}) collective-permute-start(bf16[2,256,768]{2,1,0:T(8,128)(2,1)S(1)} %pad_maximum_fusion.4.refs_0_.refs_3_), channel_id=1, source_target_pairs={{0,6},{2,0},{4,2},{6,4},{1,7},{3,1},{5,3},{7,5},{8,14},{10,8},{12,... | collective-permute-start | bytes 2359304 | tf_op jit(solution)/shard_map/ppermute | solution.py:184
  45.4 0.9 copy-start
  46.3 7.6 %collective-permute-start.7 = (bf16[8,144,384]{2,1,0:T(8,128)(2,1)}, bf16[8,144,384]{2,1,0:T(8,128)(2,1)}, u32[]{:S(2)}, u32[]{:S(2)}) collective-permute-start(bf16[8,144,384]{2,1,0:T(8,128)(2,1)} %all_to_all.15), channel_id=1, source_target_pairs={{0,8},{8,0},{1,9},{9,1},{2,10},{10,2},{3,11},{11,3},{4,12},{12,4},... | collective-permute-start | bytes 2654216 | tf_op jit(solution)/shard_map/ppermute | solution.py:42
  46.7 3.1 %copy-start.1 = (bf16[3,192,768]{2,1,0:T(8,128)(2,1)S(1)}, bf16[3,192,768]{2,1,0:T(8,128)(2,1)}, u32[]{:S(2)}) copy-start(bf16[3,192,768]{2,1,0:T(8,128)(2,1)} %copy-done) | copy-start | bytes 2654212
  46.8 13.7 %collective-permute-start.5 = (bf16[1,256,768]{2,1,0:T(8,128)(2,1)S(1)}, bf16[1,256,768]{2,1,0:T(8,128)(2,1)S(1)}, u32[]{:S(2)}, u32[]{:S(2)}) collective-permute-start(bf16[1,256,768]{2,1,0:T(8,128)(2,1)S(1)} %slice.103), channel_id=1, source_target_pairs={{0,2},{2,4},{4,6},{6,0},{1,3},{3,5},{5,7},{7,1},{8,10},{10,12},{12... | collective-permute-start | bytes 1179656 | tf_op jit(solution)/shard_map/ppermute | solution.py:185
  48.0 12.5 %collective-permute-start.6 = (bf16[1,256,768]{2,1,0:T(8,128)(2,1)S(1)}, bf16[1,256,768]{2,1,0:T(8,128)(2,1)S(1)}, u32[]{:S(2)}, u32[]{:S(2)}) collective-permute-start(bf16[1,256,768]{2,1,0:T(8,128)(2,1)S(1)} %slice.104), channel_id=1, source_target_pairs={{0,6},{2,0},{4,2},{6,4},{1,7},{3,1},{5,3},{7,5},{8,14},{10,8},{12,... | collective-permute-start | bytes 1179656 | tf_op jit(solution)/shard_map/ppermute | solution.py:185
  53.9 9.3 %copy-start.4 = (bf16[6,144,384]{2,1,0:T(8,128)(2,1)}, bf16[6,144,384]{2,1,0:T(8,128)(2,1)S(1)}, u32[]{:S(2)}) copy-start(bf16[6,144,384]{2,1,0:T(8,128)(2,1)S(1)} %get-tuple-element.61) | copy-start | bytes 1990660
  53.9 9.3 %copy-start.6 = (bf16[6,144,384]{2,1,0:T(8,128)(2,1)}, bf16[6,144,384]{2,1,0:T(8,128)(2,1)S(1)}, u32[]{:S(2)}) copy-start(bf16[6,144,384]{2,1,0:T(8,128)(2,1)S(1)} %get-tuple-element.62) | copy-start | bytes 1990660
  63.4 32.5 %collective-permute-start.8 = (bf16[8,144,384]{2,1,0:T(8,128)(2,1)S(1)}, bf16[8,144,384]{2,1,0:T(8,128)(2,1)}, u32[]{:S(2)}, u32[]{:S(2)}) collective-permute-start(bf16[8,144,384]{2,1,0:T(8,128)(2,1)S(1)} %broadcast_select_fusion.2), channel_id=1, source_target_pairs={{0,8},{8,0},{1,9},{9,1},{2,10},{10,2},{3,11},{11,3},{4,12},{12,4},... | collective-permute-start | bytes 2654216 | tf_op jit(solution)/shard_map/ppermute | solution.py:42
  64.3 31.6 %copy-start.5 = (bf16[6,144,384]{2,1,0:T(8,128)(2,1)S(1)}, bf16[6,144,384]{2,1,0:T(8,128)(2,1)}, u32[]{:S(2)}) copy-start(bf16[6,144,384]{2,1,0:T(8,128)(2,1)} %copy-done.4) | copy-start | bytes 1990660
  64.3 31.6 %copy-start.7 = (bf16[6,144,384]{2,1,0:T(8,128)(2,1)S(1)}, bf16[6,144,384]{2,1,0:T(8,128)(2,1)}, u32[]{:S(2)}) copy-start(bf16[6,144,384]{2,1,0:T(8,128)(2,1)} %copy-done.6) | copy-start | bytes 1990660
  64.4 13.4 %collective-permute-start.10 = (bf16[576,384]{1,0:T(8,128)(2,1)S(1)}, bf16[576,384]{1,0:T(8,128)(2,1)S(1)}, u32[]{:S(2)}, u32[]{:S(2)}) collective-permute-start(bf16[576,384]{1,0:T(8,128)(2,1)S(1)} %get-tuple-element.58), channel_id=1, source_target_pairs={{0,1},{16,17},{1,0},{17,16},{2,3},{18,19},{3,2},{19,18},{4,5},{20,... | collective-permute-start | bytes 1327112 | tf_op jit(solution)/shard_map/ppermute | solution.py:215
  64.5 21.4 %collective-permute-start.11 = (bf16[576,384]{1,0:T(8,128)(2,1)S(1)}, bf16[576,384]{1,0:T(8,128)(2,1)S(1)}, u32[]{:S(2)}, u32[]{:S(2)}) collective-permute-start(bf16[576,384]{1,0:T(8,128)(2,1)S(1)} %get-tuple-element.57), channel_id=1, source_target_pairs={{0,17},{16,0},{1,16},{17,1},{2,19},{18,2},{3,18},{19,3},{4,21},{20... | collective-permute-start | bytes 1327112 | tf_op jit(solution)/shard_map/ppermute | solution.py:215
  66.4 21.1 %collective-permute-start.9 = (bf16[576,384]{1,0:T(8,128)(2,1)S(1)}, bf16[576,384]{1,0:T(8,128)(2,1)S(1)}, u32[]{:S(2)}, u32[]{:S(2)}) collective-permute-start(bf16[576,384]{1,0:T(8,128)(2,1)S(1)} %get-tuple-element.56), channel_id=1, source_target_pairs={{0,16},{16,1},{1,17},{17,0},{2,18},{18,3},{3,19},{19,2},{4,20},{20... | collective-permute-start | bytes 1327112 | tf_op jit(solution)/shard_map/ppermute | solution.py:215
  88.5 23.7 %all-to-all-start.1 = ((bf16[8,72,384]{2,1,0:T(8,128)(2,1)}), bf16[8,72,384]{2,1,0:T(8,128)(2,1)}, u32[]{:S(2)}, u32[]{:S(2)}) async-start(bf16[8,72,384]{2,1,0:T(8,128)(2,1)} %bitcast.9), calls=%async_computation.1 | async-start | bytes 884736 | tf_op jit(solution)/shard_map/all_to_all | solution.py:218
  97.5 6.3 %collective-permute-start.12 = (bf16[8,16,384]{2,1,0:T(8,128)(2,1)S(1)}, bf16[8,16,384]{2,1,0:T(8,128)(2,1)S(1)}, u32[]{:S(2)}, u32[]{:S(2)}) collective-permute-start(bf16[8,16,384]{2,1,0:T(8,128)(2,1)S(1)} %fusion.14), channel_id=1, source_target_pairs={{8,16},{16,8},{24,32},{32,24},{40,48},{48,40},{56,64},{64,56},{72,... | collective-permute-start | bytes 294920 | tf_op jit(solution)/shard_map/ppermute | solution.py:236
  115.2 26.3 %all-to-all-start.2 = ((bf16[16,72,384]{2,1,0:T(8,128)(2,1)}), bf16[16,72,384]{2,1,0:T(8,128)(2,1)S(1)}, u32[]{:S(2)}, u32[]{:S(2)}) async-start(bf16[16,72,384]{2,1,0:T(8,128)(2,1)} %broadcast_in_dim.5), calls=%async_computation.2 | async-start | bytes 1769472 | tf_op jit(solution)/shard_map/all_to_all | solution.py:259
  119.3 6.1 %collective-permute-start.13 = (bf16[2,128,384]{2,1,0:T(8,128)(2,1)S(1)}, bf16[2,128,384]{2,1,0:T(8,128)(2,1)S(1)}, u32[]{:S(2)}, u32[]{:S(2)}) collective-permute-start(bf16[2,128,384]{2,1,0:T(8,128)(2,1)S(1)} %get-tuple-element.67), channel_id=1, source_target_pairs={{0,6},{2,0},{4,2},{6,4},{1,7},{3,1},{5,3},{7,5},{8,14},{10,8},{12,... | collective-permute-start | bytes 589832 | tf_op jit(solution)/shard_map/ppermute | solution.py:246
  120.9 11.1 %collective-permute-start.14 = (bf16[2,128,384]{2,1,0:T(8,128)(2,1)S(1)}, bf16[2,128,384]{2,1,0:T(8,128)(2,1)S(1)}, u32[]{:S(2)}, u32[]{:S(2)}) collective-permute-start(bf16[2,128,384]{2,1,0:T(8,128)(2,1)S(1)} %get-tuple-element.66), channel_id=1, source_target_pairs={{0,2},{2,4},{4,6},{6,0},{1,3},{3,5},{5,7},{7,1},{8,10},{10,12},{12... | collective-permute-start | bytes 589832 | tf_op jit(solution)/shard_map/ppermute | solution.py:246
  120.9 11.1 %collective-permute-start.15 = (bf16[2,128,384]{2,1,0:T(8,128)(2,1)S(1)}, bf16[2,128,384]{2,1,0:T(8,128)(2,1)S(1)}, u32[]{:S(2)}, u32[]{:S(2)}) collective-permute-start(bf16[2,128,384]{2,1,0:T(8,128)(2,1)S(1)} %get-tuple-element.65), channel_id=1, source_target_pairs={{0,4},{2,6},{4,0},{6,2},{1,5},{3,7},{5,1},{7,3},{8,12},{10,14},{12... | collective-permute-start | bytes 589832 | tf_op jit(solution)/shard_map/ppermute | solution.py:246
  142.4 4.0 %copy-start.3 = (bf16[2,128,1536]{2,1,0:T(8,128)(2,1)S(1)}, bf16[2,128,1536]{2,1,0:T(8,128)(2,1)}, u32[]{:S(2)}) copy-start(bf16[2,128,1536]{2,1,0:T(8,128)(2,1)} %param.5) | copy-start | bytes 2359300
  142.4 5.8 %collective-permute-start.16 = (bf16[576,768]{1,0:T(8,128)(2,1)S(1)}, bf16[576,768]{1,0:T(8,128)(2,1)S(1)}, u32[]{:S(2)}, u32[]{:S(2)}) collective-permute-start(bf16[576,768]{1,0:T(8,128)(2,1)S(1)} %bitcast.40), channel_id=1, source_target_pairs={{0,8},{8,0},{1,9},{9,1},{2,10},{10,2},{3,11},{11,3},{4,12},{12,4},... | collective-permute-start | bytes 2654216 | tf_op jit(solution)/shard_map/ppermute | solution.py:42

commit v4 on v3

--- a/solution.py
+++ b/solution.py
@@ -126,6 +126,23 @@
                     )
 
 
+def update_kernel(eta, terms, param, noise, out):
+    total = jnp.sum(terms[...].astype(F32), axis=0)
+    new = (
+        param[...].astype(F32) - eta * total + math.sqrt(2.0 * eta) * noise[...].astype(F32)
+    ).astype(BF16)
+    for i in range(out.shape[0]):
+        out[i] = new
+
+
+def place_kernel(core, own, mate, out):
+    rows, columns = own.shape[1:]
+    for source, side in ((own, core[0]), (mate, 1 - core[0])):
+        for i in range(own.shape[0]):
+            start = pl.multiple_of(side * (2 * columns) + (i % 2) * columns, columns)
+            out[(i // 2) * rows : (i // 2 + 1) * rows, pl.ds(start, columns)] = source[i]
+
+
 def mixed_kernel(scale, over, one, two, *refs):
     blocks, (result, weights, total) = sequences(refs[:-3]), refs[-3:]
     rows, n = one.shape[1], blocks[0].shape[0]
@@ -246,16 +263,18 @@
         lax.ppermute(total[i], "x", around_x(-d)) for i, d in enumerate(ORDER) if d > 0
     ]
 
-    summed = jnp.sum(terms.astype(F32), axis=0)
     at = (z * piece, core * half + ylo * quarter)
     own_param = lax.dynamic_slice(kernel.reshape(3 * rows, width), at, (piece, quarter))
     own_noise = lax.dynamic_slice(
         jnp.transpose(noise, (1, 0, 2)).reshape(3 * rows, width), at, (piece, quarter)
     )
-    new = (
-        own_param.astype(F32) - eta * summed + math.sqrt(2.0 * eta) * own_noise.astype(F32)
-    ).astype(BF16)
-    copies = jnp.broadcast_to(new[None], (16, piece, quarter))
+    (copies,) = call(
+        functools.partial(update_kernel, eta),
+        [jax.ShapeDtypeStruct((16, piece, quarter), BF16)],
+        (),
+        (terms, own_param, own_noise),
+        0,
+    )
     sent = lax.all_to_all(copies, ("z", "ylo"), 0, 0, tiled=True)
 
     back, sent = lax.optimization_barrier((back, sent))
@@ -264,9 +283,13 @@
         result = lax.dynamic_update_slice_in_dim(result, rows_back, lax.rem(x + d, 4) * outs, 2)
     outputs = (inputs.astype(F32) + result.astype(F32)).astype(BF16)
 
-    sent = jnp.transpose(sent.reshape(8, 2, piece, quarter), (0, 2, 1, 3)).reshape(3 * rows, half)
-    mate = swap(sent)
-    sent = jnp.concatenate([jnp.where(first, sent, mate), jnp.where(first, mate, sent)], axis=1)
+    (sent,) = call(
+        place_kernel,
+        [jax.ShapeDtypeStruct((3 * rows, width), BF16)],
+        (core.astype(jnp.int32).reshape(1),),
+        (sent, swap(sent)),
+        0,
+    )
     new_param = jnp.transpose(sent.reshape(3, rows, width), (1, 0, 2))
     return (outputs, new_param)
 

time: 150 us -> 147 us (0.980)
  other arithmetic: 13.8 us -> 10.5 us
  Pallas kernels: 10.9 us -> 13.1 us
  waiting for transfers between devices: 52.7 us -> 50.8 us
    pallas_call x5 -> x7, Pallas kernels: 10.9 us -> 13.1 us  [call(): pl.pallas_call(kernel, out_shape=shapes, in_specs=[pl.BlockSpec(memory_sp...]
    ppermute x2, waiting for transfers between devices: 2.97 us -> 1.23 us  [shards(): edge = lax.ppermute(edge, SEQ, outward())]
    dynamic_slice x0 -> x2, local copies, waits for them, and re-layouts: none -> 1.65 us  [the longest x1 0.83 us: shards(): lax.dynamic_slice(jnp.transpose(noise, (1, 0, 2)).reshape(3 * rows, width...]
  transfers between devices with their start and end apart: 19 -> 19, of which waited for: 9 -> 9; matrix products, arithmetic and copies ran while one was open for 5% -> 6% of each run, Pallas kernels for 6% -> 6%
where the time goes in v4:
time: 147 us; the launch traced here: 146 us
  waiting for transfers between devices  50.8 us (35%)
  starting transfers between devices  37.9 us (26%)
  blocking collectives  28.2 us (19%)
  Pallas kernels  13.1 us (9%)
  other arithmetic  10.5 us (7%)
  local copies, waits for them, and re-layouts  4.84 us (3%)
    all_to_all x1, blocking collectives, shards(): cot = lax.all_to_all(cot.reshape(8, span + D, outs), 'x', 0, 0, tiled=True)  28.2 us
    ppermute x3, waiting for transfers between devices, shards(): lax.ppermute(grad[d], PLANE, around_y(d))  21.1 us
    pallas_call x7, Pallas kernels, call(): pl.pallas_call(kernel, out_shape=shapes, in_specs=[pl.BlockSpec(memory_sp...  13.1 us
    ppermute x3, waiting for transfers between devices, shards(): lax.ppermute(total[i], 'x', around_x(-d))  9.81 us
    all_to_all x1, waiting for transfers between devices, shards(): sent = lax.all_to_all(copies, ('z', 'ylo'), 0, 0, tiled=True)  9.53 us
    all_to_all x1, waiting for transfers between devices, shards(): lax.all_to_all(summed.reshape(8, piece, quarter), 'z', 0, 0, tiled=True)  8.3 us
    ppermute x4, starting transfers between devices, swap(): return lax.ppermute(v, 'core', [(0, 1), (1, 0)])  8.14 us
    all_to_all x1, starting transfers between devices, shards(): lax.all_to_all(summed.reshape(8, piece, quarter), 'z', 0, 0, tiled=True)  7.41 us
  transfers between devices with their start and end apart: 19, of which 9 were waited for; matrix products, arithmetic and copies ran while one was open for 6% of the time, Pallas kernels for 6%

profile of v4, /device:TPU:1, one launch (start us, length us, event | category | flops | bytes accessed | tf_op | source)
XLA Modules:
  0.0 146.4 jit_solution(11840277605991071752)
XLA Ops:
  1.7 1.4 fusion
  3.1 1.4 fusion.4
  4.5 3.3 %collective-permute-start = (bf16[2,128,768]{2,1,0:T(8,128)(2,1)S(1)}, bf16[2,128,768]{2,1,0:T(8,128)(2,1)S(1)}, u32[]{:S(2)}, u32[]{:S(2)}) collective-permute-start(bf16[2,128,768]{2,1,0:T(8,128)(2,1)S(1)} %broadcast_select_fusion.5), channel_id=1, source_target_pairs={{0,8},{8,0},{1,9},{9,1},{2,10},{10,2},{3,11},{11,3},{4,12},{12,4},... | collective-permute-start | bytes 1179656 | tf_op jit(solution)/shard_map/ppermute | solution.py:42
  7.9 1.9 %collective-permute-start.1 = (bf16[2,16,1536]{2,1,0:T(8,128)(2,1)S(1)}, bf16[2,16,1536]{2,1,0:T(8,128)(2,1)S(1)}, u32[]{:S(2)}, u32[]{:S(2)}) collective-permute-start(bf16[2,16,1536]{2,1,0:T(8,128)(2,1)S(1)} %slice_select_fusion.1), channel_id=1, source_target_pairs={{8,16},{16,8},{24,32},{32,24},{40,48},{48,40},{56,64},{64,56},{72,... | collective-permute-start | bytes 294920 | tf_op jit(solution)/shard_map/ppermute | solution.py:186
  9.9 1.3 copy-done.8
  11.3 2.8 %collective-permute-start.2 = (bf16[3,192,768]{2,1,0:T(8,128)(2,1)S(1)}, bf16[3,192,768]{2,1,0:T(8,128)(2,1)S(1)}, u32[]{:S(2)}, u32[]{:S(2)}) collective-permute-start(bf16[3,192,768]{2,1,0:T(8,128)(2,1)S(1)} %constant_dynamic-slice_fusion.one), channel_id=1, source_target_pairs={{0,17},{16,1},{1,16},{17,0},{2,19},{18,3},{3,18},{19,2},{4,21},{20... | collective-permute-start | bytes 2654216 | tf_op jit(solution)/shard_map/ppermute | solution.py:206
  14.2 1.3 collective-permute-start.3
  15.5 1.5 %collective-permute-start.4 = (bf16[2,256,768]{2,1,0:T(8,128)(2,1)S(1)}, bf16[2,256,768]{2,1,0:T(8,128)(2,1)S(1)}, u32[]{:S(2)}, u32[]{:S(2)}) collective-permute-start(bf16[2,256,768]{2,1,0:T(8,128)(2,1)S(1)} %pad_maximum_fusion.3.refs_0_.refs_3_), channel_id=1, source_target_pairs={{0,6},{2,0},{4,2},{6,4},{1,7},{3,1},{5,3},{7,5},{8,14},{10,8},{12,... | collective-permute-start | bytes 2359304 | tf_op jit(solution)/shard_map/ppermute | solution.py:201
  17.2 28.2 %all_to_all.15 = bf16[8,144,384]{2,1,0:T(8,128)(2,1)} all-to-all(bf16[8,144,384]{2,1,0:T(8,128)(2,1)S(1)} %bitcast.32), channel_id=1, replica_groups=mesh['z'=8,'ylo'=2,'core'=2,'x'=4,'yhi'=2] {'x'}, dimensions={0} | all-to-all | bytes 1769472 | tf_op jit(solution)/shard_map/all_to_all | solution.py:193
  48.0 1.8 %collective-permute-start.6 = (bf16[1,256,768]{2,1,0:T(8,128)(2,1)S(1)}, bf16[1,256,768]{2,1,0:T(8,128)(2,1)S(1)}, u32[]{:S(2)}, u32[]{:S(2)}) collective-permute-start(bf16[1,256,768]{2,1,0:T(8,128)(2,1)S(1)} %slice.104), channel_id=1, source_target_pairs={{0,6},{2,0},{4,2},{6,4},{1,7},{3,1},{5,3},{7,5},{8,14},{10,8},{12,... | collective-permute-start | bytes 1179656 | tf_op jit(solution)/shard_map/ppermute | solution.py:202
  49.8 3.9 %shard_map.68 = bf16[6,288,384]{2,1,0:T(8,128)(2,1)S(1)} custom-call(s32[1]{0:T(128)} %bitcast.over, bf16[3,192,768]{2,1,0:T(8,128)(2,1)S(1)} %constant_dynamic-slice_fusion.one, bf16[3,192,768]{2,1,0:T(8,128)(2,1)S(1)} %copy-done.1, bf16[2,256,768]{2,1,0:T(8,128)(2,1)S(1)} %pad_maximum_fusion.3.refs_0_.refs_3_, ...), custom_call_target="tpu_custom_call" | custom-call | bytes 5455872 | tf_op jit(solution)/shard_map/pallas_call | solution.py:57
  53.9 2.1 %broadcast_select_fusion.2 = (bf16[8,144,384]{2,1,0:T(8,128)(2,1)S(1)}, bf16[8,144,384]{2,1,0:T(8,128)(2,1)S(1)}) fusion(bf16[8,144,384]{2,1,0:T(8,128)(2,1)} %all_to_all.15, bf16[8,144,384]{2,1,0:T(8,128)(2,1)} %collective-permute-done.7, pred[]{:T(512)S(6)} %eq.3), kind=kLoop, calls=%fused_computation.27 | loop fusion | flops 884736 | bytes 3538945 | tf_op jit(solution)/shard_map/jit(_where)/select_n | solution.py:210
  56.2 1.3 shard_map.69
  57.5 2.9 %shard_map.70.sums = f32[3,384,768]{2,1,0:T(8,128)S(1)} custom-call(bf16[384,2048]{1,0:T(8,128)(2,1)S(1)} %get-tuple-element.34.refs_0_, bf16[384,2048]{1,0:T(8,128)(2,1)S(1)} %get-tuple-element.35.refs_1_, bf16[384,2048]{1,0:T(8,128)(2,1)S(1)} %get-tuple-element.36.refs_2_, bf16[2,256,768]{2,1,0:T(8,128)(2,1)S(1)} %pad_maximum_fusion.3.refs_0_.refs_3_, ...), custom_call_target="tpu_custom_call" | custom-call | flops 2717908992 | bytes 10616832 | tf_op jit(solution)/shard_map/pallas_call | solution.py:57
  61.6 1.5 %shard_map.72 = bf16[2,288,384]{2,1,0:T(8,128)(2,1)S(1)} custom-call(s32[1]{0:T(128)} %bitcast.over, bf16[3,192,768]{2,1,0:T(8,128)(2,1)S(1)} %constant_dynamic-slice_fusion.one, bf16[3,192,768]{2,1,0:T(8,128)(2,1)S(1)} %copy-done.1, bf16[1,256,768]{2,1,0:T(8,128)(2,1)S(1)} %collective-permute-done.5.refs_3_.refs_0_, ...), custom_call_target="tpu_custom_call" | custom-call | bytes 2998272 | tf_op jit(solution)/shard_map/pallas_call | solution.py:57
  64.3 1.9 %collective-permute-start.11 = (bf16[576,384]{1,0:T(8,128)(2,1)S(1)}, bf16[576,384]{1,0:T(8,128)(2,1)S(1)}, u32[]{:S(2)}, u32[]{:S(2)}) collective-permute-start(bf16[576,384]{1,0:T(8,128)(2,1)S(1)} %get-tuple-element.55), channel_id=1, source_target_pairs={{0,17},{16,0},{1,16},{17,1},{2,19},{18,2},{3,18},{19,3},{4,21},{20... | collective-permute-start | bytes 1327112 | tf_op jit(solution)/shard_map/ppermute | solution.py:232
  66.3 11.4 %collective-permute-done.10 = bf16[576,384]{1,0:T(8,128)(2,1)S(1)} collective-permute-done((bf16[576,384]{1,0:T(8,128)(2,1)S(1)}, bf16[576,384]{1,0:T(8,128)(2,1)S(1)}, u32[]{:S(2)}, u32[]{:S(2)}) %collective-permute-start.10) | collective-permute-done | bytes 442400 | tf_op jit(solution)/shard_map/ppermute | solution.py:232
  77.7 8.1 %collective-permute-done.11 = bf16[576,384]{1,0:T(8,128)(2,1)S(1)} collective-permute-done((bf16[576,384]{1,0:T(8,128)(2,1)S(1)}, bf16[576,384]{1,0:T(8,128)(2,1)S(1)}, u32[]{:S(2)}, u32[]{:S(2)}) %collective-permute-start.11) | collective-permute-done | bytes 442400 | tf_op jit(solution)/shard_map/ppermute | solution.py:232
  85.7 1.7 %collective-permute-done.9 = bf16[576,384]{1,0:T(8,128)(2,1)S(1)} collective-permute-done((bf16[576,384]{1,0:T(8,128)(2,1)S(1)}, bf16[576,384]{1,0:T(8,128)(2,1)S(1)}, u32[]{:S(2)}, u32[]{:S(2)}) %collective-permute-start.9) | collective-permute-done | bytes 442400 | tf_op jit(solution)/shard_map/ppermute | solution.py:232
  88.4 7.4 %all-to-all-start.1 = ((bf16[8,72,384]{2,1,0:T(8,128)(2,1)}), bf16[8,72,384]{2,1,0:T(8,128)(2,1)S(1)}, u32[]{:S(2)}, u32[]{:S(2)}) async-start(bf16[8,72,384]{2,1,0:T(8,128)(2,1)} %bitcast.9), calls=%async_computation.1 | async-start | bytes 884736 | tf_op jit(solution)/shard_map/all_to_all | solution.py:235
  95.8 1.6 %convert_add_fusion = f32[8,144,384]{2,1,0:T(8,128)S(1)} fusion(bf16[8,144,384]{2,1,0:T(8,128)(2,1)} %collective-permute-done.8, pred[]{:T(512)S(6)} %eq.3, bf16[2,144,384]{2,1,0:T(8,128)(2,1)S(1)} %get-tuple-element.68, bf16[6,144,384]{2,1,0:T(8,128)(2,1)} %copy-done.6, bf16[2,144,384]{2,1,0:T(8,128)(2,1)S(1)} %get-tuple-element.67, ...), kind=kLoop, calls=%fused_computation.4 | loop fusion | flops 2654208 | bytes 4423681 | tf_op jit(solution)/shard_map/add | solution.py:251
  97.5 3.3 %collective-permute-start.12 = (bf16[8,16,384]{2,1,0:T(8,128)(2,1)S(1)}, bf16[8,16,384]{2,1,0:T(8,128)(2,1)S(1)}, u32[]{:S(2)}, u32[]{:S(2)}) collective-permute-start(bf16[8,16,384]{2,1,0:T(8,128)(2,1)S(1)} %fusion.14), channel_id=1, source_target_pairs={{8,16},{16,8},{24,32},{32,24},{40,48},{48,40},{56,64},{64,56},{72,... | collective-permute-start | bytes 294920 | tf_op jit(solution)/shard_map/ppermute | solution.py:253
  102.5 1.2 collective-permute-done.12
  103.7 8.3 %all-to-all-done.1.terms = bf16[8,72,384]{2,1,0:T(8,128)(2,1)S(1)} async-done(((bf16[8,72,384]{2,1,0:T(8,128)(2,1)}), bf16[8,72,384]{2,1,0:T(8,128)(2,1)S(1)}, u32[]{:S(2)}, u32[]{:S(2)}) %all-to-all-start.1) | async-done | bytes 442400 | tf_op jit(solution)/shard_map/all_to_all | solution.py:235
  113.0 3.6 %all-to-all-start.2 = ((bf16[16,72,384]{2,1,0:T(8,128)(2,1)}), bf16[16,72,384]{2,1,0:T(8,128)(2,1)S(1)}, u32[]{:S(2)}, u32[]{:S(2)}) async-start(bf16[16,72,384]{2,1,0:T(8,128)(2,1)} %shard_map.73), calls=%async_computation.2 | async-start | bytes 1769472 | tf_op jit(solution)/shard_map/all_to_all | solution.py:278
  117.2 1.6 %collective-permute-start.13 = (bf16[2,128,384]{2,1,0:T(8,128)(2,1)S(1)}, bf16[2,128,384]{2,1,0:T(8,128)(2,1)S(1)}, u32[]{:S(2)}, u32[]{:S(2)}) collective-permute-start(bf16[2,128,384]{2,1,0:T(8,128)(2,1)S(1)} %get-tuple-element.65), channel_id=1, source_target_pairs={{0,6},{2,0},{4,2},{6,4},{1,7},{3,1},{5,3},{7,5},{8,14},{10,8},{12,... | collective-permute-start | bytes 589832 | tf_op jit(solution)/shard_map/ppermute | solution.py:263
  118.7 1.3 collective-permute-start.15
  120.0 3.2 %collective-permute-done.13 = bf16[2,128,384]{2,1,0:T(8,128)(2,1)S(1)} collective-permute-done((bf16[2,128,384]{2,1,0:T(8,128)(2,1)S(1)}, bf16[2,128,384]{2,1,0:T(8,128)(2,1)S(1)}, u32[]{:S(2)}, u32[]{:S(2)}) %collective-permute-start.13) | collective-permute-done | bytes 196640 | tf_op jit(solution)/shard_map/ppermute | solution.py:263
  123.2 6.6 %collective-permute-done.14 = bf16[2,128,384]{2,1,0:T(8,128)(2,1)S(1)} collective-permute-done((bf16[2,128,384]{2,1,0:T(8,128)(2,1)S(1)}, bf16[2,128,384]{2,1,0:T(8,128)(2,1)S(1)}, u32[]{:S(2)}, u32[]{:S(2)}) %collective-permute-start.14) | collective-permute-done | bytes 196640 | tf_op jit(solution)/shard_map/ppermute | solution.py:263
  129.8 9.5 %all-to-all-done.2.own = bf16[16,72,384]{2,1,0:T(8,128)(2,1)S(1)} async-done(((bf16[16,72,384]{2,1,0:T(8,128)(2,1)}), bf16[16,72,384]{2,1,0:T(8,128)(2,1)S(1)}, u32[]{:S(2)}, u32[]{:S(2)}) %all-to-all-start.2) | async-done | bytes 884768 | tf_op jit(solution)/shard_map/all_to_all | solution.py:278
  139.4 3.6 %collective-permute-start.16 = (bf16[16,72,384]{2,1,0:T(8,128)(2,1)S(1)}, bf16[16,72,384]{2,1,0:T(8,128)(2,1)S(1)}, u32[]{:S(2)}, u32[]{:S(2)}) collective-permute-start(bf16[16,72,384]{2,1,0:T(8,128)(2,1)S(1)} %all-to-all-done.2.own), channel_id=1, source_target_pairs={{0,8},{8,0},{1,9},{9,1},{2,10},{10,2},{3,11},{11,3},{4,12},{12,4},... | collective-permute-start | bytes 2654216 | tf_op jit(solution)/shard_map/ppermute | solution.py:42
  145.0 1.4 shard_map.74
  (66 shorter events, 12.9 us)
Async XLA Ops:
  0.6 2.4 %copy-start.2 = (bf16[2,128,1536]{2,1,0:T(8,128)(2,1)S(1)}, bf16[2,128,1536]{2,1,0:T(8,128)(2,1)}, u32[]{:S(2)}) copy-start(bf16[2,128,1536]{2,1,0:T(8,128)(2,1)} %param.5) | copy-start | bytes 2359300
  4.5 5.3 %collective-permute-start = (bf16[2,128,768]{2,1,0:T(8,128)(2,1)S(1)}, bf16[2,128,768]{2,1,0:T(8,128)(2,1)S(1)}, u32[]{:S(2)}, u32[]{:S(2)}) collective-permute-start(bf16[2,128,768]{2,1,0:T(8,128)(2,1)S(1)} %broadcast_select_fusion.5), channel_id=1, source_target_pairs={{0,8},{8,0},{1,9},{9,1},{2,10},{10,2},{3,11},{11,3},{4,12},{12,4},... | collective-permute-start | bytes 1179656 | tf_op jit(solution)/shard_map/ppermute | solution.py:42
  7.9 6.4 %collective-permute-start.1 = (bf16[2,16,1536]{2,1,0:T(8,128)(2,1)S(1)}, bf16[2,16,1536]{2,1,0:T(8,128)(2,1)S(1)}, u32[]{:S(2)}, u32[]{:S(2)}) collective-permute-start(bf16[2,16,1536]{2,1,0:T(8,128)(2,1)S(1)} %slice_select_fusion.1), channel_id=1, source_target_pairs={{8,16},{16,8},{24,32},{32,24},{40,48},{48,40},{56,64},{64,56},{72,... | collective-permute-start | bytes 294920 | tf_op jit(solution)/shard_map/ppermute | solution.py:186
  9.8 1.5 %copy-start.8 = (bf16[192,3,1536]{2,0,1:T(8,128)(2,1)S(1)}, bf16[192,3,1536]{2,0,1:T(8,128)(2,1)}, u32[]{:S(2)}) copy-start(bf16[192,3,1536]{2,0,1:T(8,128)(2,1)} %param.7) | copy-start | bytes 5308420
  9.9 4.2 %copy-start.7 = (bf16[2,128,1536]{2,1,0:T(8,128)(2,1)S(1)}, bf16[2,128,1536]{2,1,0:T(8,128)(2,1)}, u32[]{:S(2)}) copy-start(bf16[2,128,1536]{2,1,0:T(8,128)(2,1)} %param.8) | copy-start | bytes 2359300
  11.3 34.1 %collective-permute-start.2 = (bf16[3,192,768]{2,1,0:T(8,128)(2,1)S(1)}, bf16[3,192,768]{2,1,0:T(8,128)(2,1)S(1)}, u32[]{:S(2)}, u32[]{:S(2)}) collective-permute-start(bf16[3,192,768]{2,1,0:T(8,128)(2,1)S(1)} %constant_dynamic-slice_fusion.one), channel_id=1, source_target_pairs={{0,17},{16,1},{1,16},{17,0},{2,19},{18,3},{3,18},{19,2},{4,21},{20... | collective-permute-start | bytes 2654216 | tf_op jit(solution)/shard_map/ppermute | solution.py:206
  14.2 31.2 %collective-permute-start.3 = (bf16[2,256,768]{2,1,0:T(8,128)(2,1)S(1)}, bf16[2,256,768]{2,1,0:T(8,128)(2,1)S(1)}, u32[]{:S(2)}, u32[]{:S(2)}) collective-permute-start(bf16[2,256,768]{2,1,0:T(8,128)(2,1)S(1)} %pad_maximum_fusion.3.refs_0_.refs_3_), channel_id=1, source_target_pairs={{0,2},{2,4},{4,6},{6,0},{1,3},{3,5},{5,7},{7,1},{8,10},{10,12},{12... | collective-permute-start | bytes 2359304 | tf_op jit(solution)/shard_map/ppermute | solution.py:200
  15.5 29.9 %collective-permute-start.4 = (bf16[2,256,768]{2,1,0:T(8,128)(2,1)S(1)}, bf16[2,256,768]{2,1,0:T(8,128)(2,1)S(1)}, u32[]{:S(2)}, u32[]{:S(2)}) collective-permute-start(bf16[2,256,768]{2,1,0:T(8,128)(2,1)S(1)} %pad_maximum_fusion.3.refs_0_.refs_3_), channel_id=1, source_target_pairs={{0,6},{2,0},{4,2},{6,4},{1,7},{3,1},{5,3},{7,5},{8,14},{10,8},{12,... | collective-permute-start | bytes 2359304 | tf_op jit(solution)/shard_map/ppermute | solution.py:201
  45.4 0.9 copy-start
  46.3 7.6 %collective-permute-start.7 = (bf16[8,144,384]{2,1,0:T(8,128)(2,1)}, bf16[8,144,384]{2,1,0:T(8,128)(2,1)}, u32[]{:S(2)}, u32[]{:S(2)}) collective-permute-start(bf16[8,144,384]{2,1,0:T(8,128)(2,1)} %all_to_all.15), channel_id=1, source_target_pairs={{0,8},{8,0},{1,9},{9,1},{2,10},{10,2},{3,11},{11,3},{4,12},{12,4},... | collective-permute-start | bytes 2654216 | tf_op jit(solution)/shard_map/ppermute | solution.py:42
  46.7 3.1 %copy-start.1 = (bf16[3,192,768]{2,1,0:T(8,128)(2,1)S(1)}, bf16[3,192,768]{2,1,0:T(8,128)(2,1)}, u32[]{:S(2)}) copy-start(bf16[3,192,768]{2,1,0:T(8,128)(2,1)} %copy-done) | copy-start | bytes 2654212
  46.8 13.7 %collective-permute-start.5 = (bf16[1,256,768]{2,1,0:T(8,128)(2,1)S(1)}, bf16[1,256,768]{2,1,0:T(8,128)(2,1)S(1)}, u32[]{:S(2)}, u32[]{:S(2)}) collective-permute-start(bf16[1,256,768]{2,1,0:T(8,128)(2,1)S(1)} %slice.103), channel_id=1, source_target_pairs={{0,2},{2,4},{4,6},{6,0},{1,3},{3,5},{5,7},{7,1},{8,10},{10,12},{12... | collective-permute-start | bytes 1179656 | tf_op jit(solution)/shard_map/ppermute | solution.py:202
  48.0 12.5 %collective-permute-start.6 = (bf16[1,256,768]{2,1,0:T(8,128)(2,1)S(1)}, bf16[1,256,768]{2,1,0:T(8,128)(2,1)S(1)}, u32[]{:S(2)}, u32[]{:S(2)}) collective-permute-start(bf16[1,256,768]{2,1,0:T(8,128)(2,1)S(1)} %slice.104), channel_id=1, source_target_pairs={{0,6},{2,0},{4,2},{6,4},{1,7},{3,1},{5,3},{7,5},{8,14},{10,8},{12,... | collective-permute-start | bytes 1179656 | tf_op jit(solution)/shard_map/ppermute | solution.py:202
  53.9 9.2 %copy-start.4 = (bf16[6,144,384]{2,1,0:T(8,128)(2,1)}, bf16[6,144,384]{2,1,0:T(8,128)(2,1)S(1)}, u32[]{:S(2)}) copy-start(bf16[6,144,384]{2,1,0:T(8,128)(2,1)S(1)} %get-tuple-element.59) | copy-start | bytes 1990660
  53.9 9.2 %copy-start.6 = (bf16[6,144,384]{2,1,0:T(8,128)(2,1)}, bf16[6,144,384]{2,1,0:T(8,128)(2,1)S(1)}, u32[]{:S(2)}) copy-start(bf16[6,144,384]{2,1,0:T(8,128)(2,1)S(1)} %get-tuple-element.60) | copy-start | bytes 1990660
  63.3 32.5 %collective-permute-start.8 = (bf16[8,144,384]{2,1,0:T(8,128)(2,1)S(1)}, bf16[8,144,384]{2,1,0:T(8,128)(2,1)}, u32[]{:S(2)}, u32[]{:S(2)}) collective-permute-start(bf16[8,144,384]{2,1,0:T(8,128)(2,1)S(1)} %broadcast_select_fusion), channel_id=1, source_target_pairs={{0,8},{8,0},{1,9},{9,1},{2,10},{10,2},{3,11},{11,3},{4,12},{12,4},... | collective-permute-start | bytes 2654216 | tf_op jit(solution)/shard_map/ppermute | solution.py:42
  64.2 31.6 %copy-start.5 = (bf16[6,144,384]{2,1,0:T(8,128)(2,1)S(1)}, bf16[6,144,384]{2,1,0:T(8,128)(2,1)}, u32[]{:S(2)}) copy-start(bf16[6,144,384]{2,1,0:T(8,128)(2,1)} %copy-done.4) | copy-start | bytes 1990660
  64.2 13.4 %collective-permute-start.10 = (bf16[576,384]{1,0:T(8,128)(2,1)S(1)}, bf16[576,384]{1,0:T(8,128)(2,1)S(1)}, u32[]{:S(2)}, u32[]{:S(2)}) collective-permute-start(bf16[576,384]{1,0:T(8,128)(2,1)S(1)} %get-tuple-element.56), channel_id=1, source_target_pairs={{0,1},{16,17},{1,0},{17,16},{2,3},{18,19},{3,2},{19,18},{4,5},{20,... | collective-permute-start | bytes 1327112 | tf_op jit(solution)/shard_map/ppermute | solution.py:232
  64.3 21.4 %collective-permute-start.11 = (bf16[576,384]{1,0:T(8,128)(2,1)S(1)}, bf16[576,384]{1,0:T(8,128)(2,1)S(1)}, u32[]{:S(2)}, u32[]{:S(2)}) collective-permute-start(bf16[576,384]{1,0:T(8,128)(2,1)S(1)} %get-tuple-element.55), channel_id=1, source_target_pairs={{0,17},{16,0},{1,16},{17,1},{2,19},{18,2},{3,18},{19,3},{4,21},{20... | collective-permute-start | bytes 1327112 | tf_op jit(solution)/shard_map/ppermute | solution.py:232
  66.3 21.1 %collective-permute-start.9 = (bf16[576,384]{1,0:T(8,128)(2,1)S(1)}, bf16[576,384]{1,0:T(8,128)(2,1)S(1)}, u32[]{:S(2)}, u32[]{:S(2)}) collective-permute-start(bf16[576,384]{1,0:T(8,128)(2,1)S(1)} %get-tuple-element.54), channel_id=1, source_target_pairs={{0,16},{16,1},{1,17},{17,0},{2,18},{18,3},{3,19},{19,2},{4,20},{20... | collective-permute-start | bytes 1327112 | tf_op jit(solution)/shard_map/ppermute | solution.py:232
  88.4 23.6 %all-to-all-start.1 = ((bf16[8,72,384]{2,1,0:T(8,128)(2,1)}), bf16[8,72,384]{2,1,0:T(8,128)(2,1)S(1)}, u32[]{:S(2)}, u32[]{:S(2)}) async-start(bf16[8,72,384]{2,1,0:T(8,128)(2,1)} %bitcast.9), calls=%async_computation.1 | async-start | bytes 884736 | tf_op jit(solution)/shard_map/all_to_all | solution.py:235
  97.5 6.2 %collective-permute-start.12 = (bf16[8,16,384]{2,1,0:T(8,128)(2,1)S(1)}, bf16[8,16,384]{2,1,0:T(8,128)(2,1)S(1)}, u32[]{:S(2)}, u32[]{:S(2)}) collective-permute-start(bf16[8,16,384]{2,1,0:T(8,128)(2,1)S(1)} %fusion.14), channel_id=1, source_target_pairs={{8,16},{16,8},{24,32},{32,24},{40,48},{48,40},{56,64},{64,56},{72,... | collective-permute-start | bytes 294920 | tf_op jit(solution)/shard_map/ppermute | solution.py:253
  113.0 26.3 %all-to-all-start.2 = ((bf16[16,72,384]{2,1,0:T(8,128)(2,1)}), bf16[16,72,384]{2,1,0:T(8,128)(2,1)S(1)}, u32[]{:S(2)}, u32[]{:S(2)}) async-start(bf16[16,72,384]{2,1,0:T(8,128)(2,1)} %shard_map.73), calls=%async_computation.2 | async-start | bytes 1769472 | tf_op jit(solution)/shard_map/all_to_all | solution.py:278
  117.1 26.1 %copy-start.3 = (bf16[2,128,1536]{2,1,0:T(8,128)(2,1)S(1)}, bf16[2,128,1536]{2,1,0:T(8,128)(2,1)}, u32[]{:S(2)}) copy-start(bf16[2,128,1536]{2,1,0:T(8,128)(2,1)} %param.5) | copy-start | bytes 2359300
  117.2 6.1 %collective-permute-start.13 = (bf16[2,128,384]{2,1,0:T(8,128)(2,1)S(1)}, bf16[2,128,384]{2,1,0:T(8,128)(2,1)S(1)}, u32[]{:S(2)}, u32[]{:S(2)}) collective-permute-start(bf16[2,128,384]{2,1,0:T(8,128)(2,1)S(1)} %get-tuple-element.65), channel_id=1, source_target_pairs={{0,6},{2,0},{4,2},{6,4},{1,7},{3,1},{5,3},{7,5},{8,14},{10,8},{12,... | collective-permute-start | bytes 589832 | tf_op jit(solution)/shard_map/ppermute | solution.py:263
  118.7 11.1 %collective-permute-start.14 = (bf16[2,128,384]{2,1,0:T(8,128)(2,1)S(1)}, bf16[2,128,384]{2,1,0:T(8,128)(2,1)S(1)}, u32[]{:S(2)}, u32[]{:S(2)}) collective-permute-start(bf16[2,128,384]{2,1,0:T(8,128)(2,1)S(1)} %get-tuple-element.64), channel_id=1, source_target_pairs={{0,2},{2,4},{4,6},{6,0},{1,3},{3,5},{5,7},{7,1},{8,10},{10,12},{12... | collective-permute-start | bytes 589832 | tf_op jit(solution)/shard_map/ppermute | solution.py:263
  118.7 11.1 %collective-permute-start.15 = (bf16[2,128,384]{2,1,0:T(8,128)(2,1)S(1)}, bf16[2,128,384]{2,1,0:T(8,128)(2,1)S(1)}, u32[]{:S(2)}, u32[]{:S(2)}) collective-permute-start(bf16[2,128,384]{2,1,0:T(8,128)(2,1)S(1)} %get-tuple-element.63), channel_id=1, source_target_pairs={{0,4},{2,6},{4,0},{6,2},{1,5},{3,7},{5,1},{7,3},{8,12},{10,14},{12... | collective-permute-start | bytes 589832 | tf_op jit(solution)/shard_map/ppermute | solution.py:263
  139.4 5.7 %collective-permute-start.16 = (bf16[16,72,384]{2,1,0:T(8,128)(2,1)S(1)}, bf16[16,72,384]{2,1,0:T(8,128)(2,1)S(1)}, u32[]{:S(2)}, u32[]{:S(2)}) collective-permute-start(bf16[16,72,384]{2,1,0:T(8,128)(2,1)S(1)} %all-to-all-done.2.own), channel_id=1, source_target_pairs={{0,8},{8,0},{1,9},{9,1},{2,10},{10,2},{3,11},{11,3},{4,12},{12,4},... | collective-permute-start | bytes 2654216 | tf_op jit(solution)/shard_map/ppermute | solution.py:42

commit v5 on v4

--- a/solution.py
+++ b/solution.py
@@ -68,14 +68,19 @@
 ORDER = (0, 1, 3, 2)
 
 
-def turn_kernel(x, source, *targets):
-    n = source.shape[1] - 2 * D
-    for k, target in enumerate(targets):
-        for i, d in enumerate(ORDER):
-            for b in range(2):
-                place = ((x[0] - d) & 3) * 2 + b
-                at = (2 * i + b) * n
-                target[:, at : at + n] = source[place, (2 - k) * D : (2 - k) * D + n].T
+def turn_kernel(x, core, own, mate, *targets):
+    n = 2 * own.shape[1] - 2 * D
+    low = core[0] == 0
+    for i, d in enumerate(ORDER):
+        for b in range(2):
+            place = ((x[0] - d) & 3) * 2 + b
+            mine, other = own[place], mate[place]
+            rows = jnp.concatenate(
+                [jnp.where(low, mine, other), jnp.where(low, other, mine)], axis=0
+            )
+            at = (2 * i + b) * n
+            for k, target in enumerate(targets):
+                target[:, at : at + n] = rows[(2 - k) * D : (2 - k) * D + n].T
 
 
 def sequences(blocks):
@@ -143,13 +148,19 @@
             out[(i // 2) * rows : (i // 2 + 1) * rows, pl.ds(start, columns)] = source[i]
 
 
-def mixed_kernel(scale, over, one, two, *refs):
-    blocks, (result, weights, total) = sequences(refs[:-3]), refs[-3:]
-    rows, n = one.shape[1], blocks[0].shape[0]
+def near_mixed_kernel(scale, over, one, two, *refs):
+    weights = refs[-2]
+    rows = one.shape[1]
     swapped = jnp.where(over[0] < 2, 0, rows)
     for k in range(3):
         weights[k, pl.ds(pl.multiple_of(swapped, rows), rows), :] = one[k]
         weights[k, pl.ds(pl.multiple_of(rows - swapped, rows), rows), :] = two[k]
+    mixed_kernel(scale, weights, *refs[:-2], refs[-1])
+
+
+def mixed_kernel(scale, weights, *refs):
+    blocks, (result, total) = sequences(refs[:-2]), refs[-2:]
+    n = blocks[0].shape[0]
     for b, block in enumerate(blocks):
         for k in (0, 2, 1):
             part = lax.dot_general(
@@ -206,10 +217,9 @@
     other = lax.ppermute(share, PLANE, other_y())
 
     cot, other, left, right = lax.optimization_barrier((cot, other, left, right))
-    mate = swap(cot)
-    cot = jnp.concatenate([jnp.where(first, cot, mate), jnp.where(first, mate, cot)], axis=1)
+    at_core = core.astype(jnp.int32).reshape(1)
     turned = call(
-        turn_kernel, [jax.ShapeDtypeStruct((outs, 8 * 2 * span), BF16)] * 3, (at_x,), (cot,), 0
+        turn_kernel, [jax.ShapeDtypeStruct((outs, 8 * 2 * span), BF16)] * 3, (at_x, at_core), (cot, swap(cot)), 0
     )
 
     work = 2 * 2 * span * outs * half * 3
@@ -234,17 +244,27 @@
 
     terms = lax.all_to_all(summed.reshape(8, piece, quarter), "z", 0, 0, tiled=True)
 
-    mixed = []
-    for group in ((block, left, right), far):
-        (part,) = call(
-            functools.partial(mixed_kernel, scale),
-            [jax.ShapeDtypeStruct((sum(g.shape[0] for g in group), 2 * (span + D), outs), BF16)],
-            (at_y,),
-            (share, other, *group),
-            0,
-            [pltpu.VMEM((3, outs, half), BF16), pltpu.VMEM((2 * (span + D), outs), F32)],
-        )
-        mixed.append(part)
+    sums_at = pltpu.VMEM((2 * (span + D), outs), F32)
+    near_mixed, weights = call(
+        functools.partial(near_mixed_kernel, scale),
+        [
+            jax.ShapeDtypeStruct((6, 2 * (span + D), outs), BF16),
+            jax.ShapeDtypeStruct((3, outs, half), BF16),
+        ],
+        (at_y,),
+        (share, other, block, left, right),
+        0,
+        [sums_at],
+    )
+    (far_mixed,) = call(
+        functools.partial(mixed_kernel, scale),
+        [jax.ShapeDtypeStruct((2, 2 * (span + D), outs), BF16)],
+        (),
+        (weights, *far),
+        0,
+        [sums_at],
+    )
+    mixed = [near_mixed, far_mixed]
     near = jnp.concatenate([m[:, : span + D] for m in mixed], axis=0)
     away = jnp.concatenate([m[:, span + D :] for m in mixed], axis=0)
     mate = swap(jnp.where(first, away, near))
@@ -286,7 +306,7 @@
     (sent,) = call(
         place_kernel,
         [jax.ShapeDtypeStruct((3 * rows, width), BF16)],
-        (core.astype(jnp.int32).reshape(1),),
+        (at_core,),
         (sent, swap(sent)),
         0,
     )

time: 147 us -> 148 us (level)
  other arithmetic: 10.5 us -> 8.26 us
  Pallas kernels: 13.1 us -> 14.7 us
    select_n x1 -> x0, other arithmetic: 2.07 us -> none  [shards(): jnp.where(first, cot, mate)]
    pallas_call x7, Pallas kernels: 13.1 us -> 14.7 us  [call(): pl.pallas_call(kernel, out_shape=shapes, in_specs=[pl.BlockSpec(memory_sp...]
    unnamed x18 -> x22, local copies, waits for them, and re-layouts: 2.26 us -> 3.45 us
  transfers between devices with their start and end apart: 19 -> 19, of which waited for: 9 -> 9; matrix products, arithmetic and copies ran while one was open for 6% -> 5% of each run, Pallas kernels for 6% -> 7%
where the time goes in v5:
time: 148 us; the launch traced here: 147 us
  waiting for transfers between devices  51.3 us (35%)
  starting transfers between devices  37.5 us (25%)
  blocking collectives  28.1 us (19%)
  Pallas kernels  14.7 us (10%)
  other arithmetic  8.26 us (6%)
  local copies, waits for them, and re-layouts  6.03 us (4%)
    all_to_all x1, blocking collectives, shards(): cot = lax.all_to_all(cot.reshape(8, span + D, outs), 'x', 0, 0, tiled=True)  28.1 us
    ppermute x3, waiting for transfers between devices, shards(): lax.ppermute(grad[d], PLANE, around_y(d))  21.2 us
    pallas_call x7, Pallas kernels, call(): pl.pallas_call(kernel, out_shape=shapes, in_specs=[pl.BlockSpec(memory_sp...  14.7 us
    all_to_all x1, waiting for transfers between devices, shards(): sent = lax.all_to_all(copies, ('z', 'ylo'), 0, 0, tiled=True)  10.1 us
    ppermute x3, waiting for transfers between devices, shards(): lax.ppermute(total[i], 'x', around_x(-d))  9.81 us
    all_to_all x1, waiting for transfers between devices, shards(): lax.all_to_all(summed.reshape(8, piece, quarter), 'z', 0, 0, tiled=True)  8.3 us
    ppermute x4, starting transfers between devices, swap(): return lax.ppermute(v, 'core', [(0, 1), (1, 0)])  8.13 us
    all_to_all x1, starting transfers between devices, shards(): lax.all_to_all(summed.reshape(8, piece, quarter), 'z', 0, 0, tiled=True)  7.4 us
  transfers between devices with their start and end apart: 19, of which 9 were waited for; matrix products, arithmetic and copies ran while one was open for 5% of the time, Pallas kernels for 7%

profile of v5, /device:TPU:1, one launch (start us, length us, event | category | flops | bytes accessed | tf_op | source)
XLA Modules:
  0.0 147.0 jit_solution(975593332992723110)
XLA Ops:
  1.7 1.4 fusion
  3.1 1.4 fusion.4
  4.5 3.3 %collective-permute-start = (bf16[2,128,768]{2,1,0:T(8,128)(2,1)S(1)}, bf16[2,128,768]{2,1,0:T(8,128)(2,1)S(1)}, u32[]{:S(2)}, u32[]{:S(2)}) collective-permute-start(bf16[2,128,768]{2,1,0:T(8,128)(2,1)S(1)} %broadcast_select_fusion.3), channel_id=1, source_target_pairs={{0,8},{8,0},{1,9},{9,1},{2,10},{10,2},{3,11},{11,3},{4,12},{12,4},... | collective-permute-start | bytes 1179656 | tf_op jit(solution)/shard_map/ppermute | solution.py:42
  7.9 1.9 %collective-permute-start.1 = (bf16[2,16,1536]{2,1,0:T(8,128)(2,1)S(1)}, bf16[2,16,1536]{2,1,0:T(8,128)(2,1)S(1)}, u32[]{:S(2)}, u32[]{:S(2)}) collective-permute-start(bf16[2,16,1536]{2,1,0:T(8,128)(2,1)S(1)} %slice_select_fusion.1), channel_id=1, source_target_pairs={{8,16},{16,8},{24,32},{32,24},{40,48},{48,40},{56,64},{64,56},{72,... | collective-permute-start | bytes 294920 | tf_op jit(solution)/shard_map/ppermute | solution.py:197
  9.9 1.3 copy-done.10
  11.3 2.8 %collective-permute-start.2 = (bf16[3,192,768]{2,1,0:T(8,128)(2,1)S(1)}, bf16[3,192,768]{2,1,0:T(8,128)(2,1)S(1)}, u32[]{:S(2)}, u32[]{:S(2)}) collective-permute-start(bf16[3,192,768]{2,1,0:T(8,128)(2,1)S(1)} %constant_dynamic-slice_fusion.one), channel_id=1, source_target_pairs={{0,17},{16,1},{1,16},{17,0},{2,19},{18,3},{3,18},{19,2},{4,21},{20... | collective-permute-start | bytes 2654216 | tf_op jit(solution)/shard_map/ppermute | solution.py:217
  14.3 1.3 collective-permute-start.3
  15.5 1.5 collective-permute-start.4
  17.2 28.1 %all_to_all.15.own = bf16[8,144,384]{2,1,0:T(8,128)(2,1)S(1)} all-to-all(bf16[8,144,384]{2,1,0:T(8,128)(2,1)S(1)} %bitcast.32), channel_id=1, replica_groups=mesh['z'=8,'ylo'=2,'core'=2,'x'=4,'yhi'=2] {'x'}, dimensions={0} | all-to-all | bytes 1769472 | tf_op jit(solution)/shard_map/all_to_all | solution.py:204
  46.7 1.2 collective-permute-start.5
  47.9 1.8 %collective-permute-start.6 = (bf16[1,256,768]{2,1,0:T(8,128)(2,1)S(1)}, bf16[1,256,768]{2,1,0:T(8,128)(2,1)S(1)}, u32[]{:S(2)}, u32[]{:S(2)}) collective-permute-start(bf16[1,256,768]{2,1,0:T(8,128)(2,1)S(1)} %slice.103), channel_id=1, source_target_pairs={{0,6},{2,0},{4,2},{6,4},{1,7},{3,1},{5,3},{7,5},{8,14},{10,8},{12,... | collective-permute-start | bytes 1179656 | tf_op jit(solution)/shard_map/ppermute | solution.py:213
  49.7 1.2 copy-done.3
  50.9 3.9 %shard_map.68 = (bf16[6,288,384]{2,1,0:T(8,128)(2,1)S(1)}, bf16[3,384,768]{2,1,0:T(8,128)(2,1)S(1)}) custom-call(s32[1]{0:T(128)} %bitcast.over, bf16[3,192,768]{2,1,0:T(8,128)(2,1)S(1)} %copy-done.1, bf16[3,192,768]{2,1,0:T(8,128)(2,1)S(1)} %copy-done.3, bf16[2,256,768]{2,1,0:T(8,128)(2,1)S(1)} %pad_maximum_fusion.2.refs_0_.refs_3_, ...), custom_call_target="tpu_custom_call" | custom-call | bytes 7225344 | tf_op jit(solution)/shard_map/pallas_call | solution.py:57
  55.0 3.0 %shard_map.69 = (bf16[384,2048]{1,0:T(8,128)(2,1)S(1)}, bf16[384,2048]{1,0:T(8,128)(2,1)S(1)}, bf16[384,2048]{1,0:T(8,128)(2,1)S(1)}) custom-call(s32[1]{0:T(128)} %bitcast.4.x, s32[1]{0:T(128)} %bitcast.5.core, bf16[8,144,384]{2,1,0:T(8,128)(2,1)S(1)} %all_to_all.15.own, bf16[8,144,384]{2,1,0:T(8,128)(2,1)} %collective-permute-done.7.mate), custom_call_target="tpu_custom_call" | custom-call | bytes 6488064 | tf_op jit(solution)/shard_map/pallas_call | solution.py:57
  58.0 2.9 %shard_map.70.sums = f32[3,384,768]{2,1,0:T(8,128)S(1)} custom-call(bf16[384,2048]{1,0:T(8,128)(2,1)S(1)} %get-tuple-element.38.refs_0_, bf16[384,2048]{1,0:T(8,128)(2,1)S(1)} %get-tuple-element.39.refs_1_, bf16[384,2048]{1,0:T(8,128)(2,1)S(1)} %get-tuple-element.40.refs_2_, bf16[2,256,768]{2,1,0:T(8,128)(2,1)S(1)} %pad_maximum_fusion.2.refs_0_.refs_3_, ...), custom_call_target="tpu_custom_call" | custom-call | flops 2717908992 | bytes 10616832 | tf_op jit(solution)/shard_map/pallas_call | solution.py:57
  60.9 1.1 shard_map.71
  62.0 1.4 shard_map.72
  64.7 1.9 %collective-permute-start.11 = (bf16[576,384]{1,0:T(8,128)(2,1)S(1)}, bf16[576,384]{1,0:T(8,128)(2,1)S(1)}, u32[]{:S(2)}, u32[]{:S(2)}) collective-permute-start(bf16[576,384]{1,0:T(8,128)(2,1)S(1)} %get-tuple-element.59), channel_id=1, source_target_pairs={{0,17},{16,0},{1,16},{17,1},{2,19},{18,2},{3,18},{19,3},{4,21},{20... | collective-permute-start | bytes 1327112 | tf_op jit(solution)/shard_map/ppermute | solution.py:242
  66.6 11.4 %collective-permute-done.10 = bf16[576,384]{1,0:T(8,128)(2,1)S(1)} collective-permute-done((bf16[576,384]{1,0:T(8,128)(2,1)S(1)}, bf16[576,384]{1,0:T(8,128)(2,1)S(1)}, u32[]{:S(2)}, u32[]{:S(2)}) %collective-permute-start.10) | collective-permute-done | bytes 442400 | tf_op jit(solution)/shard_map/ppermute | solution.py:242
  78.0 8.0 %collective-permute-done.11 = bf16[576,384]{1,0:T(8,128)(2,1)S(1)} collective-permute-done((bf16[576,384]{1,0:T(8,128)(2,1)S(1)}, bf16[576,384]{1,0:T(8,128)(2,1)S(1)}, u32[]{:S(2)}, u32[]{:S(2)}) %collective-permute-start.11) | collective-permute-done | bytes 442400 | tf_op jit(solution)/shard_map/ppermute | solution.py:242
  86.1 1.7 %collective-permute-done.9 = bf16[576,384]{1,0:T(8,128)(2,1)S(1)} collective-permute-done((bf16[576,384]{1,0:T(8,128)(2,1)S(1)}, bf16[576,384]{1,0:T(8,128)(2,1)S(1)}, u32[]{:S(2)}, u32[]{:S(2)}) %collective-permute-start.9) | collective-permute-done | bytes 442400 | tf_op jit(solution)/shard_map/ppermute | solution.py:242
  88.8 7.4 %all-to-all-start.1 = ((bf16[8,72,384]{2,1,0:T(8,128)(2,1)}), bf16[8,72,384]{2,1,0:T(8,128)(2,1)S(1)}, u32[]{:S(2)}, u32[]{:S(2)}) async-start(bf16[8,72,384]{2,1,0:T(8,128)(2,1)} %bitcast.10), calls=%async_computation.1 | async-start | bytes 884736 | tf_op jit(solution)/shard_map/all_to_all | solution.py:245
  96.2 1.6 %convert_add_fusion = f32[8,144,384]{2,1,0:T(8,128)S(1)} fusion(bf16[8,144,384]{2,1,0:T(8,128)(2,1)} %collective-permute-done.8, pred[]{:T(512)S(6)} %eq.3, bf16[2,144,384]{2,1,0:T(8,128)(2,1)S(1)} %get-tuple-element.70, bf16[6,144,384]{2,1,0:T(8,128)(2,1)} %copy-done.8, bf16[2,144,384]{2,1,0:T(8,128)(2,1)S(1)} %get-tuple-element.69, ...), kind=kLoop, calls=%fused_computation.3 | loop fusion | flops 2654208 | bytes 4423681 | tf_op jit(solution)/shard_map/add | solution.py:271
  97.8 3.3 %collective-permute-start.12 = (bf16[8,16,384]{2,1,0:T(8,128)(2,1)S(1)}, bf16[8,16,384]{2,1,0:T(8,128)(2,1)S(1)}, u32[]{:S(2)}, u32[]{:S(2)}) collective-permute-start(bf16[8,16,384]{2,1,0:T(8,128)(2,1)S(1)} %fusion.14), channel_id=1, source_target_pairs={{8,16},{16,8},{24,32},{32,24},{40,48},{48,40},{56,64},{64,56},{72,... | collective-permute-start | bytes 294920 | tf_op jit(solution)/shard_map/ppermute | solution.py:273
  102.8 1.2 collective-permute-done.12
  104.1 8.3 %all-to-all-done.1.terms = bf16[8,72,384]{2,1,0:T(8,128)(2,1)S(1)} async-done(((bf16[8,72,384]{2,1,0:T(8,128)(2,1)}), bf16[8,72,384]{2,1,0:T(8,128)(2,1)S(1)}, u32[]{:S(2)}, u32[]{:S(2)}) %all-to-all-start.1) | async-done | bytes 442400 | tf_op jit(solution)/shard_map/all_to_all | solution.py:245
  113.4 3.9 %all-to-all-start.2 = ((bf16[16,72,384]{2,1,0:T(8,128)(2,1)}), bf16[16,72,384]{2,1,0:T(8,128)(2,1)S(1)}, u32[]{:S(2)}, u32[]{:S(2)}) async-start(bf16[16,72,384]{2,1,0:T(8,128)(2,1)} %shard_map.73), calls=%async_computation.2 | async-start | bytes 1769472 | tf_op jit(solution)/shard_map/all_to_all | solution.py:298
  120.0 3.7 %collective-permute-done.13 = bf16[2,128,384]{2,1,0:T(8,128)(2,1)S(1)} collective-permute-done((bf16[2,128,384]{2,1,0:T(8,128)(2,1)S(1)}, bf16[2,128,384]{2,1,0:T(8,128)(2,1)S(1)}, u32[]{:S(2)}, u32[]{:S(2)}) %collective-permute-start.13) | collective-permute-done | bytes 196640 | tf_op jit(solution)/shard_map/ppermute | solution.py:283
  123.8 6.1 %collective-permute-done.14 = bf16[2,128,384]{2,1,0:T(8,128)(2,1)S(1)} collective-permute-done((bf16[2,128,384]{2,1,0:T(8,128)(2,1)S(1)}, bf16[2,128,384]{2,1,0:T(8,128)(2,1)S(1)}, u32[]{:S(2)}, u32[]{:S(2)}) %collective-permute-start.14) | collective-permute-done | bytes 196640 | tf_op jit(solution)/shard_map/ppermute | solution.py:283
  129.8 10.1 %all-to-all-done.2.own = bf16[16,72,384]{2,1,0:T(8,128)(2,1)S(1)} async-done(((bf16[16,72,384]{2,1,0:T(8,128)(2,1)}), bf16[16,72,384]{2,1,0:T(8,128)(2,1)S(1)}, u32[]{:S(2)}, u32[]{:S(2)}) %all-to-all-start.2) | async-done | bytes 884768 | tf_op jit(solution)/shard_map/all_to_all | solution.py:298
  139.9 3.6 %collective-permute-start.16 = (bf16[16,72,384]{2,1,0:T(8,128)(2,1)S(1)}, bf16[16,72,384]{2,1,0:T(8,128)(2,1)S(1)}, u32[]{:S(2)}, u32[]{:S(2)}) collective-permute-start(bf16[16,72,384]{2,1,0:T(8,128)(2,1)S(1)} %all-to-all-done.2.own), channel_id=1, source_target_pairs={{0,8},{8,0},{1,9},{9,1},{2,10},{10,2},{3,11},{11,3},{4,12},{12,4},... | collective-permute-start | bytes 2654216 | tf_op jit(solution)/shard_map/ppermute | solution.py:42
  145.6 1.4 shard_map.74
  (68 shorter events, 12.8 us)
Async XLA Ops:
  0.6 2.4 %copy-start.4 = (bf16[2,128,1536]{2,1,0:T(8,128)(2,1)S(1)}, bf16[2,128,1536]{2,1,0:T(8,128)(2,1)}, u32[]{:S(2)}) copy-start(bf16[2,128,1536]{2,1,0:T(8,128)(2,1)} %param.5) | copy-start | bytes 2359300
  4.5 5.3 %collective-permute-start = (bf16[2,128,768]{2,1,0:T(8,128)(2,1)S(1)}, bf16[2,128,768]{2,1,0:T(8,128)(2,1)S(1)}, u32[]{:S(2)}, u32[]{:S(2)}) collective-permute-start(bf16[2,128,768]{2,1,0:T(8,128)(2,1)S(1)} %broadcast_select_fusion.3), channel_id=1, source_target_pairs={{0,8},{8,0},{1,9},{9,1},{2,10},{10,2},{3,11},{11,3},{4,12},{12,4},... | collective-permute-start | bytes 1179656 | tf_op jit(solution)/shard_map/ppermute | solution.py:42
  7.9 6.4 %collective-permute-start.1 = (bf16[2,16,1536]{2,1,0:T(8,128)(2,1)S(1)}, bf16[2,16,1536]{2,1,0:T(8,128)(2,1)S(1)}, u32[]{:S(2)}, u32[]{:S(2)}) collective-permute-start(bf16[2,16,1536]{2,1,0:T(8,128)(2,1)S(1)} %slice_select_fusion.1), channel_id=1, source_target_pairs={{8,16},{16,8},{24,32},{32,24},{40,48},{48,40},{56,64},{64,56},{72,... | collective-permute-start | bytes 294920 | tf_op jit(solution)/shard_map/ppermute | solution.py:197
  9.8 1.5 %copy-start.10 = (bf16[192,3,1536]{2,0,1:T(8,128)(2,1)S(1)}, bf16[192,3,1536]{2,0,1:T(8,128)(2,1)}, u32[]{:S(2)}) copy-start(bf16[192,3,1536]{2,0,1:T(8,128)(2,1)} %param.7) | copy-start | bytes 5308420
  9.9 4.3 %copy-start.9 = (bf16[2,128,1536]{2,1,0:T(8,128)(2,1)S(1)}, bf16[2,128,1536]{2,1,0:T(8,128)(2,1)}, u32[]{:S(2)}) copy-start(bf16[2,128,1536]{2,1,0:T(8,128)(2,1)} %param.8) | copy-start | bytes 2359300
  11.3 5.9 %copy-start = (bf16[3,192,768]{2,1,0:T(8,128)(2,1)}, bf16[3,192,768]{2,1,0:T(8,128)(2,1)S(1)}, u32[]{:S(2)}) copy-start(bf16[3,192,768]{2,1,0:T(8,128)(2,1)S(1)} %constant_dynamic-slice_fusion.one) | copy-start | bytes 2654212
  11.3 34.0 %collective-permute-start.2 = (bf16[3,192,768]{2,1,0:T(8,128)(2,1)S(1)}, bf16[3,192,768]{2,1,0:T(8,128)(2,1)S(1)}, u32[]{:S(2)}, u32[]{:S(2)}) collective-permute-start(bf16[3,192,768]{2,1,0:T(8,128)(2,1)S(1)} %constant_dynamic-slice_fusion.one), channel_id=1, source_target_pairs={{0,17},{16,1},{1,16},{17,0},{2,19},{18,3},{3,18},{19,2},{4,21},{20... | collective-permute-start | bytes 2654216 | tf_op jit(solution)/shard_map/ppermute | solution.py:217
  14.3 31.1 %collective-permute-start.3 = (bf16[2,256,768]{2,1,0:T(8,128)(2,1)S(1)}, bf16[2,256,768]{2,1,0:T(8,128)(2,1)S(1)}, u32[]{:S(2)}, u32[]{:S(2)}) collective-permute-start(bf16[2,256,768]{2,1,0:T(8,128)(2,1)S(1)} %pad_maximum_fusion.2.refs_0_.refs_3_), channel_id=1, source_target_pairs={{0,2},{2,4},{4,6},{6,0},{1,3},{3,5},{5,7},{7,1},{8,10},{10,12},{12... | collective-permute-start | bytes 2359304 | tf_op jit(solution)/shard_map/ppermute | solution.py:211
  15.5 29.8 %collective-permute-start.4 = (bf16[2,256,768]{2,1,0:T(8,128)(2,1)S(1)}, bf16[2,256,768]{2,1,0:T(8,128)(2,1)S(1)}, u32[]{:S(2)}, u32[]{:S(2)}) collective-permute-start(bf16[2,256,768]{2,1,0:T(8,128)(2,1)S(1)} %pad_maximum_fusion.2.refs_0_.refs_3_), channel_id=1, source_target_pairs={{0,6},{2,0},{4,2},{6,4},{1,7},{3,1},{5,3},{7,5},{8,14},{10,8},{12,... | collective-permute-start | bytes 2359304 | tf_op jit(solution)/shard_map/ppermute | solution.py:212
  45.3 0.9 copy-start.2
  46.3 8.8 %collective-permute-start.7 = (bf16[8,144,384]{2,1,0:T(8,128)(2,1)S(1)}, bf16[8,144,384]{2,1,0:T(8,128)(2,1)}, u32[]{:S(2)}, u32[]{:S(2)}) collective-permute-start(bf16[8,144,384]{2,1,0:T(8,128)(2,1)S(1)} %all_to_all.15.own), channel_id=1, source_target_pairs={{0,8},{8,0},{1,9},{9,1},{2,10},{10,2},{3,11},{11,3},{4,12},{12,4},... | collective-permute-start | bytes 2654216 | tf_op jit(solution)/shard_map/ppermute | solution.py:42
  46.6 3.1 %copy-start.1 = (bf16[3,192,768]{2,1,0:T(8,128)(2,1)S(1)}, bf16[3,192,768]{2,1,0:T(8,128)(2,1)}, u32[]{:S(2)}) copy-start(bf16[3,192,768]{2,1,0:T(8,128)(2,1)} %copy-done) | copy-start | bytes 2654212
  46.7 14.2 %collective-permute-start.5 = (bf16[1,256,768]{2,1,0:T(8,128)(2,1)S(1)}, bf16[1,256,768]{2,1,0:T(8,128)(2,1)S(1)}, u32[]{:S(2)}, u32[]{:S(2)}) collective-permute-start(bf16[1,256,768]{2,1,0:T(8,128)(2,1)S(1)} %slice.102), channel_id=1, source_target_pairs={{0,2},{2,4},{4,6},{6,0},{1,3},{3,5},{5,7},{7,1},{8,10},{10,12},{12... | collective-permute-start | bytes 1179656 | tf_op jit(solution)/shard_map/ppermute | solution.py:213
  47.9 13.0 %collective-permute-start.6 = (bf16[1,256,768]{2,1,0:T(8,128)(2,1)S(1)}, bf16[1,256,768]{2,1,0:T(8,128)(2,1)S(1)}, u32[]{:S(2)}, u32[]{:S(2)}) collective-permute-start(bf16[1,256,768]{2,1,0:T(8,128)(2,1)S(1)} %slice.103), channel_id=1, source_target_pairs={{0,6},{2,0},{4,2},{6,4},{1,7},{3,1},{5,3},{7,5},{8,14},{10,8},{12,... | collective-permute-start | bytes 1179656 | tf_op jit(solution)/shard_map/ppermute | solution.py:213
  49.7 1.2 copy-start.3
  55.0 8.5 %copy-start.6 = (bf16[6,144,384]{2,1,0:T(8,128)(2,1)}, bf16[6,144,384]{2,1,0:T(8,128)(2,1)S(1)}, u32[]{:S(2)}) copy-start(bf16[6,144,384]{2,1,0:T(8,128)(2,1)S(1)} %get-tuple-element.61) | copy-start | bytes 1990660
  55.0 8.5 %copy-start.8 = (bf16[6,144,384]{2,1,0:T(8,128)(2,1)}, bf16[6,144,384]{2,1,0:T(8,128)(2,1)S(1)}, u32[]{:S(2)}) copy-start(bf16[6,144,384]{2,1,0:T(8,128)(2,1)S(1)} %get-tuple-element.62) | copy-start | bytes 1990660
  63.7 32.5 %collective-permute-start.8 = (bf16[8,144,384]{2,1,0:T(8,128)(2,1)S(1)}, bf16[8,144,384]{2,1,0:T(8,128)(2,1)}, u32[]{:S(2)}, u32[]{:S(2)}) collective-permute-start(bf16[8,144,384]{2,1,0:T(8,128)(2,1)S(1)} %broadcast_select_fusion), channel_id=1, source_target_pairs={{0,8},{8,0},{1,9},{9,1},{2,10},{10,2},{3,11},{11,3},{4,12},{12,4},... | collective-permute-start | bytes 2654216 | tf_op jit(solution)/shard_map/ppermute | solution.py:42
  64.6 31.6 %copy-start.7 = (bf16[6,144,384]{2,1,0:T(8,128)(2,1)S(1)}, bf16[6,144,384]{2,1,0:T(8,128)(2,1)}, u32[]{:S(2)}) copy-start(bf16[6,144,384]{2,1,0:T(8,128)(2,1)} %copy-done.6) | copy-start | bytes 1990660
  64.6 13.4 %collective-permute-start.10 = (bf16[576,384]{1,0:T(8,128)(2,1)S(1)}, bf16[576,384]{1,0:T(8,128)(2,1)S(1)}, u32[]{:S(2)}, u32[]{:S(2)}) collective-permute-start(bf16[576,384]{1,0:T(8,128)(2,1)S(1)} %get-tuple-element.60), channel_id=1, source_target_pairs={{0,1},{16,17},{1,0},{17,16},{2,3},{18,19},{3,2},{19,18},{4,5},{20,... | collective-permute-start | bytes 1327112 | tf_op jit(solution)/shard_map/ppermute | solution.py:242
  64.7 21.4 %collective-permute-start.11 = (bf16[576,384]{1,0:T(8,128)(2,1)S(1)}, bf16[576,384]{1,0:T(8,128)(2,1)S(1)}, u32[]{:S(2)}, u32[]{:S(2)}) collective-permute-start(bf16[576,384]{1,0:T(8,128)(2,1)S(1)} %get-tuple-element.59), channel_id=1, source_target_pairs={{0,17},{16,0},{1,16},{17,1},{2,19},{18,2},{3,18},{19,3},{4,21},{20... | collective-permute-start | bytes 1327112 | tf_op jit(solution)/shard_map/ppermute | solution.py:242
  66.6 21.2 %collective-permute-start.9 = (bf16[576,384]{1,0:T(8,128)(2,1)S(1)}, bf16[576,384]{1,0:T(8,128)(2,1)S(1)}, u32[]{:S(2)}, u32[]{:S(2)}) collective-permute-start(bf16[576,384]{1,0:T(8,128)(2,1)S(1)} %get-tuple-element.58), channel_id=1, source_target_pairs={{0,16},{16,1},{1,17},{17,0},{2,18},{18,3},{3,19},{19,2},{4,20},{20... | collective-permute-start | bytes 1327112 | tf_op jit(solution)/shard_map/ppermute | solution.py:242
  88.8 23.6 %all-to-all-start.1 = ((bf16[8,72,384]{2,1,0:T(8,128)(2,1)}), bf16[8,72,384]{2,1,0:T(8,128)(2,1)S(1)}, u32[]{:S(2)}, u32[]{:S(2)}) async-start(bf16[8,72,384]{2,1,0:T(8,128)(2,1)} %bitcast.10), calls=%async_computation.1 | async-start | bytes 884736 | tf_op jit(solution)/shard_map/all_to_all | solution.py:245
  97.8 6.2 %collective-permute-start.12 = (bf16[8,16,384]{2,1,0:T(8,128)(2,1)S(1)}, bf16[8,16,384]{2,1,0:T(8,128)(2,1)S(1)}, u32[]{:S(2)}, u32[]{:S(2)}) collective-permute-start(bf16[8,16,384]{2,1,0:T(8,128)(2,1)S(1)} %fusion.14), channel_id=1, source_target_pairs={{8,16},{16,8},{24,32},{32,24},{40,48},{48,40},{56,64},{64,56},{72,... | collective-permute-start | bytes 294920 | tf_op jit(solution)/shard_map/ppermute | solution.py:273
  113.4 26.6 %all-to-all-start.2 = ((bf16[16,72,384]{2,1,0:T(8,128)(2,1)}), bf16[16,72,384]{2,1,0:T(8,128)(2,1)S(1)}, u32[]{:S(2)}, u32[]{:S(2)}) async-start(bf16[16,72,384]{2,1,0:T(8,128)(2,1)} %shard_map.73), calls=%async_computation.2 | async-start | bytes 1769472 | tf_op jit(solution)/shard_map/all_to_all | solution.py:298
  117.7 26.1 %copy-start.5 = (bf16[2,128,1536]{2,1,0:T(8,128)(2,1)S(1)}, bf16[2,128,1536]{2,1,0:T(8,128)(2,1)}, u32[]{:S(2)}) copy-start(bf16[2,128,1536]{2,1,0:T(8,128)(2,1)} %param.5) | copy-start | bytes 2359300
  117.7 6.1 %collective-permute-start.13 = (bf16[2,128,384]{2,1,0:T(8,128)(2,1)S(1)}, bf16[2,128,384]{2,1,0:T(8,128)(2,1)S(1)}, u32[]{:S(2)}, u32[]{:S(2)}) collective-permute-start(bf16[2,128,384]{2,1,0:T(8,128)(2,1)S(1)} %get-tuple-element.67), channel_id=1, source_target_pairs={{0,6},{2,0},{4,2},{6,4},{1,7},{3,1},{5,3},{7,5},{8,14},{10,8},{12,... | collective-permute-start | bytes 589832 | tf_op jit(solution)/shard_map/ppermute | solution.py:283
  118.8 11.1 %collective-permute-start.14 = (bf16[2,128,384]{2,1,0:T(8,128)(2,1)S(1)}, bf16[2,128,384]{2,1,0:T(8,128)(2,1)S(1)}, u32[]{:S(2)}, u32[]{:S(2)}) collective-permute-start(bf16[2,128,384]{2,1,0:T(8,128)(2,1)S(1)} %get-tuple-element.66), channel_id=1, source_target_pairs={{0,2},{2,4},{4,6},{6,0},{1,3},{3,5},{5,7},{7,1},{8,10},{10,12},{12... | collective-permute-start | bytes 589832 | tf_op jit(solution)/shard_map/ppermute | solution.py:283
  119.3 10.6 %collective-permute-start.15 = (bf16[2,128,384]{2,1,0:T(8,128)(2,1)S(1)}, bf16[2,128,384]{2,1,0:T(8,128)(2,1)S(1)}, u32[]{:S(2)}, u32[]{:S(2)}) collective-permute-start(bf16[2,128,384]{2,1,0:T(8,128)(2,1)S(1)} %get-tuple-element.65), channel_id=1, source_target_pairs={{0,4},{2,6},{4,0},{6,2},{1,5},{3,7},{5,1},{7,3},{8,12},{10,14},{12... | collective-permute-start | bytes 589832 | tf_op jit(solution)/shard_map/ppermute | solution.py:283
  139.9 5.7 %collective-permute-start.16 = (bf16[16,72,384]{2,1,0:T(8,128)(2,1)S(1)}, bf16[16,72,384]{2,1,0:T(8,128)(2,1)S(1)}, u32[]{:S(2)}, u32[]{:S(2)}) collective-permute-start(bf16[16,72,384]{2,1,0:T(8,128)(2,1)S(1)} %all-to-all-done.2.own), channel_id=1, source_target_pairs={{0,8},{8,0},{1,9},{9,1},{2,10},{10,2},{3,11},{11,3},{4,12},{12,4},... | collective-permute-start | bytes 2654216 | tf_op jit(solution)/shard_map/ppermute | solution.py:42

commit v6 on v4

--- a/solution.py
+++ b/solution.py
@@ -228,10 +228,10 @@
         (sums, *turned, *far),
         2 * work,
     )
-    grad, far = lax.optimization_barrier((grad, far))
     terms = [grad[0]] + [lax.ppermute(grad[d], PLANE, around_y(d)) for d in range(1, 4)]
     summed = sum(t.astype(F32) for t in terms).astype(BF16)
 
+    summed, far = lax.optimization_barrier((summed, far))
     terms = lax.all_to_all(summed.reshape(8, piece, quarter), "z", 0, 0, tiled=True)
 
     mixed = []

time: 147 us -> 146 us (level)
  waiting for transfers between devices: 50.8 us -> 47.6 us
  starting transfers between devices: 37.9 us -> 41 us
    ppermute x3, waiting for transfers between devices: 21.1 us -> 14.4 us  [shards(): lax.ppermute(grad[d], PLANE, around_y(d))]
    ppermute x1, waiting for transfers between devices: 0.01 us -> 2.96 us  [shards(): lax.ppermute(left[:1], 'x', around_x(1))]
    all_to_all x1, waiting for transfers between devices: 8.3 us -> 11 us  [shards(): lax.all_to_all(summed.reshape(8, piece, quarter), 'z', 0, 0, tiled=True)]
    ppermute x4, starting transfers between devices: 8.14 us -> 10.7 us  [swap(): return lax.ppermute(v, 'core', [(0, 1), (1, 0)])]
  transfers between devices with their start and end apart: 19 -> 19, of which waited for: 9 -> 9; matrix products, arithmetic and copies ran while one was open for 6% -> 5% of each run, Pallas kernels for 6% -> 6%
where the time goes in v6:
time: 146 us
  waiting for transfers between devices  47.6 us (33%)
  starting transfers between devices  41 us (28%)
  blocking collectives  28.2 us (19%)
  Pallas kernels  13.1 us (9%)
  other arithmetic  10 us (7%)
  local copies, waits for them, and re-layouts  4.83 us (3%)
    all_to_all x1, blocking collectives, shards(): cot = lax.all_to_all(cot.reshape(8, span + D, outs), 'x', 0, 0, tiled=True)  28.2 us
    ppermute x3, waiting for transfers between devices, shards(): lax.ppermute(grad[d], PLANE, around_y(d))  14.4 us
    pallas_call x7, Pallas kernels, call(): pl.pallas_call(kernel, out_shape=shapes, in_specs=[pl.BlockSpec(memory_sp...  13.1 us
    all_to_all x1, waiting for transfers between devices, shards(): lax.all_to_all(summed.reshape(8, piece, quarter), 'z', 0, 0, tiled=True)  11 us
    ppermute x4, starting transfers between devices, swap(): return lax.ppermute(v, 'core', [(0, 1), (1, 0)])  10.7 us
    ppermute x3, waiting for transfers between devices, shards(): lax.ppermute(total[i], 'x', around_x(-d))  9.84 us
    all_to_all x1, waiting for transfers between devices, shards(): sent = lax.all_to_all(copies, ('z', 'ylo'), 0, 0, tiled=True)  8.56 us
    all_to_all x1, starting transfers between devices, shards(): lax.all_to_all(summed.reshape(8, piece, quarter), 'z', 0, 0, tiled=True)  8.18 us
  transfers between devices with their start and end apart: 19, of which 9 were waited for; matrix products, arithmetic and copies ran while one was open for 5% of the time, Pallas kernels for 6%

profile of v6, /device:TPU:1, one launch (start us, length us, event | category | flops | bytes accessed | tf_op | source)
XLA Modules:
  0.0 145.8 jit_solution(17084604065990711745)
XLA Ops:
  1.7 1.4 fusion
  3.1 1.4 fusion.4
  4.5 3.3 %collective-permute-start = (bf16[2,128,768]{2,1,0:T(8,128)(2,1)S(1)}, bf16[2,128,768]{2,1,0:T(8,128)(2,1)S(1)}, u32[]{:S(2)}, u32[]{:S(2)}) collective-permute-start(bf16[2,128,768]{2,1,0:T(8,128)(2,1)S(1)} %broadcast_select_fusion.5), channel_id=1, source_target_pairs={{0,8},{8,0},{1,9},{9,1},{2,10},{10,2},{3,11},{11,3},{4,12},{12,4},... | collective-permute-start | bytes 1179656 | tf_op jit(solution)/shard_map/ppermute | solution.py:42
  7.9 1.9 %collective-permute-start.1 = (bf16[2,16,1536]{2,1,0:T(8,128)(2,1)S(1)}, bf16[2,16,1536]{2,1,0:T(8,128)(2,1)S(1)}, u32[]{:S(2)}, u32[]{:S(2)}) collective-permute-start(bf16[2,16,1536]{2,1,0:T(8,128)(2,1)S(1)} %slice_select_fusion.1), channel_id=1, source_target_pairs={{8,16},{16,8},{24,32},{32,24},{40,48},{48,40},{56,64},{64,56},{72,... | collective-permute-start | bytes 294920 | tf_op jit(solution)/shard_map/ppermute | solution.py:186
  9.9 1.3 copy-done.6
  11.3 2.8 %collective-permute-start.2 = (bf16[3,192,768]{2,1,0:T(8,128)(2,1)S(1)}, bf16[3,192,768]{2,1,0:T(8,128)(2,1)S(1)}, u32[]{:S(2)}, u32[]{:S(2)}) collective-permute-start(bf16[3,192,768]{2,1,0:T(8,128)(2,1)S(1)} %constant_dynamic-slice_fusion.one), channel_id=1, source_target_pairs={{0,17},{16,1},{1,16},{17,0},{2,19},{18,3},{3,18},{19,2},{4,21},{20... | collective-permute-start | bytes 2654216 | tf_op jit(solution)/shard_map/ppermute | solution.py:206
  14.2 1.3 collective-permute-start.3
  15.5 1.5 %collective-permute-start.4 = (bf16[2,256,768]{2,1,0:T(8,128)(2,1)S(1)}, bf16[2,256,768]{2,1,0:T(8,128)(2,1)S(1)}, u32[]{:S(2)}, u32[]{:S(2)}) collective-permute-start(bf16[2,256,768]{2,1,0:T(8,128)(2,1)S(1)} %pad_maximum_fusion.3.refs_0_.refs_3_), channel_id=1, source_target_pairs={{0,6},{2,0},{4,2},{6,4},{1,7},{3,1},{5,3},{7,5},{8,14},{10,8},{12,... | collective-permute-start | bytes 2359304 | tf_op jit(solution)/shard_map/ppermute | solution.py:201
  17.2 28.2 %all_to_all.15 = bf16[8,144,384]{2,1,0:T(8,128)(2,1)} all-to-all(bf16[8,144,384]{2,1,0:T(8,128)(2,1)S(1)} %bitcast.34), channel_id=1, replica_groups=mesh['z'=8,'ylo'=2,'core'=2,'x'=4,'yhi'=2] {'x'}, dimensions={0} | all-to-all | bytes 1769472 | tf_op jit(solution)/shard_map/all_to_all | solution.py:193
  48.0 1.6 %collective-permute-start.6 = (bf16[1,256,768]{2,1,0:T(8,128)(2,1)S(1)}, bf16[1,256,768]{2,1,0:T(8,128)(2,1)S(1)}, u32[]{:S(2)}, u32[]{:S(2)}) collective-permute-start(bf16[1,256,768]{2,1,0:T(8,128)(2,1)S(1)} %slice.104), channel_id=1, source_target_pairs={{0,6},{2,0},{4,2},{6,4},{1,7},{3,1},{5,3},{7,5},{8,14},{10,8},{12,... | collective-permute-start | bytes 1179656 | tf_op jit(solution)/shard_map/ppermute | solution.py:202
  49.6 1.6 %broadcast_select_fusion.2 = (bf16[8,144,384]{2,1,0:T(8,128)(2,1)S(1)}, bf16[8,144,384]{2,1,0:T(8,128)(2,1)S(1)}) fusion(bf16[8,144,384]{2,1,0:T(8,128)(2,1)} %all_to_all.15, bf16[8,144,384]{2,1,0:T(8,128)(2,1)} %collective-permute-done.7, pred[]{:T(512)S(6)} %eq.3), kind=kLoop, calls=%fused_computation.27 | loop fusion | flops 884736 | bytes 3538945 | tf_op jit(solution)/shard_map/jit(_where)/select_n | solution.py:210
  51.4 1.3 shard_map.69
  52.8 2.9 %shard_map.70.sums = f32[3,384,768]{2,1,0:T(8,128)S(1)} custom-call(bf16[384,2048]{1,0:T(8,128)(2,1)S(1)} %get-tuple-element.34.refs_0_, bf16[384,2048]{1,0:T(8,128)(2,1)S(1)} %get-tuple-element.35.refs_1_, bf16[384,2048]{1,0:T(8,128)(2,1)S(1)} %get-tuple-element.36.refs_2_, bf16[2,256,768]{2,1,0:T(8,128)(2,1)S(1)} %pad_maximum_fusion.3.refs_0_.refs_3_, ...), custom_call_target="tpu_custom_call" | custom-call | flops 2717908992 | bytes 10616832 | tf_op jit(solution)/shard_map/pallas_call | solution.py:57
  55.7 3.0 %collective-permute-done.5.refs_3_.refs_0_ = bf16[1,256,768]{2,1,0:T(8,128)(2,1)S(1)} collective-permute-done((bf16[1,256,768]{2,1,0:T(8,128)(2,1)S(1)}, bf16[1,256,768]{2,1,0:T(8,128)(2,1)S(1)}, u32[]{:S(2)}, u32[]{:S(2)}) %collective-permute-start.5) | collective-permute-done | bytes 393248 | tf_op jit(solution)/shard_map/ppermute | solution.py:202
  62.4 3.9 %shard_map.68 = bf16[6,288,384]{2,1,0:T(8,128)(2,1)S(1)} custom-call(s32[1]{0:T(128)} %bitcast.over, bf16[3,192,768]{2,1,0:T(8,128)(2,1)S(1)} %constant_dynamic-slice_fusion.one, bf16[3,192,768]{2,1,0:T(8,128)(2,1)S(1)} %copy-done.1, bf16[2,256,768]{2,1,0:T(8,128)(2,1)S(1)} %pad_maximum_fusion.3.refs_0_.refs_3_, ...), custom_call_target="tpu_custom_call" | custom-call | bytes 5455872 | tf_op jit(solution)/shard_map/pallas_call | solution.py:57
  66.5 4.2 %collective-permute-done.10 = bf16[576,384]{1,0:T(8,128)(2,1)S(1)} collective-permute-done((bf16[576,384]{1,0:T(8,128)(2,1)S(1)}, bf16[576,384]{1,0:T(8,128)(2,1)S(1)}, u32[]{:S(2)}, u32[]{:S(2)}) %collective-permute-start.10) | collective-permute-done | bytes 442400 | tf_op jit(solution)/shard_map/ppermute | solution.py:231
  70.7 2.6 %collective-permute-done.8 = bf16[576,384]{1,0:T(8,128)(2,1)S(1)} collective-permute-done((bf16[576,384]{1,0:T(8,128)(2,1)S(1)}, bf16[576,384]{1,0:T(8,128)(2,1)S(1)}, u32[]{:S(2)}, u32[]{:S(2)}) %collective-permute-start.8) | collective-permute-done | bytes 442400 | tf_op jit(solution)/shard_map/ppermute | solution.py:231
  73.2 7.7 %collective-permute-done.9 = bf16[576,384]{1,0:T(8,128)(2,1)S(1)} collective-permute-done((bf16[576,384]{1,0:T(8,128)(2,1)S(1)}, bf16[576,384]{1,0:T(8,128)(2,1)S(1)}, u32[]{:S(2)}, u32[]{:S(2)}) %collective-permute-start.9) | collective-permute-done | bytes 442400 | tf_op jit(solution)/shard_map/ppermute | solution.py:231
  81.9 1.5 %shard_map.72 = bf16[2,288,384]{2,1,0:T(8,128)(2,1)S(1)} custom-call(s32[1]{0:T(128)} %bitcast.over, bf16[3,192,768]{2,1,0:T(8,128)(2,1)S(1)} %constant_dynamic-slice_fusion.one, bf16[3,192,768]{2,1,0:T(8,128)(2,1)S(1)} %copy-done.1, bf16[1,256,768]{2,1,0:T(8,128)(2,1)S(1)} %collective-permute-done.5.refs_3_.refs_0_, ...), custom_call_target="tpu_custom_call" | custom-call | bytes 2998272 | tf_op jit(solution)/shard_map/pallas_call | solution.py:57
  83.6 3.4 %collective-permute-start.11 = (bf16[8,144,384]{2,1,0:T(8,128)(2,1)S(1)}, bf16[8,144,384]{2,1,0:T(8,128)(2,1)}, u32[]{:S(2)}, u32[]{:S(2)}) collective-permute-start(bf16[8,144,384]{2,1,0:T(8,128)(2,1)S(1)} %broadcast_select_fusion), channel_id=1, source_target_pairs={{0,8},{8,0},{1,9},{9,1},{2,10},{10,2},{3,11},{11,3},{4,12},{12,4},... | collective-permute-start | bytes 2654216 | tf_op jit(solution)/shard_map/ppermute | solution.py:42
  87.0 8.2 %all-to-all-start.1 = ((bf16[8,72,384]{2,1,0:T(8,128)(2,1)}), bf16[8,72,384]{2,1,0:T(8,128)(2,1)S(1)}, u32[]{:S(2)}, u32[]{:S(2)}) async-start(bf16[8,72,384]{2,1,0:T(8,128)(2,1)} %bitcast.9), calls=%async_computation.1 | async-start | bytes 884736 | tf_op jit(solution)/shard_map/all_to_all | solution.py:235
  95.2 1.6 %convert_add_fusion = f32[8,144,384]{2,1,0:T(8,128)S(1)} fusion(bf16[8,144,384]{2,1,0:T(8,128)(2,1)} %collective-permute-done.11, pred[]{:T(512)S(6)} %eq.3, bf16[2,144,384]{2,1,0:T(8,128)(2,1)S(1)} %get-tuple-element.68, bf16[6,144,384]{2,1,0:T(8,128)(2,1)} %copy-done.4, bf16[2,144,384]{2,1,0:T(8,128)(2,1)S(1)} %get-tuple-element.67, ...), kind=kLoop, calls=%fused_computation.4 | loop fusion | flops 2654208 | bytes 4423681 | tf_op jit(solution)/shard_map/add | solution.py:251
  96.8 1.9 %collective-permute-start.12 = (bf16[8,16,384]{2,1,0:T(8,128)(2,1)S(1)}, bf16[8,16,384]{2,1,0:T(8,128)(2,1)S(1)}, u32[]{:S(2)}, u32[]{:S(2)}) collective-permute-start(bf16[8,16,384]{2,1,0:T(8,128)(2,1)S(1)} %fusion.14), channel_id=1, source_target_pairs={{8,16},{16,8},{24,32},{32,24},{40,48},{48,40},{56,64},{64,56},{72,... | collective-permute-start | bytes 294920 | tf_op jit(solution)/shard_map/ppermute | solution.py:253
  100.4 11.0 %all-to-all-done.1.terms = bf16[8,72,384]{2,1,0:T(8,128)(2,1)S(1)} async-done(((bf16[8,72,384]{2,1,0:T(8,128)(2,1)}), bf16[8,72,384]{2,1,0:T(8,128)(2,1)S(1)}, u32[]{:S(2)}, u32[]{:S(2)}) %all-to-all-start.1) | async-done | bytes 442400 | tf_op jit(solution)/shard_map/all_to_all | solution.py:235
  112.5 3.6 %all-to-all-start.2 = ((bf16[16,72,384]{2,1,0:T(8,128)(2,1)}), bf16[16,72,384]{2,1,0:T(8,128)(2,1)S(1)}, u32[]{:S(2)}, u32[]{:S(2)}) async-start(bf16[16,72,384]{2,1,0:T(8,128)(2,1)} %shard_map.73), calls=%async_computation.2 | async-start | bytes 1769472 | tf_op jit(solution)/shard_map/all_to_all | solution.py:278
  116.6 2.5 %collective-permute-start.13 = (bf16[2,128,384]{2,1,0:T(8,128)(2,1)S(1)}, bf16[2,128,384]{2,1,0:T(8,128)(2,1)S(1)}, u32[]{:S(2)}, u32[]{:S(2)}) collective-permute-start(bf16[2,128,384]{2,1,0:T(8,128)(2,1)S(1)} %get-tuple-element.65), channel_id=1, source_target_pairs={{0,6},{2,0},{4,2},{6,4},{1,7},{3,1},{5,3},{7,5},{8,14},{10,8},{12,... | collective-permute-start | bytes 589832 | tf_op jit(solution)/shard_map/ppermute | solution.py:263
  119.1 1.3 collective-permute-start.15
  120.4 2.4 %collective-permute-done.13 = bf16[2,128,384]{2,1,0:T(8,128)(2,1)S(1)} collective-permute-done((bf16[2,128,384]{2,1,0:T(8,128)(2,1)S(1)}, bf16[2,128,384]{2,1,0:T(8,128)(2,1)S(1)}, u32[]{:S(2)}, u32[]{:S(2)}) %collective-permute-start.13) | collective-permute-done | bytes 196640 | tf_op jit(solution)/shard_map/ppermute | solution.py:263
  122.8 7.4 %collective-permute-done.14 = bf16[2,128,384]{2,1,0:T(8,128)(2,1)S(1)} collective-permute-done((bf16[2,128,384]{2,1,0:T(8,128)(2,1)S(1)}, bf16[2,128,384]{2,1,0:T(8,128)(2,1)S(1)}, u32[]{:S(2)}, u32[]{:S(2)}) %collective-permute-start.14) | collective-permute-done | bytes 196640 | tf_op jit(solution)/shard_map/ppermute | solution.py:263
  130.3 8.6 %all-to-all-done.2.own = bf16[16,72,384]{2,1,0:T(8,128)(2,1)S(1)} async-done(((bf16[16,72,384]{2,1,0:T(8,128)(2,1)}), bf16[16,72,384]{2,1,0:T(8,128)(2,1)S(1)}, u32[]{:S(2)}, u32[]{:S(2)}) %all-to-all-start.2) | async-done | bytes 884768 | tf_op jit(solution)/shard_map/all_to_all | solution.py:278
  138.8 3.6 %collective-permute-start.16 = (bf16[16,72,384]{2,1,0:T(8,128)(2,1)S(1)}, bf16[16,72,384]{2,1,0:T(8,128)(2,1)S(1)}, u32[]{:S(2)}, u32[]{:S(2)}) collective-permute-start(bf16[16,72,384]{2,1,0:T(8,128)(2,1)S(1)} %all-to-all-done.2.own), channel_id=1, source_target_pairs={{0,8},{8,0},{1,9},{9,1},{2,10},{10,2},{3,11},{11,3},{4,12},{12,4},... | collective-permute-start | bytes 2654216 | tf_op jit(solution)/shard_map/ppermute | solution.py:42
  144.5 1.4 shard_map.74
  (62 shorter events, 14.5 us)
Async XLA Ops:
  0.6 2.4 %copy-start.2 = (bf16[2,128,1536]{2,1,0:T(8,128)(2,1)S(1)}, bf16[2,128,1536]{2,1,0:T(8,128)(2,1)}, u32[]{:S(2)}) copy-start(bf16[2,128,1536]{2,1,0:T(8,128)(2,1)} %param.5) | copy-start | bytes 2359300
  4.5 5.3 %collective-permute-start = (bf16[2,128,768]{2,1,0:T(8,128)(2,1)S(1)}, bf16[2,128,768]{2,1,0:T(8,128)(2,1)S(1)}, u32[]{:S(2)}, u32[]{:S(2)}) collective-permute-start(bf16[2,128,768]{2,1,0:T(8,128)(2,1)S(1)} %broadcast_select_fusion.5), channel_id=1, source_target_pairs={{0,8},{8,0},{1,9},{9,1},{2,10},{10,2},{3,11},{11,3},{4,12},{12,4},... | collective-permute-start | bytes 1179656 | tf_op jit(solution)/shard_map/ppermute | solution.py:42
  7.9 6.4 %collective-permute-start.1 = (bf16[2,16,1536]{2,1,0:T(8,128)(2,1)S(1)}, bf16[2,16,1536]{2,1,0:T(8,128)(2,1)S(1)}, u32[]{:S(2)}, u32[]{:S(2)}) collective-permute-start(bf16[2,16,1536]{2,1,0:T(8,128)(2,1)S(1)} %slice_select_fusion.1), channel_id=1, source_target_pairs={{8,16},{16,8},{24,32},{32,24},{40,48},{48,40},{56,64},{64,56},{72,... | collective-permute-start | bytes 294920 | tf_op jit(solution)/shard_map/ppermute | solution.py:186
  9.8 1.5 %copy-start.6 = (bf16[192,3,1536]{2,0,1:T(8,128)(2,1)S(1)}, bf16[192,3,1536]{2,0,1:T(8,128)(2,1)}, u32[]{:S(2)}) copy-start(bf16[192,3,1536]{2,0,1:T(8,128)(2,1)} %param.7) | copy-start | bytes 5308420
  9.9 4.2 %copy-start.5 = (bf16[2,128,1536]{2,1,0:T(8,128)(2,1)S(1)}, bf16[2,128,1536]{2,1,0:T(8,128)(2,1)}, u32[]{:S(2)}) copy-start(bf16[2,128,1536]{2,1,0:T(8,128)(2,1)} %param.8) | copy-start | bytes 2359300
  11.3 34.1 %collective-permute-start.2 = (bf16[3,192,768]{2,1,0:T(8,128)(2,1)S(1)}, bf16[3,192,768]{2,1,0:T(8,128)(2,1)S(1)}, u32[]{:S(2)}, u32[]{:S(2)}) collective-permute-start(bf16[3,192,768]{2,1,0:T(8,128)(2,1)S(1)} %constant_dynamic-slice_fusion.one), channel_id=1, source_target_pairs={{0,17},{16,1},{1,16},{17,0},{2,19},{18,3},{3,18},{19,2},{4,21},{20... | collective-permute-start | bytes 2654216 | tf_op jit(solution)/shard_map/ppermute | solution.py:206
  14.2 31.2 %collective-permute-start.3 = (bf16[2,256,768]{2,1,0:T(8,128)(2,1)S(1)}, bf16[2,256,768]{2,1,0:T(8,128)(2,1)S(1)}, u32[]{:S(2)}, u32[]{:S(2)}) collective-permute-start(bf16[2,256,768]{2,1,0:T(8,128)(2,1)S(1)} %pad_maximum_fusion.3.refs_0_.refs_3_), channel_id=1, source_target_pairs={{0,2},{2,4},{4,6},{6,0},{1,3},{3,5},{5,7},{7,1},{8,10},{10,12},{12... | collective-permute-start | bytes 2359304 | tf_op jit(solution)/shard_map/ppermute | solution.py:200
  15.5 29.9 %collective-permute-start.4 = (bf16[2,256,768]{2,1,0:T(8,128)(2,1)S(1)}, bf16[2,256,768]{2,1,0:T(8,128)(2,1)S(1)}, u32[]{:S(2)}, u32[]{:S(2)}) collective-permute-start(bf16[2,256,768]{2,1,0:T(8,128)(2,1)S(1)} %pad_maximum_fusion.3.refs_0_.refs_3_), channel_id=1, source_target_pairs={{0,6},{2,0},{4,2},{6,4},{1,7},{3,1},{5,3},{7,5},{8,14},{10,8},{12,... | collective-permute-start | bytes 2359304 | tf_op jit(solution)/shard_map/ppermute | solution.py:201
  45.4 0.9 copy-start
  46.3 3.3 %collective-permute-start.7 = (bf16[8,144,384]{2,1,0:T(8,128)(2,1)}, bf16[8,144,384]{2,1,0:T(8,128)(2,1)}, u32[]{:S(2)}, u32[]{:S(2)}) collective-permute-start(bf16[8,144,384]{2,1,0:T(8,128)(2,1)} %all_to_all.15), channel_id=1, source_target_pairs={{0,8},{8,0},{1,9},{9,1},{2,10},{10,2},{3,11},{11,3},{4,12},{12,4},... | collective-permute-start | bytes 2654216 | tf_op jit(solution)/shard_map/ppermute | solution.py:42
  46.8 11.9 %collective-permute-start.5 = (bf16[1,256,768]{2,1,0:T(8,128)(2,1)S(1)}, bf16[1,256,768]{2,1,0:T(8,128)(2,1)S(1)}, u32[]{:S(2)}, u32[]{:S(2)}) collective-permute-start(bf16[1,256,768]{2,1,0:T(8,128)(2,1)S(1)} %slice.103), channel_id=1, source_target_pairs={{0,2},{2,4},{4,6},{6,0},{1,3},{3,5},{5,7},{7,1},{8,10},{10,12},{12... | collective-permute-start | bytes 1179656 | tf_op jit(solution)/shard_map/ppermute | solution.py:202
  48.0 10.6 %collective-permute-start.6 = (bf16[1,256,768]{2,1,0:T(8,128)(2,1)S(1)}, bf16[1,256,768]{2,1,0:T(8,128)(2,1)S(1)}, u32[]{:S(2)}, u32[]{:S(2)}) collective-permute-start(bf16[1,256,768]{2,1,0:T(8,128)(2,1)S(1)} %slice.104), channel_id=1, source_target_pairs={{0,6},{2,0},{4,2},{6,4},{1,7},{3,1},{5,3},{7,5},{8,14},{10,8},{12,... | collective-permute-start | bytes 1179656 | tf_op jit(solution)/shard_map/ppermute | solution.py:202
  59.7 2.6 %copy-start.1 = (bf16[3,192,768]{2,1,0:T(8,128)(2,1)S(1)}, bf16[3,192,768]{2,1,0:T(8,128)(2,1)}, u32[]{:S(2)}) copy-start(bf16[3,192,768]{2,1,0:T(8,128)(2,1)} %copy-done) | copy-start | bytes 2654212
  59.9 10.8 %collective-permute-start.10 = (bf16[576,384]{1,0:T(8,128)(2,1)S(1)}, bf16[576,384]{1,0:T(8,128)(2,1)S(1)}, u32[]{:S(2)}, u32[]{:S(2)}) collective-permute-start(bf16[576,384]{1,0:T(8,128)(2,1)S(1)} %get-tuple-element.55), channel_id=1, source_target_pairs={{0,17},{16,0},{1,16},{17,1},{2,19},{18,2},{3,18},{19,3},{4,21},{20... | collective-permute-start | bytes 1327112 | tf_op jit(solution)/shard_map/ppermute | solution.py:231
  60.9 12.3 %collective-permute-start.8 = (bf16[576,384]{1,0:T(8,128)(2,1)S(1)}, bf16[576,384]{1,0:T(8,128)(2,1)S(1)}, u32[]{:S(2)}, u32[]{:S(2)}) collective-permute-start(bf16[576,384]{1,0:T(8,128)(2,1)S(1)} %get-tuple-element.54), channel_id=1, source_target_pairs={{0,16},{16,1},{1,17},{17,0},{2,18},{18,3},{3,19},{19,2},{4,20},{20... | collective-permute-start | bytes 1327112 | tf_op jit(solution)/shard_map/ppermute | solution.py:231
  61.4 19.5 %collective-permute-start.9 = (bf16[576,384]{1,0:T(8,128)(2,1)S(1)}, bf16[576,384]{1,0:T(8,128)(2,1)S(1)}, u32[]{:S(2)}, u32[]{:S(2)}) collective-permute-start(bf16[576,384]{1,0:T(8,128)(2,1)S(1)} %get-tuple-element.56), channel_id=1, source_target_pairs={{0,1},{16,17},{1,0},{17,16},{2,3},{18,19},{3,2},{19,18},{4,5},{20,... | collective-permute-start | bytes 1327112 | tf_op jit(solution)/shard_map/ppermute | solution.py:231
  66.5 17.0 %copy-start.4 = (bf16[6,144,384]{2,1,0:T(8,128)(2,1)}, bf16[6,144,384]{2,1,0:T(8,128)(2,1)S(1)}, u32[]{:S(2)}) copy-start(bf16[6,144,384]{2,1,0:T(8,128)(2,1)S(1)} %get-tuple-element.60) | copy-start | bytes 1990660
  83.6 11.6 %collective-permute-start.11 = (bf16[8,144,384]{2,1,0:T(8,128)(2,1)S(1)}, bf16[8,144,384]{2,1,0:T(8,128)(2,1)}, u32[]{:S(2)}, u32[]{:S(2)}) collective-permute-start(bf16[8,144,384]{2,1,0:T(8,128)(2,1)S(1)} %broadcast_select_fusion), channel_id=1, source_target_pairs={{0,8},{8,0},{1,9},{9,1},{2,10},{10,2},{3,11},{11,3},{4,12},{12,4},... | collective-permute-start | bytes 2654216 | tf_op jit(solution)/shard_map/ppermute | solution.py:42
  87.0 24.5 %all-to-all-start.1 = ((bf16[8,72,384]{2,1,0:T(8,128)(2,1)}), bf16[8,72,384]{2,1,0:T(8,128)(2,1)S(1)}, u32[]{:S(2)}, u32[]{:S(2)}) async-start(bf16[8,72,384]{2,1,0:T(8,128)(2,1)} %bitcast.9), calls=%async_computation.1 | async-start | bytes 884736 | tf_op jit(solution)/shard_map/all_to_all | solution.py:235
  96.8 14.6 %collective-permute-start.12 = (bf16[8,16,384]{2,1,0:T(8,128)(2,1)S(1)}, bf16[8,16,384]{2,1,0:T(8,128)(2,1)S(1)}, u32[]{:S(2)}, u32[]{:S(2)}) collective-permute-start(bf16[8,16,384]{2,1,0:T(8,128)(2,1)S(1)} %fusion.14), channel_id=1, source_target_pairs={{8,16},{16,8},{24,32},{32,24},{40,48},{48,40},{56,64},{64,56},{72,... | collective-permute-start | bytes 294920 | tf_op jit(solution)/shard_map/ppermute | solution.py:253
  112.5 26.4 %all-to-all-start.2 = ((bf16[16,72,384]{2,1,0:T(8,128)(2,1)}), bf16[16,72,384]{2,1,0:T(8,128)(2,1)S(1)}, u32[]{:S(2)}, u32[]{:S(2)}) async-start(bf16[16,72,384]{2,1,0:T(8,128)(2,1)} %shard_map.73), calls=%async_computation.2 | async-start | bytes 1769472 | tf_op jit(solution)/shard_map/all_to_all | solution.py:278
  116.6 26.1 %copy-start.3 = (bf16[2,128,1536]{2,1,0:T(8,128)(2,1)S(1)}, bf16[2,128,1536]{2,1,0:T(8,128)(2,1)}, u32[]{:S(2)}) copy-start(bf16[2,128,1536]{2,1,0:T(8,128)(2,1)} %param.5) | copy-start | bytes 2359300
  116.6 6.2 %collective-permute-start.13 = (bf16[2,128,384]{2,1,0:T(8,128)(2,1)S(1)}, bf16[2,128,384]{2,1,0:T(8,128)(2,1)S(1)}, u32[]{:S(2)}, u32[]{:S(2)}) collective-permute-start(bf16[2,128,384]{2,1,0:T(8,128)(2,1)S(1)} %get-tuple-element.65), channel_id=1, source_target_pairs={{0,6},{2,0},{4,2},{6,4},{1,7},{3,1},{5,3},{7,5},{8,14},{10,8},{12,... | collective-permute-start | bytes 589832 | tf_op jit(solution)/shard_map/ppermute | solution.py:263
  119.1 11.1 %collective-permute-start.14 = (bf16[2,128,384]{2,1,0:T(8,128)(2,1)S(1)}, bf16[2,128,384]{2,1,0:T(8,128)(2,1)S(1)}, u32[]{:S(2)}, u32[]{:S(2)}) collective-permute-start(bf16[2,128,384]{2,1,0:T(8,128)(2,1)S(1)} %get-tuple-element.64), channel_id=1, source_target_pairs={{0,2},{2,4},{4,6},{6,0},{1,3},{3,5},{5,7},{7,1},{8,10},{10,12},{12... | collective-permute-start | bytes 589832 | tf_op jit(solution)/shard_map/ppermute | solution.py:263
  119.1 11.1 %collective-permute-start.15 = (bf16[2,128,384]{2,1,0:T(8,128)(2,1)S(1)}, bf16[2,128,384]{2,1,0:T(8,128)(2,1)S(1)}, u32[]{:S(2)}, u32[]{:S(2)}) collective-permute-start(bf16[2,128,384]{2,1,0:T(8,128)(2,1)S(1)} %get-tuple-element.63), channel_id=1, source_target_pairs={{0,4},{2,6},{4,0},{6,2},{1,5},{3,7},{5,1},{7,3},{8,12},{10,14},{12... | collective-permute-start | bytes 589832 | tf_op jit(solution)/shard_map/ppermute | solution.py:263
  138.8 5.6 %collective-permute-start.16 = (bf16[16,72,384]{2,1,0:T(8,128)(2,1)S(1)}, bf16[16,72,384]{2,1,0:T(8,128)(2,1)S(1)}, u32[]{:S(2)}, u32[]{:S(2)}) collective-permute-start(bf16[16,72,384]{2,1,0:T(8,128)(2,1)S(1)} %all-to-all-done.2.own), channel_id=1, source_target_pairs={{0,8},{8,0},{1,9},{9,1},{2,10},{10,2},{3,11},{11,3},{4,12},{12,4},... | collective-permute-start | bytes 2654216 | tf_op jit(solution)/shard_map/ppermute | solution.py:42
